TPU v7x, 512 devices: a whole 4x8x8 slice. The times are simulated.
512 devices in a mesh: dp: 64 (over y, x, core), mp: 8 (over z).
Axes of the slice: x: 4, y: 8, z: 8, core: 2. Of those that a mesh axis runs over, the one named last changes fastest.
Arguments:
- tokens: bfloat16 [32768, 2048], P('dp'), may hold values from -6 to 6
- q_weight: bfloat16 [2048, 256], P('dp', 'mp'), may hold values from -0.125 to 0.125
- k_weight: bfloat16 [2048, 256], P('dp', 'mp'), may hold values from -0.125 to 0.125
- v_weight: bfloat16 [2048, 2048], P('dp', 'mp'), may hold values from -0.125 to 0.125
- adapter_down: bfloat16 [2048, 256], P(None, 'mp'), may hold values from -0.125 to 0.125
- adapter_up: bfloat16 [256, 2048], P(None, 'mp'), may hold values from -1.5 to 1.5
- lengths: int32 [4], replicated, may hold values from 1 to 16384, 32768 in all
- adapter_ids: int32 [4], replicated, may hold values from 0 to 15
- head_gain: float32 [2048], P('mp'), may hold values from 0.1 to 1.9
- out_weight: bfloat16 [2048, 2048], P('mp', 'dp'), may hold values from -0.125 to 0.125
Outputs:
- layer_out: bfloat16 [32768, 2048], P('dp', 'mp')
Inputs may be any that keep to these rules, and one draw needn't show every extreme that they name: The lengths sum to 32768 and the longest request has exactly 32768 // 2 tokens.
All inputs are finite; a program needn't handle non-finite values.
Results may differ from a plain program's by a relative error of at most 0.022.
Values may be sent and summed in bfloat16 or wider, within the bound.
A program may use at most 128 MiB of HBM per device.

v0:
```python
import math

import jax
import jax.numpy as jnp
from jax import lax
from jax.sharding import PartitionSpec as P

F = 16
R = 16


EPSILON = 1e-05


def carried_in(value, axis, combine, identity):
    length, place = (lax.axis_size(axis), lax.axis_index(axis))
    everything = jax.tree.map(
        lambda part, kind: lax.all_gather(part.astype(kind), axis),
        value,
        (jnp.bfloat16, jnp.bfloat16),
    )
    start = jax.tree.map(
        lambda part, zero: jnp.broadcast_to(jnp.asarray(zero, part.dtype), part.shape),
        value,
        identity,
    )

    def turn(k, before):
        reached = k < place
        new = combine(
            before, jax.tree.map(lambda part, own: part[k].astype(own.dtype), everything, value)
        )
        return jax.tree.map(lambda a, b: jnp.where(reached, a, b), new, before)

    return lax.fori_loop(0, length, turn, start)


def taylor(inputs):
    squares = (inputs[..., :, None] * inputs[..., None, :]).reshape(
        inputs.shape[:-1] + (inputs.shape[-1] * inputs.shape[-1],)
    )
    constant = jnp.ones(inputs.shape[:-1] + (1,), jnp.float32)
    return jnp.concatenate([constant, 0.5 * inputs, squares * (0.25 / math.sqrt(2.0))], axis=-1)


def token_tables(lengths, adapter_ids, positions):
    bounds = jnp.cumsum(lengths)
    request = jnp.sum((positions[:, None] >= bounds[None, :]).astype(jnp.int32), axis=1)
    openings = bounds - lengths
    starts = jnp.any(positions[:, None] == openings[None, :], axis=1)
    picked = request[:, None] == jnp.arange(lengths.shape[0], dtype=jnp.int32)[None, :]
    adapter = jnp.sum(jnp.where(picked, adapter_ids[None, :], 0), axis=1)
    return (request, starts, adapter)


def block_local(query, key_rows, values, request, starts):
    scores = jnp.einsum("ihd,jhd->hij", query, key_rows, preferred_element_type=jnp.float32) * 0.25
    weights = 1.0 + scores + 0.5 * scores * scores
    indexes = jnp.arange(request.shape[0], dtype=jnp.int32)
    allowed = (indexes[None, :] <= indexes[:, None]) & (request[None, :] == request[:, None])
    weights = jnp.where(allowed[None], weights, 0.0).astype(jnp.bfloat16)
    within = jnp.einsum("hij,jhe->ihe", weights, values, preferred_element_type=jnp.float32)
    query_map = taylor(query.astype(jnp.float32)).astype(jnp.bfloat16)
    key_map = taylor(key_rows.astype(jnp.float32)).astype(jnp.bfloat16)
    tail_mask = (request == request[-1]).astype(jnp.bfloat16)
    masked_keys = key_map * tail_mask[:, None, None]
    summary = jnp.einsum("ihf,ihe->hfe", masked_keys, values, preferred_element_type=jnp.float32)
    restart = jnp.max(starts.astype(jnp.float32))
    return (within, query_map, summary, restart)


def finish(within, query_map, carried, request, starts, gains):
    follows = ((request == request[0]) & jnp.logical_not(starts[0])).astype(jnp.float32)
    cross = jnp.einsum(
        "ihf,hfe->ihe", query_map, carried.astype(jnp.bfloat16), preferred_element_type=jnp.float32
    )
    combined = within + follows[:, None, None] * cross
    factor = lax.rsqrt(jnp.mean(combined * combined, axis=-1, keepdims=True) + EPSILON)
    return (combined * factor * gains[None]).astype(jnp.bfloat16)


def combine(earlier, later):
    return (
        jnp.maximum(earlier[0], later[0]),
        jnp.where(later[0] > 0, later[1], earlier[1] + later[1]),
    )


def per_device(
    tokens,
    q_weight,
    k_weight,
    v_weight,
    adapter_down,
    adapter_up,
    lengths,
    adapter_ids,
    head_gain,
    out_weight,
):
    row_count = tokens.shape[0]
    heads_here = q_weight.shape[1] // F
    value_width = v_weight.shape[1] // heads_here
    positions = lax.axis_index("dp") * row_count + jnp.arange(row_count, dtype=jnp.int32)
    request, starts, adapter = token_tables(lengths, adapter_ids, positions)
    query_sum = jnp.dot(
        tokens,
        lax.all_gather(q_weight, "dp", axis=0, tiled=True),
        preferred_element_type=jnp.float32,
    )
    key_sum = jnp.dot(
        tokens,
        lax.all_gather(k_weight, "dp", axis=0, tiled=True),
        preferred_element_type=jnp.float32,
    )
    value_sum = jnp.dot(
        tokens,
        lax.all_gather(v_weight, "dp", axis=0, tiled=True),
        preferred_element_type=jnp.float32,
    )
    query = query_sum.astype(jnp.bfloat16).reshape(row_count, heads_here, F)
    key_rows = key_sum.astype(jnp.bfloat16).reshape(row_count, heads_here, F)
    piece = lax.all_gather(adapter_down, "mp", axis=1, tiled=True)
    partial_low = jnp.dot(tokens, piece, preferred_element_type=jnp.float32)
    owners = jnp.arange(piece.shape[1], dtype=jnp.int32) // R
    low_rank = jnp.where(adapter[:, None] == owners[None, :], partial_low, 0.0).astype(jnp.bfloat16)
    values = value_sum + jnp.dot(low_rank, adapter_up, preferred_element_type=jnp.float32)
    values = values.astype(jnp.bfloat16).reshape(row_count, heads_here, value_width)
    within, query_map, summary, restart = block_local(query, key_rows, values, request, starts)
    identity = (jnp.zeros((), jnp.float32), jnp.zeros_like(summary))
    _, carried = carried_in((restart, summary), "dp", combine, identity)
    gains = head_gain.reshape(heads_here, value_width)
    normed = finish(within, query_map, carried, request, starts, gains).reshape(
        row_count, heads_here * value_width
    )
    partial_terms = jnp.dot(
        normed,
        lax.all_gather(out_weight, "dp", axis=1, tiled=True),
        preferred_element_type=jnp.float32,
    )
    return lax.psum_scatter(
        partial_terms.astype(jnp.bfloat16), "mp", scatter_dimension=1, tiled=True
    )


def solution(mesh):
    placed = (
        P("dp", None),
        P("dp", "mp"),
        P("dp", "mp"),
        P("dp", "mp"),
        P(None, "mp"),
        P(None, "mp"),
        P(),
        P(),
        P("mp"),
        P("mp", "dp"),
    )
    return jax.shard_map(
        per_device, mesh=mesh, in_specs=placed, out_specs=P("dp", "mp"), check_vma=False
    )
```

profile of v0, /device:TPU:6, one launch (start us, length us, event | category | flops | bytes accessed | tf_op | source)
XLA Modules:
  0.0 530.6 jit_solution(14623870171346762429)
XLA Ops:
  9.7 52.8 %all_gather.30 = bf16[2048,32]{1,0:T(8,128)(2,1)S(1)} all-gather(bf16[32,32]{1,0:T(8,128)(2,1)} %param.14), channel_id=1, replica_groups=mesh['dp'=64,'mp'=8] {'dp'}, dimensions={0}, use_global_device_ids=true | all-gather | bytes 133120 | tf_op jit(solution)/shard_map/all_gather | solution.py:113
  64.0 1.3 compare_convert_fusion
  65.5 2.2 fusion.6
  67.7 70.5 %all-gather.6.cloned.1.call-done = bf16[2048,256]{1,0:T(8,128)(2,1)} async-done(((bf16[32,256]{1,0:T(8,128)(2,1)}), bf16[2048,256]{1,0:T(8,128)(2,1)}) %all-gather.6.cloned.1.call-update) | async-done | bytes 1048592 | tf_op jit(solution)/shard_map/all_gather | solution.py:118
  138.2 2.0 fusion.4
  140.9 1.1 convolution_convert_fusion.1
  143.5 48.5 %all_gather.29 = bf16[2048,32]{1,0:T(8,128)(2,1)S(1)} all-gather(bf16[32,32]{1,0:T(8,128)(2,1)S(1)} %copy-done.1), channel_id=1, replica_groups=mesh['dp'=64,'mp'=8] {'dp'}, dimensions={0}, use_global_device_ids=true | all-gather | bytes 133120 | tf_op jit(solution)/shard_map/all_gather | solution.py:108
  192.8 1.3 dynamic-slice
  194.1 1.4 dynamic-update-slice
  195.6 113.9 %all-reduce = bf16[64]{0:T(256)(128)(2,1)S(1)} all-reduce(bf16[64]{0:T(256)(128)(2,1)S(1)} %dynamic-update-slice), channel_id=1, replica_groups=mesh['dp'=64,'mp'=8] {'dp'}, use_global_device_ids=true, to_apply=%add | all-reduce | flops 64 | bytes 256
  309.5 2.8 fusion.1
  312.3 149.2 %while.14 = (s32[]{:T(128)}, f32[2,273,128]{2,1,0:T(8,128)S(1)}, s32[]{:T(128)}, bf16[64]{0:T(256)(128)(2,1)S(1)}, bf16[64,2,273,128]{3,2,1,0:T(8,128)(2,1)}, /*index=5*/s32[]{:T(128)}, s32[]{:T(128)}, f32[1]{0:T(128)}) while((s32[]{:T(128)}, f32[2,273,128]{2,1,0:T(8,128)S(1)}, s32[]{:T(128)}, bf16[64]{0:T(256)(128)(2,1)S(1)}, ...), condition=%wide.region_6.7_spmd.clone, body=%wide.region_5.6_spmd.clone.sunk | while | flops 349445 | bytes 699005 | solution.py:35
  315.9 1.1 fusion.52
  318.2 1.1 fusion.52
  320.6 1.1 fusion.52
  322.9 1.1 fusion.52
  325.2 1.1 fusion.52
  327.5 1.1 fusion.52
  329.9 1.1 fusion.52
  332.2 1.1 fusion.52
  334.5 1.1 fusion.52
  336.9 1.1 fusion.52
  341.5 1.1 fusion.52
  343.9 1.1 fusion.52
  346.2 1.1 fusion.52
  350.9 1.1 fusion.52
  353.2 1.1 fusion.52
  355.5 1.1 fusion.52
  360.2 1.1 fusion.52
  362.5 1.1 fusion.52
  364.9 1.1 fusion.52
  367.2 1.1 fusion.52
  369.5 1.1 fusion.52
  371.9 1.1 fusion.52
  374.2 1.1 fusion.52
  376.5 1.1 fusion.52
  378.9 1.1 fusion.52
  381.2 1.1 fusion.52
  385.9 1.1 fusion.52
  388.2 1.1 fusion.52
  390.5 1.1 fusion.52
  395.2 1.1 fusion.52
  397.5 1.1 fusion.52
  399.8 1.1 fusion.52
  404.5 1.1 fusion.52
  461.6 1.5 multiply_reduce_fusion
  463.3 3.3 convolution_convert_fusion
  466.6 57.5 %reduce-scatter.2.cloned.1.call-done = bf16[512,256]{1,0:T(8,128)(2,1)} async-done(((bf16[512,2048]{1,0:T(8,128)(2,1)}), bf16[512,256]{1,0:T(8,128)(2,1)}) %reduce-scatter.2.cloned.1.call-update) | async-done | bytes 262160 | tf_op jit(solution)/shard_map/reduce_scatter | solution.py:141
  (143 shorter events, 78.4 us)
Async XLA Ops:
  6.5 56.0 %copy-start = (bf16[512,2048]{1,0:T(8,128)(2,1)S(1)}, bf16[512,2048]{1,0:T(8,128)(2,1)}, u32[]{:S(2)}) copy-start(bf16[512,2048]{1,0:T(8,128)(2,1)} %param.12) | copy-start | bytes 6291460
  6.5 57.4 %copy-start.3 = (s32[4]{0:T(128)S(1)}, s32[4]{0:T(128)}, u32[]{:S(2)}) copy-start(s32[4]{0:T(128)} %param.19) | copy-start | bytes 52
  6.5 58.9 %copy-start.4 = (bf16[256,256]{1,0:T(8,128)(2,1)S(1)}, bf16[256,256]{1,0:T(8,128)(2,1)}, u32[]{:S(2)}) copy-start(bf16[256,256]{1,0:T(8,128)(2,1)} %param.17) | copy-start | bytes 393220
  6.5 58.9 %all-gather.8.cloned.1.call-start = ((), (), s32[]{:S(2)}) async-start(), calls=%async_computation.2 | async-start | bytes 1179648 | tf_op jit(solution)/shard_map/all_gather | solution.py:123
  7.3 130.9 %all-gather.6.cloned.1.call-start = ((), (), s32[]{:S(2)}) async-start(), calls=%async_computation.1 | async-start | bytes 1064960 | tf_op jit(solution)/shard_map/all_gather | solution.py:118
  8.0 304.3 %all-gather.12.cloned.1.call-start = ((), (), s32[]{:S(2)}) async-start(), calls=%async_computation.5 | async-start | bytes 9318400 | tf_op jit(solution)/shard_map/all_gather | solution.py:18
  140.2 0.7 copy-start.5
  140.2 3.3 copy-start.1
  142.0 321.2 %all-gather.10.cloned.1.call-start = ((), (), s32[]{:S(2)}) async-start(), calls=%async_computation.3 | async-start | bytes 1064960 | tf_op jit(solution)/shard_map/all_gather | solution.py:138
  142.6 381.5 %reduce-scatter.2.cloned.1.call-start = ((), (), s32[]{:S(2)}) async-start(), calls=%async_computation.4 | async-start | bytes 2359296 | tf_op jit(solution)/shard_map/reduce_scatter | solution.py:141
  312.3 150.8 %copy-start.2 = (f32[256]{0:T(256)S(1)}, f32[256]{0:T(256)}, u32[]{:S(2)}) copy-start(f32[256]{0:T(256)} %param.20) | copy-start | bytes 3076
Sparse Core Ops, SparseCore 0:
  9.4 46.9 all-gather.7
  59.7 78.4 all-gather.5
  142.1 86.8 all-gather.11
  232.3 80.0 all-gather.9
  466.7 57.2 reduce-scatter.1
where the time goes:
time: 533 us; the launch traced here: 531 us
  blocking collectives  215 us (40%)
  waiting for transfers between devices  130 us (24%)
  other arithmetic  72.4 us (14%)
  loops' own time  43.5 us (8%)
  local copies, waits for them, and re-layouts  41.7 us (8%)
  matrix products  14.4 us (3%)
  between operations  13.4 us (3%)
    unnamed x1, blocking collectives  114 us
    all_gather x1, waiting for transfers between devices, per_device(): lax.all_gather(v_weight, 'dp', axis=0, tiled=True)  70.5 us
    select_n x64, other arithmetic, turn(): return jax.tree.map(lambda a, b: jnp.where(reached, a, b), new, before)  68.1 us
    reduce_scatter x1, waiting for transfers between devices, per_device(): lax.psum_scatter(partial_terms.astype(jnp.bfloat16), 'mp', scatter_dimens...  57.5 us
    all_gather x1, blocking collectives, per_device(): lax.all_gather(k_weight, 'dp', axis=0, tiled=True)  52.8 us
    all_gather x1, blocking collectives, per_device(): lax.all_gather(q_weight, 'dp', axis=0, tiled=True)  48.5 us
    another operation x1, loops' own time, carried_in(): return lax.fori_loop(0, length, turn, start)  43.5 us
    dynamic_slice x64, local copies, waits for them, and re-layouts, turn(): part[k].astype(own.dtype)  37.6 us
  transfers between devices with their start and end apart: 5, of which 2 were waited for; matrix products, arithmetic and copies ran while one was open for 23% of the time, Pallas kernels for 0%

commit v1 on v0

v1 whole, which is shorter than its diff:
```python
import math

import jax
import jax.numpy as jnp
from jax import lax
from jax.sharding import PartitionSpec as P

F = 16
R = 16


EPSILON = 1e-05


def taylor(inputs):
    squares = (inputs[..., :, None] * inputs[..., None, :]).reshape(
        inputs.shape[:-1] + (inputs.shape[-1] * inputs.shape[-1],)
    )
    constant = jnp.ones(inputs.shape[:-1] + (1,), jnp.float32)
    return jnp.concatenate([constant, 0.5 * inputs, squares * (0.25 / math.sqrt(2.0))], axis=-1)


def request_of(bounds, positions):
    return jnp.sum((positions[:, None] >= bounds[None, :]).astype(jnp.int32), axis=1)


def token_tables(lengths, adapter_ids, positions):
    bounds = jnp.cumsum(lengths)
    request = request_of(bounds, positions)
    openings = bounds - lengths
    starts = jnp.any(positions[:, None] == openings[None, :], axis=1)
    picked = request[:, None] == jnp.arange(lengths.shape[0], dtype=jnp.int32)[None, :]
    adapter = jnp.sum(jnp.where(picked, adapter_ids[None, :], 0), axis=1)
    return (request, starts, adapter)


def block_local(query, key_rows, values, request, starts):
    scores = jnp.einsum("ihd,jhd->hij", query, key_rows, preferred_element_type=jnp.float32) * 0.25
    weights = 1.0 + scores + 0.5 * scores * scores
    indexes = jnp.arange(request.shape[0], dtype=jnp.int32)
    allowed = (indexes[None, :] <= indexes[:, None]) & (request[None, :] == request[:, None])
    weights = jnp.where(allowed[None], weights, 0.0).astype(jnp.bfloat16)
    within = jnp.einsum("hij,jhe->ihe", weights, values, preferred_element_type=jnp.float32)
    query_map = taylor(query.astype(jnp.float32)).astype(jnp.bfloat16)
    key_map = taylor(key_rows.astype(jnp.float32)).astype(jnp.bfloat16)
    tail_mask = (request == request[-1]).astype(jnp.bfloat16)
    masked_keys = key_map * tail_mask[:, None, None]
    summary = jnp.einsum("ihf,ihe->hfe", masked_keys, values, preferred_element_type=jnp.float32)
    return (within, query_map, summary)


def finish(within, query_map, carried, request, starts, gains):
    follows = ((request == request[0]) & jnp.logical_not(starts[0])).astype(jnp.float32)
    cross = jnp.einsum(
        "ihf,hfe->ihe", query_map, carried.astype(jnp.bfloat16), preferred_element_type=jnp.float32
    )
    combined = within + follows[:, None, None] * cross
    factor = lax.rsqrt(jnp.mean(combined * combined, axis=-1, keepdims=True) + EPSILON)
    return (combined * factor * gains[None]).astype(jnp.bfloat16)


def carry_weights(lengths, row_count, place, blocks):
    bounds = jnp.cumsum(lengths)
    firsts = jnp.arange(blocks, dtype=jnp.int32) * row_count
    tails = request_of(bounds, firsts + (row_count - 1))
    head = request_of(bounds, place[None] * row_count)[0]
    chosen = (jnp.arange(blocks, dtype=jnp.int32) < place) & (tails == head)
    return chosen.astype(jnp.bfloat16)


def per_device(
    tokens,
    q_weight,
    k_weight,
    v_weight,
    adapter_down,
    adapter_up,
    lengths,
    adapter_ids,
    head_gain,
    out_weight,
):
    row_count = tokens.shape[0]
    qf = q_weight.shape[1]
    heads_here = qf // F
    vw = v_weight.shape[1]
    value_width = vw // heads_here
    blocks = lax.axis_size("dp")
    place = lax.axis_index("dp")
    positions = place * row_count + jnp.arange(row_count, dtype=jnp.int32)
    request, starts, adapter = token_tables(lengths, adapter_ids, positions)

    local = jnp.concatenate([q_weight, k_weight, v_weight, out_weight.T], axis=1)
    gathered = lax.all_gather(local, "dp", axis=0, tiled=True)
    q_full = gathered[:, :qf]
    k_full = gathered[:, qf : 2 * qf]
    v_full = gathered[:, 2 * qf : 2 * qf + vw]
    out_t = gathered[:, 2 * qf + vw :]

    part_low = jnp.dot(tokens, adapter_down, preferred_element_type=jnp.float32)
    owners = lax.axis_index("mp") * (adapter_down.shape[1] // R) + (
        jnp.arange(adapter_down.shape[1], dtype=jnp.int32) // R
    )
    part_low = jnp.where(adapter[:, None] == owners[None, :], part_low, 0.0).astype(jnp.bfloat16)
    low_rank = lax.all_gather(part_low, "mp", axis=1, tiled=True)

    query_sum = jnp.dot(tokens, q_full, preferred_element_type=jnp.float32)
    key_sum = jnp.dot(tokens, k_full, preferred_element_type=jnp.float32)
    value_sum = jnp.dot(tokens, v_full, preferred_element_type=jnp.float32)
    query = query_sum.astype(jnp.bfloat16).reshape(row_count, heads_here, F)
    key_rows = key_sum.astype(jnp.bfloat16).reshape(row_count, heads_here, F)
    values = value_sum + jnp.dot(low_rank, adapter_up, preferred_element_type=jnp.float32)
    values = values.astype(jnp.bfloat16).reshape(row_count, heads_here, value_width)
    within, query_map, summary = block_local(query, key_rows, values, request, starts)

    every = lax.all_gather(summary.astype(jnp.bfloat16), "dp")
    chosen = carry_weights(lengths, row_count, place, blocks)
    carried = jnp.dot(
        chosen[None, :], every.reshape(blocks, -1), preferred_element_type=jnp.float32
    ).reshape(summary.shape)

    gains = head_gain.reshape(heads_here, value_width)
    normed = finish(within, query_map, carried, request, starts, gains).reshape(
        row_count, heads_here * value_width
    )
    partial_terms = lax.dot_general(
        normed, out_t, (((1,), (1,)), ((), ())), preferred_element_type=jnp.float32
    )
    return lax.psum_scatter(
        partial_terms.astype(jnp.bfloat16), "mp", scatter_dimension=1, tiled=True
    )


def solution(mesh):
    placed = (
        P("dp", None),
        P("dp", "mp"),
        P("dp", "mp"),
        P("dp", "mp"),
        P(None, "mp"),
        P(None, "mp"),
        P(),
        P(),
        P("mp"),
        P("mp", "dp"),
    )
    return jax.shard_map(
        per_device, mesh=mesh, in_specs=placed, out_specs=P("dp", "mp"), check_vma=False
    )
```

time: 533 us -> 275 us (0.52)
  the two profiles are of different devices: /device:TPU:6 before, /device:TPU:2 now
where the time goes in v1:
time: 275 us; the launch traced here: 274 us
  waiting for transfers between devices  179 us (65%)
  blocking collectives  31.1 us (11%)
  local copies, waits for them, and re-layouts  22.8 us (8%)
  matrix products  21.4 us (8%)
  between operations  13.3 us (5%)
  other arithmetic  6.59 us (2%)
    all_gather x1, waiting for transfers between devices, per_device(): every = lax.all_gather(summary.astype(jnp.bfloat16), 'dp')  82.7 us
    all_gather x1, waiting for transfers between devices, per_device(): gathered = lax.all_gather(local, 'dp', axis=0, tiled=True)  51.4 us
    reduce_scatter x1, waiting for transfers between devices, per_device(): lax.psum_scatter(partial_terms.astype(jnp.bfloat16), 'mp', scatter_dimens...  44.7 us
    all_gather x1, blocking collectives, per_device(): low_rank = lax.all_gather(part_low, 'mp', axis=1, tiled=True)  31.1 us
    dot_general x1, local copies, waits for them, and re-layouts, per_device(): jnp.dot(chosen[None, :], every.reshape(blocks, -1), preferred_element_typ...  11.1 us
    reshape x1, local copies, waits for them, and re-layouts, per_device(): every.reshape(blocks, -1)  10.9 us
    dot_general x1, matrix products, per_device(): jnp.dot(chosen[None, :], every.reshape(blocks, -1), preferred_element_typ...  5.76 us
  transfers between devices with their start and end apart: 3, of which 3 were waited for; matrix products, arithmetic and copies ran while one was open for 4% of the time, Pallas kernels for 0%

profile of v1, /device:TPU:2, one launch (start us, length us, event | category | flops | bytes accessed | tf_op | source)
XLA Modules:
  0.0 274.3 jit_solution(4233398418461733872)
XLA Ops:
  6.5 0.0 copy-start
  6.5 0.0 copy-start.1
  6.5 0.0 all-gather.4.cloned.1.call-start
  6.5 1.6 pad_maximum_fusion
  8.1 0.0 all-gather.4.cloned.1.call-update
  8.2 0.0 all-gather.6.cloned.1.call-start
  8.2 0.8 reduce-window.4
  9.1 0.7 bitcast_subtract_fusion
  9.7 0.1 compare_reduce_fusion
  9.9 0.1 convert_reduce_fusion
  10.0 0.7 fusion.43
  10.6 0.7 select_reduce_fusion
  11.4 0.0 copy-done
  11.4 1.6 fusion.7
  13.0 31.1 %all_gather.13 = bf16[512,256]{0,1:T(8,128)(2,1)S(1)} all-gather(bf16[512,32]{0,1:T(8,128)(2,1)S(1)} %fusion.7), channel_id=1, replica_groups=mesh['dp'=64,'mp'=8] {'mp'}, dimensions={1}, use_global_device_ids=true | all-gather | bytes 294912 | tf_op jit(solution)/shard_map/all_gather | solution.py:105
  44.2 1.3 compare_convert_fusion
  45.4 0.0 copy-done.1
  45.4 0.3 fusion.44
  45.7 51.4 %all-gather.4.cloned.1.call-done = bf16[2048,576]{1,0:T(8,128)(2,1)} async-done(((bf16[32,576]{1,0:T(8,128)(2,1)}), bf16[2048,576]{1,0:T(8,128)(2,1)}) %all-gather.4.cloned.1.call-update) | async-done | bytes 2359312 | tf_op jit(solution)/shard_map/all_gather | solution.py:94
  97.1 2.1 convolution_convert_fusion.2
  99.3 0.1 multiply_convert_fusion.1
  99.4 2.5 fusion.6
  101.9 1.1 convolution_convert_fusion.1
  103.0 0.0 all-gather.6.cloned.1.call-update
  103.1 0.0 reduce-scatter.2.cloned.1.call-start
  103.1 0.6 fusion.33
  103.8 0.1 convert_reduce_fusion.1
  103.9 0.2 fusion.14
  104.1 1.8 convolution_convert_fusion.3
  105.9 0.1 multiply_convert_fusion
  106.0 1.8 fusion.2
  107.8 82.7 %all-gather.6.cloned.1.call-done = bf16[128,273,128]{2,1,0:T(8,128)(2,1)} async-done(((bf16[2,273,128]{2,1,0:T(8,128)(2,1)}), bf16[128,273,128]{2,1,0:T(8,128)(2,1)}) %all-gather.6.cloned.1.call-update) | async-done | bytes 8945680 | tf_op jit(solution)/shard_map/all_gather | solution.py:116
  190.5 10.9 %reshape.177 = bf16[64,69888]{1,0:T(8,128)(2,1)} reshape(bf16[128,273,128]{2,1,0:T(8,128)(2,1)} %all-gather.6.cloned.1.call-done) | data formatting | bytes 17891328 | tf_op jit(solution)/shard_map/reshape | solution.py:119
  201.4 11.1 %dot_general.49 = bf16[2,273,128,64]{2,1,0,3:T(8,128)(2,1)} reshape(bf16[69888,64]{0,1:T(8,128)(2,1)} %bitcast.53) | data formatting | bytes 17891328 | tf_op jit(solution)/shard_map/dot_general | solution.py:118
  212.5 0.0 copy-start.3
  212.5 5.8 %fusion = bf16[1,2,273,128]{3,0,2,1:T(2,128)(2,1)S(1)} fusion(bf16[2,273,128,64]{2,1,0,3:T(8,128)(2,1)} %dot_general.49, s32[64]{0:T(128)S(1)} %convert_reduce_fusion.1, s32[]{:T(128)} %fusion.33, s32[]{:T(128)S(6)} %axis_index.23), kind=kOutput, calls=%fused_computation | convolution fusion | flops 8945856 | bytes 9085704 | tf_op jit(solution)/shard_map/dot_general | solution.py:118
  218.3 0.0 copy-start.2
  218.3 0.0 copy-done.3
  218.3 0.5 multiply_reduce_fusion
  218.8 0.1 copy-done.2
  219.0 0.1 multiply_convert_fusion.2
  219.1 3.9 %convolution_convert_fusion = bf16[512,2048]{1,0:T(8,128)(2,1)} fusion(bf16[512,256]{0,1:T(8,128)(2,1)S(1)} %bitcast.54, bf16[2048,576]{1,0:T(8,128)(2,1)} %all-gather.4.cloned.1.call-done), kind=kOutput, calls=%fused_computation.2 | convolution fusion | flops 537919488 | bytes 3407872 | tf_op jit(solution)/shard_map/dot_general | solution.py:126
  223.0 0.0 reduce-scatter.2.cloned.1.call-update
  223.0 44.7 %reduce-scatter.2.cloned.1.call-done = bf16[512,256]{1,0:T(8,128)(2,1)} async-done(((bf16[512,2048]{1,0:T(8,128)(2,1)}), bf16[512,256]{1,0:T(8,128)(2,1)}) %reduce-scatter.2.cloned.1.call-update) | async-done | bytes 262160 | tf_op jit(solution)/shard_map/reduce_scatter | solution.py:129
  (9 shorter events, 0.1 us)
Async XLA Ops:
  6.5 4.8 %copy-start = (bf16[512,2048]{1,0:T(8,128)(2,1)S(1)}, bf16[512,2048]{1,0:T(8,128)(2,1)}, u32[]{:S(2)}) copy-start(bf16[512,2048]{1,0:T(8,128)(2,1)} %param.10) | copy-start | bytes 6291460
  6.5 38.9 %copy-start.1 = (bf16[256,256]{1,0:T(8,128)(2,1)S(1)}, bf16[256,256]{1,0:T(8,128)(2,1)}, u32[]{:S(2)}) copy-start(bf16[256,256]{1,0:T(8,128)(2,1)} %param.15) | copy-start | bytes 393220
  6.5 90.6 %all-gather.4.cloned.1.call-start = ((), (), s32[]{:S(2)}) async-start(), calls=%async_computation.1 | async-start | bytes 2662400 | tf_op jit(solution)/shard_map/all_gather | solution.py:94
  8.2 182.3 %all-gather.6.cloned.1.call-start = ((), (), s32[]{:S(2)}) async-start(), calls=%async_computation.3 | async-start | bytes 9318400 | tf_op jit(solution)/shard_map/all_gather | solution.py:116
  103.1 164.7 %reduce-scatter.2.cloned.1.call-start = ((), (), s32[]{:S(2)}) async-start(), calls=%async_computation.2 | async-start | bytes 2359296 | tf_op jit(solution)/shard_map/reduce_scatter | solution.py:129
  212.5 5.8 %copy-start.3 = (f32[2,128,512]{2,1,0:T(8,128)S(1)}, f32[2,128,512]{2,1,0:T(8,128)}, u32[]{:S(2)}) copy-start(f32[2,128,512]{2,1,0:T(8,128)} %fusion.2) | copy-start | bytes 1572868
  218.3 0.7 copy-start.2
Sparse Core Ops, SparseCore 0:
  10.7 86.4 all-gather.3
  103.2 87.2 all-gather.5
  223.1 44.5 reduce-scatter.1

commit v2 on v1

--- a/solution.py
+++ b/solution.py
@@ -1,9 +1,15 @@
 import math
+
+import functools
 
 import jax
 import jax.numpy as jnp
 from jax import lax
+from jax.experimental import pallas as pl
+from jax.experimental.pallas import tpu as pltpu
 from jax.sharding import PartitionSpec as P
+
+MESH = pl.DeviceIdType.MESH
 
 F = 16
 R = 16
@@ -59,13 +65,112 @@
     return (combined * factor * gains[None]).astype(jnp.bfloat16)
 
 
-def carry_weights(lengths, row_count, place, blocks):
-    bounds = jnp.cumsum(lengths)
+def scan_masks(lengths, row_count, place, blocks, rounds):
+    openings = jnp.cumsum(lengths) - lengths
     firsts = jnp.arange(blocks, dtype=jnp.int32) * row_count
-    tails = request_of(bounds, firsts + (row_count - 1))
-    head = request_of(bounds, place[None] * row_count)[0]
-    chosen = (jnp.arange(blocks, dtype=jnp.int32) < place) & (tails == head)
-    return chosen.astype(jnp.bfloat16)
+    inside = (openings[None, :] >= firsts[:, None]) & (openings[None, :] < firsts[:, None] + row_count)
+    restarts = jnp.concatenate(
+        [jnp.zeros((1,), jnp.int32), jnp.cumsum(jnp.any(inside, axis=1).astype(jnp.int32))]
+    )
+
+    def clean(lo, hi):
+        lo = jnp.maximum(lo, 0)
+        return (restarts[hi + 1] - restarts[lo] == 0).astype(jnp.float32)
+
+    rows = []
+    for k in range(rounds):
+        d = 1 << k
+        rows.append(clean(place - d + 1, place))
+        rows.append(jnp.where(place >= 1, clean(place - d + 1, place - 1), 1.0))
+    return jnp.stack(rows)
+
+
+def scan_kernel(n, rounds, s_ref, m_ref, e_ref, parts, recv, send_sem, recv_sem):
+    me = lax.axis_index("dp")
+    col = lax.axis_index("mp")
+    barrier = pltpu.get_barrier_semaphore()
+    for k in range(rounds):
+        d = 1 << k
+
+        @pl.when(me + d < n)
+        def _():
+            pl.semaphore_signal(barrier, 1, device_id=(me + d, col), device_id_type=MESH)
+
+        @pl.when(me >= d)
+        def _():
+            pl.semaphore_signal(barrier, 1, device_id=(me - d, col), device_id_type=MESH)
+
+    peers = 0
+    for k in range(rounds):
+        d = 1 << k
+        peers = peers + (me // d + n - 1) // n + ((n - 1 - me) // d + n - 1) // n
+    pl.semaphore_wait(barrier, peers)
+
+    e_ref[...] = jnp.zeros_like(e_ref)
+    copies = []
+    for k in range(rounds):
+        d = 1 << k
+        src = s_ref if k == 0 else parts.at[k - 1]
+        copy = pltpu.make_async_remote_copy(
+            src_ref=src,
+            dst_ref=recv.at[k],
+            send_sem=send_sem.at[k],
+            recv_sem=recv_sem.at[k],
+            device_id=(me + d, col),
+            device_id_type=MESH,
+        )
+        copies.append(copy)
+
+        @pl.when(me + d < n)
+        def _():
+            copy.start()
+
+        @pl.when(me >= d)
+        def _():
+            copy.wait_recv()
+            got = recv[k]
+            if k < rounds - 1:
+                parts[k] = src[...] + m_ref[2 * k] * got
+            e_ref[...] += m_ref[2 * k + 1] * got
+
+        if k < rounds - 1:
+
+            @pl.when(me < d)
+            def _():
+                parts[k] = src[...]
+
+    for k in range(rounds):
+        d = 1 << k
+
+        @pl.when(me + d < n)
+        def _():
+            copies[k].wait_send()
+
+
+def carried_scan(summary, masks, n, rounds):
+    shape = summary.shape
+    flat = summary.reshape(-1, shape[-1])
+    size = flat.shape[0] * flat.shape[1]
+    out = pl.pallas_call(
+        functools.partial(scan_kernel, n, rounds),
+        out_shape=jax.ShapeDtypeStruct(flat.shape, jnp.float32),
+        in_specs=[
+            pl.BlockSpec(memory_space=pltpu.VMEM),
+            pl.BlockSpec(memory_space=pltpu.SMEM),
+        ],
+        out_specs=pl.BlockSpec(memory_space=pltpu.VMEM),
+        scratch_shapes=[
+            pltpu.VMEM((max(rounds - 1, 1),) + flat.shape, jnp.float32),
+            pltpu.VMEM((rounds,) + flat.shape, jnp.float32),
+            pltpu.SemaphoreType.DMA((rounds,)),
+            pltpu.SemaphoreType.DMA((rounds,)),
+        ],
+        compiler_params=pltpu.CompilerParams(collective_id=0, has_side_effects=True),
+        cost_estimate=pl.CostEstimate(
+            flops=3 * rounds * size, bytes_accessed=8 * rounds * size, transcendentals=0
+        ),
+    )(flat, masks.reshape(-1))
+    return out.reshape(shape)
 
 
 def per_device(
@@ -113,11 +218,9 @@
     values = values.astype(jnp.bfloat16).reshape(row_count, heads_here, value_width)
     within, query_map, summary = block_local(query, key_rows, values, request, starts)
 
-    every = lax.all_gather(summary.astype(jnp.bfloat16), "dp")
-    chosen = carry_weights(lengths, row_count, place, blocks)
-    carried = jnp.dot(
-        chosen[None, :], every.reshape(blocks, -1), preferred_element_type=jnp.float32
-    ).reshape(summary.shape)
+    rounds = max(1, (blocks - 1).bit_length())
+    masks = scan_masks(lengths, row_count, place, blocks, rounds)
+    carried = carried_scan(summary, masks, blocks, rounds)
 
     gains = head_gain.reshape(heads_here, value_width)
     normed = finish(within, query_map, carried, request, starts, gains).reshape(

time: 275 us -> 224 us (0.81)
  the two profiles are of different devices: /device:TPU:2 before, /device:TPU:62 now
where the time goes in v2:
time: 224 us; the launch traced here: 223 us
  waiting for transfers between devices  77 us (34%)
  Pallas kernels  58.2 us (26%)
  blocking collectives  31.3 us (14%)
  between operations  29.6 us (13%)
  matrix products  15.3 us (7%)
  other arithmetic  8.37 us (4%)
  local copies, waits for them, and re-layouts  2.77 us (1%)
    pallas_call x1, Pallas kernels, carried_scan(): pl.pallas_call(functools.partial(scan_kernel, n, rounds), out_shape=jax.S...  58.2 us
    reduce_scatter x1, waiting for transfers between devices, per_device(): lax.psum_scatter(partial_terms.astype(jnp.bfloat16), 'mp', scatter_dimens...  45.5 us
    all_gather x1, waiting for transfers between devices, per_device(): gathered = lax.all_gather(local, 'dp', axis=0, tiled=True)  31.5 us
    all_gather x1, blocking collectives, per_device(): low_rank = lax.all_gather(part_low, 'mp', axis=1, tiled=True)  31.3 us
  transfers between devices with their start and end apart: 2, of which 2 were waited for; matrix products, arithmetic and copies ran while one was open for 4% of the time, Pallas kernels for 0%

profile of v2, /device:TPU:62, one launch (start us, length us, event | category | flops | bytes accessed | tf_op | source)
XLA Modules:
  0.0 222.5 jit_solution(16788949529320907232)
XLA Ops:
  6.5 0.0 copy-start
  6.5 0.0 all-gather.2.cloned.1.call-start
  6.5 1.6 pad_maximum_fusion
  8.1 0.0 all-gather.2.cloned.1.call-update
  8.2 0.0 reduce-scatter.2.cloned.1.call-start
  8.2 0.8 reduce-window.17
  9.1 0.7 bitcast_subtract_fusion
  9.7 0.1 and_reduce_fusion
  9.8 0.1 copy.18
  9.9 0.1 reduce-window.18
  10.0 0.1 reduce
  10.1 0.1 pad_add_fusion
  10.2 0.7 fusion.35
  26.8 0.1 compare_reduce_fusion
  27.1 0.6 stack.33.m_ref
  27.6 0.1 convert_reduce_fusion
  27.7 0.6 fusion.34
  28.3 0.7 select_reduce_fusion
  29.0 0.0 copy-done
  29.1 1.6 fusion.5
  30.7 31.3 %all_gather.7 = bf16[512,256]{0,1:T(8,128)(2,1)S(1)} all-gather(bf16[512,32]{0,1:T(8,128)(2,1)S(1)} %fusion.5), channel_id=1, replica_groups=mesh['dp'=64,'mp'=8] {'mp'}, dimensions={1}, use_global_device_ids=true | all-gather | bytes 294912 | tf_op jit(solution)/shard_map/all_gather | solution.py:210
  62.0 1.2 and_convert_fusion
  63.2 0.2 fusion.12
  63.4 0.0 copy-done.2
  63.4 0.3 fusion.36
  63.7 31.5 %all-gather.2.cloned.1.call-done = bf16[2048,576]{1,0:T(8,128)(2,1)} async-done(((bf16[32,576]{1,0:T(8,128)(2,1)}), bf16[2048,576]{1,0:T(8,128)(2,1)}) %all-gather.2.cloned.1.call-update) | async-done | bytes 2359312 | tf_op jit(solution)/shard_map/all_gather | solution.py:199
  95.2 1.9 convolution_convert_fusion.2
  97.1 0.6 multiply_convert_fusion.3
  97.7 0.0 copy-done.1
  97.7 1.1 convolution_convert_fusion.1
  98.8 0.6 multiply_convert_fusion.4
  99.4 0.1 multiply_convert_fusion.1
  99.5 1.8 fusion.4
  101.4 2.8 %fusion = f32[2,128,512]{2,1,0:T(8,128)} fusion(bf16[512,2,128]{0,2,1:T(8,128)(2,1)} %bitcast.69, bf16[512,2,16]{0,2,1:T(8,128)(2,1)S(1)} %bitcast.60, bf16[512,2,16]{0,2,1:T(8,128)(2,1)S(1)} %bitcast.63, pred[512,512]{1,0:T(8,128)(4,1)S(1)} %fusion.12), kind=kOutput, calls=%fused_computation.2 | convolution fusion | flops 154664960 | bytes 1114112 | tf_op jit(solution)/shard_map/hij,jhe->ihe/dot_general | solution.py:49
  104.1 0.0 copy-done.4
  104.2 1.4 fusion.14
  105.6 0.0 copy-start.6
  105.6 0.7 reshape.255.s_ref
  106.3 58.2 %shard_map.100 = f32[546,128]{1,0:T(8,128)} custom-call(f32[546,128]{1,0:T(8,128)} %reshape.255.s_ref, f32[12]{0:T(128)} %stack.33.m_ref), custom_call_target="tpu_custom_call" | custom-call | flops 1257984 | bytes 3354624 | tf_op jit(solution)/shard_map/pallas_call | solution.py:154
  164.5 1.0 convert_element_type.178
  165.5 0.1 multiply_convert_fusion
  165.6 0.0 copy-done.3
  165.6 0.0 copy-done.6
  165.6 0.5 multiply_reduce_fusion
  166.2 0.1 multiply_convert_fusion.2
  166.3 3.9 %convolution_convert_fusion = bf16[512,2048]{1,0:T(8,128)(2,1)} fusion(bf16[512,256]{0,1:T(8,128)(2,1)S(1)} %bitcast.55, bf16[2048,576]{1,0:T(8,128)(2,1)} %all-gather.2.cloned.1.call-done), kind=kOutput, calls=%fused_computation | convolution fusion | flops 537919488 | bytes 3407872 | tf_op jit(solution)/shard_map/dot_general | solution.py:229
  170.2 0.0 reduce-scatter.2.cloned.1.call-update
  170.2 45.5 %reduce-scatter.2.cloned.1.call-done = bf16[512,256]{1,0:T(8,128)(2,1)} async-done(((bf16[512,2048]{1,0:T(8,128)(2,1)}), bf16[512,256]{1,0:T(8,128)(2,1)}) %reduce-scatter.2.cloned.1.call-update) | async-done | bytes 262160 | tf_op jit(solution)/shard_map/reduce_scatter | solution.py:232
  (15 shorter events, 0.1 us)
Async XLA Ops:
  6.5 22.5 %copy-start = (bf16[512,2048]{1,0:T(8,128)(2,1)S(1)}, bf16[512,2048]{1,0:T(8,128)(2,1)}, u32[]{:S(2)}) copy-start(bf16[512,2048]{1,0:T(8,128)(2,1)} %param.10) | copy-start | bytes 6291460
  6.5 56.9 %copy-start.2 = (bf16[256,256]{1,0:T(8,128)(2,1)S(1)}, bf16[256,256]{1,0:T(8,128)(2,1)}, u32[]{:S(2)}) copy-start(bf16[256,256]{1,0:T(8,128)(2,1)} %param.15) | copy-start | bytes 393220
  6.5 88.6 %all-gather.2.cloned.1.call-start = ((), (), s32[]{:S(2)}) async-start(), calls=%async_computation.1 | async-start | bytes 2662400 | tf_op jit(solution)/shard_map/all_gather | solution.py:199
  8.2 207.5 %reduce-scatter.2.cloned.1.call-start = ((), (), s32[]{:S(2)}) async-start(), calls=%async_computation.2 | async-start | bytes 2359296 | tf_op jit(solution)/shard_map/reduce_scatter | solution.py:232
  95.2 2.6 %copy-start.1 = (bf16[2048,576]{1,0:T(8,128)(2,1)S(1)}, bf16[2048,576]{1,0:T(8,128)(2,1)}, u32[]{:S(2)}) copy-start(bf16[2048,576]{1,0:T(8,128)(2,1)} %all-gather.2.cloned.1.call-done) | copy-start | bytes 7077892
  101.4 2.8 %copy-start.4 = (bf16[512,2,16]{0,2,1:T(8,128)(2,1)S(1)}, bf16[512,2,16]{0,2,1:T(8,128)(2,1)}, u32[]{:S(2)}) copy-start(bf16[512,2,16]{0,2,1:T(8,128)(2,1)} %multiply_convert_fusion.4) | copy-start | bytes 98308
  104.1 61.5 %copy-start.3 = (bf16[512,2,16]{0,2,1:T(8,128)(2,1)S(1)}, bf16[512,2,16]{0,2,1:T(8,128)(2,1)}, u32[]{:S(2)}) copy-start(bf16[512,2,16]{0,2,1:T(8,128)(2,1)} %multiply_convert_fusion.3) | copy-start | bytes 98308
  105.6 60.1 %copy-start.6 = (f32[2,128,512]{2,1,0:T(8,128)S(1)}, f32[2,128,512]{2,1,0:T(8,128)}, u32[]{:S(2)}) copy-start(f32[2,128,512]{2,1,0:T(8,128)} %fusion) | copy-start | bytes 1572868
  106.3 59.9 %copy-start.5 = (f32[256]{0:T(256)S(1)}, f32[256]{0:T(256)}, u32[]{:S(2)}) copy-start(f32[256]{0:T(256)} %param.18) | copy-start | bytes 3076
Sparse Core Ops, SparseCore 0:
  10.7 84.4 all-gather.1
  170.3 45.3 reduce-scatter.1

commit v3 on v2

--- a/solution.py
+++ b/solution.py
@@ -173,6 +173,105 @@
     return out.reshape(shape)
 
 
+def gather_kernel(n, m, xd_ref, xm_ref, gd_ref, gm_ref, send_d, recv_d, send_m, recv_m):
+    me = lax.axis_index("dp")
+    col = lax.axis_index("mp")
+    barrier = pltpu.get_barrier_semaphore()
+
+    def greet_dp(k, carry):
+        pl.semaphore_signal(barrier, 1, device_id=((me + k) % n, col), device_id_type=MESH)
+        return carry
+
+    def greet_mp(k, carry):
+        pl.semaphore_signal(barrier, 1, device_id=(me, (col + k) % m), device_id_type=MESH)
+        return carry
+
+    lax.fori_loop(1, n, greet_dp, 0)
+    lax.fori_loop(1, m, greet_mp, 0)
+    pl.semaphore_wait(barrier, n + m - 2)
+
+    def to_dp(k):
+        return pltpu.make_async_remote_copy(
+            src_ref=xd_ref,
+            dst_ref=gd_ref.at[me],
+            send_sem=send_d.at[k],
+            recv_sem=recv_d.at[me],
+            device_id=((me + k) % n, col),
+            device_id_type=MESH,
+        )
+
+    def to_mp(k):
+        return pltpu.make_async_remote_copy(
+            src_ref=xm_ref,
+            dst_ref=gm_ref.at[col],
+            send_sem=send_m.at[k],
+            recv_sem=recv_m.at[col],
+            device_id=(me, (col + k) % m),
+            device_id_type=MESH,
+        )
+
+    def start_mp(k, carry):
+        to_mp(k).start()
+        return carry
+
+    def start_dp(k, carry):
+        to_dp(k).start()
+        return carry
+
+    lax.fori_loop(1, m, start_mp, 0)
+    lax.fori_loop(1, n, start_dp, 0)
+    gd_ref[me] = xd_ref[...]
+    gm_ref[col] = xm_ref[...]
+
+    def land_dp(k, carry):
+        pltpu.make_async_remote_copy(
+            src_ref=xd_ref,
+            dst_ref=gd_ref.at[(me + n - k) % n],
+            send_sem=send_d.at[k],
+            recv_sem=recv_d.at[(me + n - k) % n],
+            device_id=((me + n - k) % n, col),
+            device_id_type=MESH,
+        ).wait_recv()
+        to_dp(k).wait_send()
+        return carry
+
+    def land_mp(k, carry):
+        pltpu.make_async_remote_copy(
+            src_ref=xm_ref,
+            dst_ref=gm_ref.at[(col + m - k) % m],
+            send_sem=send_m.at[k],
+            recv_sem=recv_m.at[(col + m - k) % m],
+            device_id=(me, (col + m - k) % m),
+            device_id_type=MESH,
+        ).wait_recv()
+        to_mp(k).wait_send()
+        return carry
+
+    lax.fori_loop(1, m, land_mp, 0)
+    lax.fori_loop(1, n, land_dp, 0)
+
+
+def direct_gather(xd, xm, n, m):
+    moved = n * xd.size * 2 + m * xm.size * 2
+    return pl.pallas_call(
+        functools.partial(gather_kernel, n, m),
+        out_shape=(
+            jax.ShapeDtypeStruct((n,) + xd.shape, xd.dtype),
+            jax.ShapeDtypeStruct((m,) + xm.shape, xm.dtype),
+        ),
+        in_specs=[pl.BlockSpec(memory_space=pltpu.VMEM)] * 2,
+        out_specs=(pl.BlockSpec(memory_space=pltpu.VMEM), pl.BlockSpec(memory_space=pltpu.VMEM)),
+        scratch_shapes=[
+            pltpu.SemaphoreType.DMA((n,)),
+            pltpu.SemaphoreType.DMA((n,)),
+            pltpu.SemaphoreType.DMA((m,)),
+            pltpu.SemaphoreType.DMA((m,)),
+        ],
+        compiler_params=pltpu.CompilerParams(collective_id=1, has_side_effects=True),
+        cost_estimate=pl.CostEstimate(flops=0, bytes_accessed=moved, transcendentals=0),
+    )(xd, xm)
+
+
 def per_device(
     tokens,
     q_weight,
@@ -196,18 +295,19 @@
     request, starts, adapter = token_tables(lengths, adapter_ids, positions)
 
     local = jnp.concatenate([q_weight, k_weight, v_weight, out_weight.T], axis=1)
-    gathered = lax.all_gather(local, "dp", axis=0, tiled=True)
+    part_low = jnp.dot(tokens, adapter_down, preferred_element_type=jnp.float32)
+    owners = lax.axis_index("mp") * (adapter_down.shape[1] // R) + (
+        jnp.arange(adapter_down.shape[1], dtype=jnp.int32) // R
+    )
+    part_low = jnp.where(adapter[:, None] == owners[None, :], part_low, 0.0).astype(jnp.bfloat16)
+    cols = lax.axis_size("mp")
+    gathered, low_parts = direct_gather(local, part_low, blocks, cols)
+    gathered = gathered.reshape(blocks * local.shape[0], local.shape[1])
     q_full = gathered[:, :qf]
     k_full = gathered[:, qf : 2 * qf]
     v_full = gathered[:, 2 * qf : 2 * qf + vw]
     out_t = gathered[:, 2 * qf + vw :]
-
-    part_low = jnp.dot(tokens, adapter_down, preferred_element_type=jnp.float32)
-    owners = lax.axis_index("mp") * (adapter_down.shape[1] // R) + (
-        jnp.arange(adapter_down.shape[1], dtype=jnp.int32) // R
-    )
-    part_low = jnp.where(adapter[:, None] == owners[None, :], part_low, 0.0).astype(jnp.bfloat16)
-    low_rank = lax.all_gather(part_low, "mp", axis=1, tiled=True)
+    low_rank = jnp.transpose(low_parts, (1, 0, 2)).reshape(row_count, cols * part_low.shape[1])
 
     query_sum = jnp.dot(tokens, q_full, preferred_element_type=jnp.float32)
     key_sum = jnp.dot(tokens, k_full, preferred_element_type=jnp.float32)

time: 224 us -> 244 us (1.089)
  the two profiles are of different devices: /device:TPU:62 before, /device:TPU:4 now
where the time goes in v3:
time: 244 us
  Pallas kernels  120 us (49%)
  waiting for transfers between devices  66 us (27%)
  between operations  28.3 us (12%)
  matrix products  16.6 us (7%)
  other arithmetic  9.04 us (4%)
  local copies, waits for them, and re-layouts  3.19 us (1%)
    pallas_call x1, Pallas kernels, direct_gather(): pl.pallas_call(functools.partial(gather_kernel, n, m), out_shape=(jax.Sha...  76.3 us
    reduce_scatter x1, waiting for transfers between devices, per_device(): lax.psum_scatter(partial_terms.astype(jnp.bfloat16), 'mp', scatter_dimens...  66 us
    pallas_call x1, Pallas kernels, carried_scan(): pl.pallas_call(functools.partial(scan_kernel, n, rounds), out_shape=jax.S...  44.1 us
  transfers between devices with their start and end apart: 1, of which 1 were waited for; matrix products, arithmetic and copies ran while one was open for 0% of the time, Pallas kernels for 0%

profile of v3, /device:TPU:4, one launch (start us, length us, event | category | flops | bytes accessed | tf_op | source)
XLA Modules:
  0.0 243.6 jit_solution(4175873860635058228)
XLA Ops:
  6.5 0.0 copy-start
  6.5 1.0 reduce-window.17
  7.5 0.7 bitcast_subtract_fusion
  8.2 0.1 and_reduce_fusion
  8.3 0.1 copy.21
  8.4 0.1 reduce-window.18
  8.5 0.1 reduce
  8.6 0.1 pad_add_fusion
  8.7 0.7 fusion.35
  23.9 0.1 compare_reduce_fusion
  24.0 0.1 convert_reduce_fusion
  24.1 0.6 fusion.34
  24.7 0.9 fusion.12
  25.6 0.7 select_reduce_fusion
  26.3 1.5 pad_maximum_fusion.xd_ref
  27.8 0.0 copy-done
  27.8 2.2 fusion.5.xm_ref
  30.0 76.3 %shard_map.100 = (bf16[64,32,576]{2,1,0:T(8,128)(2,1)}, bf16[8,512,32]{2,1,0:T(8,128)(2,1)}) custom-call(bf16[32,576]{1,0:T(8,128)(2,1)} %pad_maximum_fusion.xd_ref, bf16[512,32]{1,0:T(8,128)(2,1)} %fusion.5.xm_ref), custom_call_target="tpu_custom_call" | custom-call | bytes 2621440 | tf_op jit(solution)/shard_map/pallas_call | solution.py:256
  106.4 2.1 convolution_convert_fusion.1
  108.5 0.0 copy-start.1
  108.5 1.9 convolution_convert_fusion.2
  110.3 0.0 copy-start.4
  110.4 0.6 multiply_convert_fusion.3
  111.0 0.6 multiply_convert_fusion.4
  111.8 0.3 copy.19
  112.1 1.2 fusion.36
  113.3 0.0 copy-start.6
  113.3 2.6 %fusion.4 = bf16[512,256]{0,1:T(8,128)(2,1)S(1)} fusion(f32[512,256]{0,1:T(8,128)S(1)} %fusion.36, bf16[512,2048]{1,0:T(8,128)(2,1)S(1)} %copy-done, bf16[2048,576]{1,0:T(8,128)(2,1)} %bitcast.60), kind=kOutput, calls=%fused_computation.8 | convolution fusion | flops 537133056 | bytes 3932160 | tf_op jit(solution)/shard_map/dot_general | solution.py:314
  115.9 0.1 multiply_convert_fusion.1
  116.0 0.0 copy-done.3
  116.0 0.0 copy-done.5
  116.1 0.0 copy-done.6
  116.1 0.0 copy-start.8
  116.1 1.8 fusion
  117.9 1.2 and_convert_fusion
  119.1 0.4 fusion.14
  119.6 0.7 reshape.263.s_ref
  120.3 0.6 stack.33.m_ref
  120.9 44.1 %shard_map.101 = f32[546,128]{1,0:T(8,128)} custom-call(f32[546,128]{1,0:T(8,128)} %reshape.263.s_ref, f32[12]{0:T(128)} %stack.33.m_ref), custom_call_target="tpu_custom_call" | custom-call | flops 1257984 | bytes 3354624 | tf_op jit(solution)/shard_map/pallas_call | solution.py:154
  165.0 1.0 convert_element_type.178
  166.0 0.1 multiply_convert_fusion
  166.2 0.0 copy-done.7
  166.2 0.0 copy-done.10
  166.2 0.5 multiply_reduce_fusion
  166.7 0.1 multiply_convert_fusion.2
  166.8 3.9 %convolution_convert_fusion = bf16[512,2048]{1,0:T(8,128)(2,1)} fusion(bf16[512,256]{0,1:T(8,128)(2,1)S(1)} %bitcast.64, bf16[2048,576]{1,0:T(8,128)(2,1)} %bitcast.61), kind=kOutput, calls=%fused_computation | convolution fusion | flops 537919488 | bytes 3407872 | tf_op jit(solution)/shard_map/dot_general | solution.py:329
  170.7 0.0 reduce-scatter.2.cloned.1.call-update
  170.7 66.0 %reduce-scatter.2.cloned.1.call-done = bf16[512,256]{1,0:T(8,128)(2,1)} async-done(((bf16[512,2048]{1,0:T(8,128)(2,1)}), bf16[512,256]{1,0:T(8,128)(2,1)}) %reduce-scatter.2.cloned.1.call-update) | async-done | bytes 262160 | tf_op jit(solution)/shard_map/reduce_scatter | solution.py:332
  (21 shorter events, 0.1 us)
Async XLA Ops:
  6.5 21.3 %copy-start = (bf16[512,2048]{1,0:T(8,128)(2,1)S(1)}, bf16[512,2048]{1,0:T(8,128)(2,1)}, u32[]{:S(2)}) copy-start(bf16[512,2048]{1,0:T(8,128)(2,1)} %param.10) | copy-start | bytes 6291460
  6.5 230.2 %reduce-scatter.2.cloned.1.call-start = ((), (), s32[]{:S(2)}) async-start(), calls=%async_computation.1 | async-start | bytes 2359296 | tf_op jit(solution)/shard_map/reduce_scatter | solution.py:332
  108.5 3.1 %copy-start.2 = (bf16[32,512]{1,0:T(8,128)(2,1)}, bf16[32,512]{1,0:T(8,128)(2,1)S(1)}, u32[]{:S(2)}) copy-start(bf16[32,512]{1,0:T(8,128)(2,1)S(1)} %convolution_convert_fusion.1) | copy-start | bytes 98308
  108.5 3.3 %copy-start.1 = (bf16[8,512,32]{2,1,0:T(8,128)(2,1)S(1)}, bf16[8,512,32]{2,1,0:T(8,128)(2,1)}, u32[]{:S(2)}) copy-start(bf16[8,512,32]{2,1,0:T(8,128)(2,1)} %get-tuple-element.8) | copy-start | bytes 786436
  110.3 1.3 copy-start.4
  113.3 2.7 %copy-start.3 = (bf16[32,512]{1,0:T(8,128)(2,1)S(1)}, bf16[32,512]{1,0:T(8,128)(2,1)}, u32[]{:S(2)}) copy-start(bf16[32,512]{1,0:T(8,128)(2,1)} %copy-done.2) | copy-start | bytes 98308
  113.3 2.7 %copy-start.5 = (bf16[32,512]{1,0:T(8,128)(2,1)S(1)}, bf16[32,512]{1,0:T(8,128)(2,1)}, u32[]{:S(2)}) copy-start(bf16[32,512]{1,0:T(8,128)(2,1)} %copy-done.4) | copy-start | bytes 98308
  113.3 2.7 %copy-start.6 = (pred[512,512]{1,0:T(8,128)(4,1)S(1)}, pred[512,512]{1,0:T(8,128)(4,1)}, u32[]{:S(2)}) copy-start(pred[512,512]{1,0:T(8,128)(4,1)} %fusion.12) | copy-start | bytes 786436
  116.1 3.0 %copy-start.8 = (bf16[512,2,16]{0,2,1:T(8,128)(2,1)S(1)}, bf16[512,2,16]{0,2,1:T(8,128)(2,1)}, u32[]{:S(2)}) copy-start(bf16[512,2,16]{0,2,1:T(8,128)(2,1)} %multiply_convert_fusion.4) | copy-start | bytes 98308
  119.1 47.0 %copy-start.7 = (bf16[512,2,16]{0,2,1:T(8,128)(2,1)S(1)}, bf16[512,2,16]{0,2,1:T(8,128)(2,1)}, u32[]{:S(2)}) copy-start(bf16[512,2,16]{0,2,1:T(8,128)(2,1)} %multiply_convert_fusion.3) | copy-start | bytes 98308
  119.6 46.6 %copy-start.10 = (f32[2,128,512]{2,1,0:T(8,128)S(1)}, f32[2,128,512]{2,1,0:T(8,128)}, u32[]{:S(2)}) copy-start(f32[2,128,512]{2,1,0:T(8,128)} %fusion) | copy-start | bytes 1572868
  120.3 46.4 %copy-start.9 = (f32[256]{0:T(256)S(1)}, f32[256]{0:T(256)}, u32[]{:S(2)}) copy-start(f32[256]{0:T(256)} %param.18) | copy-start | bytes 3076
Sparse Core Ops, SparseCore 0:
  170.8 65.8 reduce-scatter.1

commit v4 on v3

--- a/solution.py
+++ b/solution.py
@@ -67,22 +67,16 @@
 
 def scan_masks(lengths, row_count, place, blocks, rounds):
     openings = jnp.cumsum(lengths) - lengths
-    firsts = jnp.arange(blocks, dtype=jnp.int32) * row_count
+    ids = jnp.arange(blocks, dtype=jnp.int32)
+    firsts = ids * row_count
     inside = (openings[None, :] >= firsts[:, None]) & (openings[None, :] < firsts[:, None] + row_count)
-    restarts = jnp.concatenate(
-        [jnp.zeros((1,), jnp.int32), jnp.cumsum(jnp.any(inside, axis=1).astype(jnp.int32))]
-    )
-
-    def clean(lo, hi):
-        lo = jnp.maximum(lo, 0)
-        return (restarts[hi + 1] - restarts[lo] == 0).astype(jnp.float32)
-
-    rows = []
-    for k in range(rounds):
-        d = 1 << k
-        rows.append(clean(place - d + 1, place))
-        rows.append(jnp.where(place >= 1, clean(place - d + 1, place - 1), 1.0))
-    return jnp.stack(rows)
+    flags = jnp.any(inside, axis=1).astype(jnp.int32)
+    spans = jnp.asarray([1 << (k // 2) for k in range(2 * rounds)], jnp.int32)
+    tops = place - jnp.asarray([k % 2 for k in range(2 * rounds)], jnp.int32)
+    lows = place - spans + 1
+    covered = (ids[None, :] >= lows[:, None]) & (ids[None, :] <= tops[:, None])
+    hits = jnp.sum(jnp.where(covered, flags[None, :], 0), axis=1)
+    return (hits == 0).astype(jnp.float32)
 
 
 def scan_kernel(n, rounds, s_ref, m_ref, e_ref, parts, recv, send_sem, recv_sem):
@@ -169,7 +163,7 @@
         cost_estimate=pl.CostEstimate(
             flops=3 * rounds * size, bytes_accessed=8 * rounds * size, transcendentals=0
         ),
-    )(flat, masks.reshape(-1))
+    )(flat, masks)
     return out.reshape(shape)
 
 
@@ -294,7 +288,8 @@
     positions = place * row_count + jnp.arange(row_count, dtype=jnp.int32)
     request, starts, adapter = token_tables(lengths, adapter_ids, positions)
 
-    local = jnp.concatenate([q_weight, k_weight, v_weight, out_weight.T], axis=1)
+    local = jnp.concatenate([q_weight, k_weight, v_weight], axis=1)
+    out_t = lax.all_gather(out_weight.T, "dp", axis=0, tiled=True)
     part_low = jnp.dot(tokens, adapter_down, preferred_element_type=jnp.float32)
     owners = lax.axis_index("mp") * (adapter_down.shape[1] // R) + (
         jnp.arange(adapter_down.shape[1], dtype=jnp.int32) // R
@@ -305,8 +300,7 @@
     gathered = gathered.reshape(blocks * local.shape[0], local.shape[1])
     q_full = gathered[:, :qf]
     k_full = gathered[:, qf : 2 * qf]
-    v_full = gathered[:, 2 * qf : 2 * qf + vw]
-    out_t = gathered[:, 2 * qf + vw :]
+    v_full = gathered[:, 2 * qf :]
     low_rank = jnp.transpose(low_parts, (1, 0, 2)).reshape(row_count, cols * part_low.shape[1])
 
     query_sum = jnp.dot(tokens, q_full, preferred_element_type=jnp.float32)

time: 244 us -> 205 us (0.84)
  the two profiles are of different devices: /device:TPU:4 before, /device:TPU:2 now
where the time goes in v4:
time: 205 us
  Pallas kernels  83.3 us (41%)
  waiting for transfers between devices  81.6 us (40%)
  matrix products  17.1 us (8%)
  between operations  13.7 us (7%)
  other arithmetic  7.45 us (4%)
    reduce_scatter x1, waiting for transfers between devices, per_device(): lax.psum_scatter(partial_terms.astype(jnp.bfloat16), 'mp', scatter_dimens...  80.9 us
    pallas_call x1, Pallas kernels, direct_gather(): pl.pallas_call(functools.partial(gather_kernel, n, m), out_shape=(jax.Sha...  52.3 us
    pallas_call x1, Pallas kernels, carried_scan(): pl.pallas_call(functools.partial(scan_kernel, n, rounds), out_shape=jax.S...  31 us
  transfers between devices with their start and end apart: 2, of which 1 were waited for; matrix products, arithmetic and copies ran while one was open for 11% of the time, Pallas kernels for 41%

profile of v4, /device:TPU:2, one launch (start us, length us, event | category | flops | bytes accessed | tf_op | source)
XLA Modules:
  0.0 204.9 jit_solution(17633364272897817678)
XLA Ops:
  6.5 0.0 copy-start
  6.5 0.0 all-gather.2.cloned.1.call-start
  6.5 0.7 all-gather.2.cloned.1.call-update
  7.3 0.0 reduce-scatter.2.cloned.1.call-start
  7.3 0.8 reduce-window.8
  8.2 0.7 bitcast_subtract_fusion
  8.8 0.1 convert_reduce_fusion
  8.9 0.7 fusion.34
  9.5 0.7 select_reduce_fusion.1
  10.3 1.4 pad_maximum_fusion.xd_ref
  11.7 0.0 copy-done
  11.7 2.2 %fusion.5.xm_ref = bf16[512,32]{1,0:T(8,128)(2,1)} fusion(bf16[512,2048]{1,0:T(8,128)(2,1)S(1)} %copy-done, bf16[2048,32]{0,1:T(8,128)(2,1)} %param.16, s32[32]{0:T(128)S(1)} %fusion.27, s32[512]{0:T(512)S(1)} %select_reduce_fusion.1), kind=kOutput, calls=%fused_computation.10 | convolution fusion | flops 67158016 | bytes 2263168 | tf_op jit(solution)/shard_map/dot_general | solution.py:293
  14.0 52.3 %shard_map.118 = (bf16[64,32,320]{2,1,0:T(8,128)(2,1)}, bf16[8,512,32]{2,1,0:T(8,128)(2,1)}) custom-call(bf16[32,320]{1,0:T(8,128)(2,1)} %pad_maximum_fusion.xd_ref, bf16[512,32]{1,0:T(8,128)(2,1)} %fusion.5.xm_ref), custom_call_target="tpu_custom_call" | custom-call | bytes 1572864 | tf_op jit(solution)/shard_map/pallas_call | solution.py:250
  66.3 0.0 copy-start.1
  66.3 2.2 %convolution_convert_fusion.1 = bf16[32,512]{1,0:T(8,128)(2,1)S(1)} fusion(bf16[512,2048]{1,0:T(8,128)(2,1)S(1)} %copy-done, bf16[2048,320]{1,0:T(8,128)(2,1)} %bitcast.48), kind=kOutput, calls=%fused_computation.11 | convolution fusion | flops 67125248 | bytes 2654208 | tf_op jit(solution)/shard_map/dot_general | solution.py:307
  68.5 0.1 compare_reduce_fusion
  68.6 0.0 copy-done.1
  68.6 0.3 copy.19
  69.0 1.2 fusion.35
  70.2 0.0 copy-start.3
  70.2 0.0 copy-start.4
  70.2 2.5 %fusion.4 = bf16[512,256]{0,1:T(8,128)(2,1)S(1)} fusion(f32[512,256]{0,1:T(8,128)S(1)} %fusion.35, bf16[512,2048]{1,0:T(8,128)(2,1)S(1)} %copy-done, bf16[2048,320]{1,0:T(8,128)(2,1)} %bitcast.49), kind=kOutput, calls=%fused_computation.8 | convolution fusion | flops 537133056 | bytes 3932160 | tf_op jit(solution)/shard_map/dot_general | solution.py:308
  72.7 0.1 multiply_convert_fusion.1
  72.8 0.1 and_reduce_fusion
  72.9 0.0 copy-done.3
  72.9 0.0 copy-done.4
  73.0 1.3 and_convert_fusion
  74.2 0.2 select_reduce_fusion
  74.4 0.5 fusion.13
  74.9 0.5 compare_convert_fusion.m_ref
  75.4 0.7 reshape.179.s_ref
  76.1 31.0 %shard_map.119 = f32[546,128]{1,0:T(8,128)} custom-call(f32[546,128]{1,0:T(8,128)} %reshape.179.s_ref, f32[12]{0:T(128)} %compare_convert_fusion.m_ref), custom_call_target="tpu_custom_call" | custom-call | flops 1257984 | bytes 3354624 | tf_op jit(solution)/shard_map/pallas_call | solution.py:148
  107.1 1.0 convert_element_type.97
  108.1 1.8 convolution_convert_fusion.2
  110.0 0.2 fusion.11
  110.2 0.1 multiply_convert_fusion
  110.3 0.0 copy-start.2
  110.3 1.8 fusion
  112.1 1.5 multiply_reduce_fusion
  113.7 0.0 copy-done.2
  113.7 0.1 multiply_convert_fusion.2
  113.8 0.0 all-gather.2.cloned.1.call-done
  113.8 3.3 %convolution_convert_fusion = bf16[512,2048]{1,0:T(8,128)(2,1)} fusion(bf16[512,256]{0,1:T(8,128)(2,1)S(1)} %bitcast.47, bf16[2048,256]{1,0:T(8,128)(2,1)} %all-gather.2.cloned.1.call-done), kind=kOutput, calls=%fused_computation | convolution fusion | flops 537919488 | bytes 3407872 | tf_op jit(solution)/shard_map/dot_general | solution.py:323
  117.2 0.0 reduce-scatter.2.cloned.1.call-update
  117.2 80.9 %reduce-scatter.2.cloned.1.call-done = bf16[512,256]{1,0:T(8,128)(2,1)} async-done(((bf16[512,2048]{1,0:T(8,128)(2,1)}), bf16[512,256]{1,0:T(8,128)(2,1)}) %reduce-scatter.2.cloned.1.call-update) | async-done | bytes 262160 | tf_op jit(solution)/shard_map/reduce_scatter | solution.py:326
  (12 shorter events, 0.1 us)
Async XLA Ops:
  6.5 5.2 %copy-start = (bf16[512,2048]{1,0:T(8,128)(2,1)S(1)}, bf16[512,2048]{1,0:T(8,128)(2,1)}, u32[]{:S(2)}) copy-start(bf16[512,2048]{1,0:T(8,128)(2,1)} %param.12) | copy-start | bytes 6291460
  6.5 107.3 %all-gather.2.cloned.1.call-start = ((), (), s32[]{:S(2)}) async-start(), calls=%async_computation.1 | async-start | bytes 1064960 | tf_op jit(solution)/shard_map/all_gather | solution.py:292
  7.3 190.8 %reduce-scatter.2.cloned.1.call-start = ((), (), s32[]{:S(2)}) async-start(), calls=%async_computation.2 | async-start | bytes 2359296 | tf_op jit(solution)/shard_map/reduce_scatter | solution.py:326
  66.3 2.4 %copy-start.1 = (bf16[8,512,32]{2,1,0:T(8,128)(2,1)S(1)}, bf16[8,512,32]{2,1,0:T(8,128)(2,1)}, u32[]{:S(2)}) copy-start(bf16[8,512,32]{2,1,0:T(8,128)(2,1)} %get-tuple-element.8) | copy-start | bytes 786436
  70.2 2.8 %copy-start.3 = (s32[12]{0:T(128)S(1)}, s32[12]{0:T(128)}, u32[]{:S(2)}) copy-start(s32[12]{0:T(128)} %constant.73) | copy-start | bytes 148
  70.2 2.8 %copy-start.4 = (s32[12]{0:T(128)S(1)}, s32[12]{0:T(128)}, u32[]{:S(2)}) copy-start(s32[12]{0:T(128)} %constant.74) | copy-start | bytes 148
  110.3 3.4 %copy-start.2 = (f32[256]{0:T(256)S(1)}, f32[256]{0:T(256)}, u32[]{:S(2)}) copy-start(f32[256]{0:T(256)} %param.20) | copy-start | bytes 3076
Sparse Core Ops, SparseCore 0:
  10.7 94.9 all-gather.1
  117.3 80.7 reduce-scatter.1

commit v5 on v4

--- a/solution.py
+++ b/solution.py
@@ -122,9 +122,9 @@
         @pl.when(me >= d)
         def _():
             copy.wait_recv()
-            got = recv[k]
+            got = recv[k].astype(jnp.float32)
             if k < rounds - 1:
-                parts[k] = src[...] + m_ref[2 * k] * got
+                parts[k] = (src[...].astype(jnp.float32) + m_ref[2 * k] * got).astype(parts.dtype)
             e_ref[...] += m_ref[2 * k + 1] * got
 
         if k < rounds - 1:
@@ -143,7 +143,7 @@
 
 def carried_scan(summary, masks, n, rounds):
     shape = summary.shape
-    flat = summary.reshape(-1, shape[-1])
+    flat = summary.reshape(-1, shape[-1]).astype(jnp.bfloat16)
     size = flat.shape[0] * flat.shape[1]
     out = pl.pallas_call(
         functools.partial(scan_kernel, n, rounds),
@@ -154,14 +154,14 @@
         ],
         out_specs=pl.BlockSpec(memory_space=pltpu.VMEM),
         scratch_shapes=[
-            pltpu.VMEM((max(rounds - 1, 1),) + flat.shape, jnp.float32),
-            pltpu.VMEM((rounds,) + flat.shape, jnp.float32),
+            pltpu.VMEM((max(rounds - 1, 1),) + flat.shape, jnp.bfloat16),
+            pltpu.VMEM((rounds,) + flat.shape, jnp.bfloat16),
             pltpu.SemaphoreType.DMA((rounds,)),
             pltpu.SemaphoreType.DMA((rounds,)),
         ],
         compiler_params=pltpu.CompilerParams(collective_id=0, has_side_effects=True),
         cost_estimate=pl.CostEstimate(
-            flops=3 * rounds * size, bytes_accessed=8 * rounds * size, transcendentals=0
+            flops=3 * rounds * size, bytes_accessed=6 * rounds * size, transcendentals=0
         ),
     )(flat, masks)
     return out.reshape(shape)

time: 205 us -> 179 us (0.87)
  the two profiles are of different devices: /device:TPU:2 before, /device:TPU:12 now
where the time goes in v5:
time: 179 us
  Pallas kernels  84.1 us (47%)
  waiting for transfers between devices  54.5 us (30%)
  matrix products  17.1 us (10%)
  between operations  13.7 us (8%)
  other arithmetic  7.51 us (4%)
    reduce_scatter x1, waiting for transfers between devices, per_device(): lax.psum_scatter(partial_terms.astype(jnp.bfloat16), 'mp', scatter_dimens...  53.8 us
    pallas_call x1, Pallas kernels, direct_gather(): pl.pallas_call(functools.partial(gather_kernel, n, m), out_shape=(jax.Sha...  50.9 us
    pallas_call x1, Pallas kernels, carried_scan(): pl.pallas_call(functools.partial(scan_kernel, n, rounds), out_shape=jax.S...  33.3 us
  transfers between devices with their start and end apart: 2, of which 1 were waited for; matrix products, arithmetic and copies ran while one was open for 13% of the time, Pallas kernels for 47%

profile of v5, /device:TPU:12, one launch (start us, length us, event | category | flops | bytes accessed | tf_op | source)
XLA Modules:
  0.0 178.6 jit_solution(6821320605216818984)
XLA Ops:
  6.5 0.0 copy-start
  6.5 0.0 all-gather.2.cloned.1.call-start
  6.5 0.7 all-gather.2.cloned.1.call-update
  7.3 0.0 reduce-scatter.2.cloned.1.call-start
  7.3 0.8 reduce-window.8
  8.2 0.7 bitcast_subtract_fusion
  8.8 0.1 convert_reduce_fusion
  8.9 0.7 fusion.33
  9.5 0.7 select_reduce_fusion.1
  10.3 1.4 pad_maximum_fusion.xd_ref
  11.7 0.0 copy-done
  11.7 2.2 %fusion.5.xm_ref = bf16[512,32]{1,0:T(8,128)(2,1)} fusion(bf16[512,2048]{1,0:T(8,128)(2,1)S(1)} %copy-done, bf16[2048,32]{0,1:T(8,128)(2,1)} %param.16, s32[32]{0:T(128)S(1)} %fusion.26, s32[512]{0:T(512)S(1)} %select_reduce_fusion.1), kind=kOutput, calls=%fused_computation.11 | convolution fusion | flops 67158016 | bytes 2263168 | tf_op jit(solution)/shard_map/dot_general | solution.py:293
  14.0 50.9 %shard_map.118 = (bf16[64,32,320]{2,1,0:T(8,128)(2,1)}, bf16[8,512,32]{2,1,0:T(8,128)(2,1)}) custom-call(bf16[32,320]{1,0:T(8,128)(2,1)} %pad_maximum_fusion.xd_ref, bf16[512,32]{1,0:T(8,128)(2,1)} %fusion.5.xm_ref), custom_call_target="tpu_custom_call" | custom-call | bytes 1572864 | tf_op jit(solution)/shard_map/pallas_call | solution.py:250
  64.8 0.0 copy-start.1
  64.8 2.2 %convolution_convert_fusion.2 = bf16[32,512]{1,0:T(8,128)(2,1)S(1)} fusion(bf16[512,2048]{1,0:T(8,128)(2,1)S(1)} %copy-done, bf16[2048,320]{1,0:T(8,128)(2,1)} %bitcast.48), kind=kOutput, calls=%fused_computation.12 | convolution fusion | flops 67125248 | bytes 2654208 | tf_op jit(solution)/shard_map/dot_general | solution.py:307
  67.1 0.1 compare_reduce_fusion
  67.2 0.0 copy-done.1
  67.2 0.3 copy.19
  67.5 1.2 fusion.34
  68.7 0.0 copy-start.3
  68.7 0.0 copy-start.4
  68.7 2.5 %fusion.4 = bf16[512,256]{0,1:T(8,128)(2,1)S(1)} fusion(f32[512,256]{0,1:T(8,128)S(1)} %fusion.34, bf16[512,2048]{1,0:T(8,128)(2,1)S(1)} %copy-done, bf16[2048,320]{1,0:T(8,128)(2,1)} %bitcast.49), kind=kOutput, calls=%fused_computation.8 | convolution fusion | flops 537133056 | bytes 3932160 | tf_op jit(solution)/shard_map/dot_general | solution.py:308
  71.3 0.1 multiply_convert_fusion.1
  71.4 0.1 and_reduce_fusion
  71.5 0.0 copy-done.3
  71.5 0.0 copy-done.4
  71.5 1.3 and_convert_fusion
  72.8 0.2 select_reduce_fusion
  73.0 0.5 convolution_convert_fusion.1
  73.4 0.6 compare_convert_fusion.m_ref
  74.0 0.7 convert_element_type.101.s_ref
  74.7 33.3 %shard_map.119 = f32[546,128]{1,0:T(8,128)} custom-call(bf16[546,128]{1,0:T(8,128)(2,1)} %convert_element_type.101.s_ref, f32[12]{0:T(128)} %compare_convert_fusion.m_ref), custom_call_target="tpu_custom_call" | custom-call | flops 1257984 | bytes 2515968 | tf_op jit(solution)/shard_map/pallas_call | solution.py:148
  108.0 1.0 convert_element_type.104
  109.0 1.8 convolution_convert_fusion.3
  110.8 0.2 fusion.11
  111.0 0.1 multiply_convert_fusion
  111.1 0.0 copy-start.2
  111.2 1.8 %fusion = f32[2,128,512]{2,1,0:T(8,128)} fusion(bf16[512,2,128]{0,2,1:T(8,128)(2,1)S(1)} %bitcast.65, bf16[512,2,16]{0,2,1:T(8,128)(2,1)S(1)} %bitcast.58, bf16[512,2,16]{0,2,1:T(8,128)(2,1)S(1)} %bitcast.55, pred[512,512]{1,0:T(8,128)(4,1)S(1)} %fusion.11), kind=kOutput, calls=%fused_computation.2 | convolution fusion | flops 154664960 | bytes 1114112 | tf_op jit(solution)/shard_map/hij,jhe->ihe/dot_general | solution.py:49
  113.0 1.5 multiply_reduce_fusion
  114.5 0.0 copy-done.2
  114.5 0.1 multiply_convert_fusion.2
  114.6 0.0 all-gather.2.cloned.1.call-done
  114.7 3.3 %convolution_convert_fusion = bf16[512,2048]{1,0:T(8,128)(2,1)} fusion(bf16[512,256]{0,1:T(8,128)(2,1)S(1)} %bitcast.47, bf16[2048,256]{1,0:T(8,128)(2,1)} %all-gather.2.cloned.1.call-done), kind=kOutput, calls=%fused_computation | convolution fusion | flops 537919488 | bytes 3407872 | tf_op jit(solution)/shard_map/dot_general | solution.py:323
  118.0 0.0 reduce-scatter.2.cloned.1.call-update
  118.0 53.8 %reduce-scatter.2.cloned.1.call-done = bf16[512,256]{1,0:T(8,128)(2,1)} async-done(((bf16[512,2048]{1,0:T(8,128)(2,1)}), bf16[512,256]{1,0:T(8,128)(2,1)}) %reduce-scatter.2.cloned.1.call-update) | async-done | bytes 262160 | tf_op jit(solution)/shard_map/reduce_scatter | solution.py:326
  (12 shorter events, 0.1 us)
Async XLA Ops:
  6.5 5.2 %copy-start = (bf16[512,2048]{1,0:T(8,128)(2,1)S(1)}, bf16[512,2048]{1,0:T(8,128)(2,1)}, u32[]{:S(2)}) copy-start(bf16[512,2048]{1,0:T(8,128)(2,1)} %param.12) | copy-start | bytes 6291460
  6.5 108.1 %all-gather.2.cloned.1.call-start = ((), (), s32[]{:S(2)}) async-start(), calls=%async_computation.1 | async-start | bytes 1064960 | tf_op jit(solution)/shard_map/all_gather | solution.py:292
  7.3 164.6 %reduce-scatter.2.cloned.1.call-start = ((), (), s32[]{:S(2)}) async-start(), calls=%async_computation.2 | async-start | bytes 2359296 | tf_op jit(solution)/shard_map/reduce_scatter | solution.py:326
  64.8 2.4 %copy-start.1 = (bf16[8,512,32]{2,1,0:T(8,128)(2,1)S(1)}, bf16[8,512,32]{2,1,0:T(8,128)(2,1)}, u32[]{:S(2)}) copy-start(bf16[8,512,32]{2,1,0:T(8,128)(2,1)} %get-tuple-element.8) | copy-start | bytes 786436
  68.7 2.8 %copy-start.3 = (s32[12]{0:T(128)S(1)}, s32[12]{0:T(128)}, u32[]{:S(2)}) copy-start(s32[12]{0:T(128)} %constant.73) | copy-start | bytes 148
  68.7 2.8 %copy-start.4 = (s32[12]{0:T(128)S(1)}, s32[12]{0:T(128)}, u32[]{:S(2)}) copy-start(s32[12]{0:T(128)} %constant.74) | copy-start | bytes 148
  111.1 3.4 %copy-start.2 = (f32[256]{0:T(256)S(1)}, f32[256]{0:T(256)}, u32[]{:S(2)}) copy-start(f32[256]{0:T(256)} %param.20) | copy-start | bytes 3076
Sparse Core Ops, SparseCore 0:
  10.7 94.5 all-gather.1
  118.2 53.5 reduce-scatter.1

commit v6 on v5

--- a/solution.py
+++ b/solution.py
@@ -167,30 +167,74 @@
     return out.reshape(shape)
 
 
-def gather_kernel(n, m, xd_ref, xm_ref, gd_ref, gm_ref, send_d, recv_d, send_m, recv_m):
+def gather_kernel(n, m, row, xd_ref, xm_ref, gd_ref, gm_ref, send_r, recv_r, send_c, recv_c, send_m, recv_m, own):
     me = lax.axis_index("dp")
     col = lax.axis_index("mp")
+    rows = n // row
+    pos = me % row
+    rid = me // row
+    base = rid * row
     barrier = pltpu.get_barrier_semaphore()
 
-    def greet_dp(k, carry):
-        pl.semaphore_signal(barrier, 1, device_id=((me + k) % n, col), device_id_type=MESH)
+    def greet_row(k, carry):
+        pl.semaphore_signal(barrier, 1, device_id=(base + (pos + k) % row, col), device_id_type=MESH)
+        return carry
+
+    def greet_col(j, carry):
+        pl.semaphore_signal(barrier, 1, device_id=((me + row * j) % n, col), device_id_type=MESH)
         return carry
 
     def greet_mp(k, carry):
         pl.semaphore_signal(barrier, 1, device_id=(me, (col + k) % m), device_id_type=MESH)
         return carry
 
-    lax.fori_loop(1, n, greet_dp, 0)
+    lax.fori_loop(1, row, greet_row, 0)
+    lax.fori_loop(1, rows, greet_col, 0)
     lax.fori_loop(1, m, greet_mp, 0)
-    pl.semaphore_wait(barrier, n + m - 2)
-
-    def to_dp(k):
+    pl.semaphore_wait(barrier, row + rows + m - 3)
+
+    mine = pltpu.make_async_copy(xd_ref, gd_ref.at[me], own)
+    mine.start()
+
+    def to_row(k):
         return pltpu.make_async_remote_copy(
             src_ref=xd_ref,
             dst_ref=gd_ref.at[me],
-            send_sem=send_d.at[k],
-            recv_sem=recv_d.at[me],
-            device_id=((me + k) % n, col),
+            send_sem=send_r.at[k],
+            recv_sem=recv_r.at[pos],
+            device_id=(base + (pos + k) % row, col),
+            device_id_type=MESH,
+        )
+
+    def from_row(k):
+        other = (pos + row - k) % row
+        return pltpu.make_async_remote_copy(
+            src_ref=xd_ref,
+            dst_ref=gd_ref.at[base + other],
+            send_sem=send_r.at[k],
+            recv_sem=recv_r.at[other],
+            device_id=(base + other, col),
+            device_id_type=MESH,
+        )
+
+    def to_col(j):
+        return pltpu.make_async_remote_copy(
+            src_ref=gd_ref.at[pl.ds(base, row)],
+            dst_ref=gd_ref.at[pl.ds(base, row)],
+            send_sem=send_c.at[j],
+            recv_sem=recv_c.at[rid],
+            device_id=((me + row * j) % n, col),
+            device_id_type=MESH,
+        )
+
+    def from_col(j):
+        other = (rid + rows - j) % rows
+        return pltpu.make_async_remote_copy(
+            src_ref=gd_ref.at[pl.ds(other * row, row)],
+            dst_ref=gd_ref.at[pl.ds(other * row, row)],
+            send_sem=send_c.at[j],
+            recv_sem=recv_c.at[other],
+            device_id=((me + n - row * j) % n, col),
             device_id_type=MESH,
         )
 
@@ -204,51 +248,42 @@
             device_id_type=MESH,
         )
 
-    def start_mp(k, carry):
-        to_mp(k).start()
-        return carry
-
-    def start_dp(k, carry):
-        to_dp(k).start()
-        return carry
-
-    lax.fori_loop(1, m, start_mp, 0)
-    lax.fori_loop(1, n, start_dp, 0)
-    gd_ref[me] = xd_ref[...]
+    def from_mp(k):
+        other = (col + m - k) % m
+        return pltpu.make_async_remote_copy(
+            src_ref=xm_ref,
+            dst_ref=gm_ref.at[other],
+            send_sem=send_m.at[k],
+            recv_sem=recv_m.at[other],
+            device_id=(me, other),
+            device_id_type=MESH,
+        )
+
+    def each(lo, hi, body):
+        def step(k, carry):
+            body(k)
+            return carry
+
+        lax.fori_loop(lo, hi, step, 0)
+
+    each(1, m, lambda k: to_mp(k).start())
+    each(1, row, lambda k: to_row(k).start())
     gm_ref[col] = xm_ref[...]
-
-    def land_dp(k, carry):
-        pltpu.make_async_remote_copy(
-            src_ref=xd_ref,
-            dst_ref=gd_ref.at[(me + n - k) % n],
-            send_sem=send_d.at[k],
-            recv_sem=recv_d.at[(me + n - k) % n],
-            device_id=((me + n - k) % n, col),
-            device_id_type=MESH,
-        ).wait_recv()
-        to_dp(k).wait_send()
-        return carry
-
-    def land_mp(k, carry):
-        pltpu.make_async_remote_copy(
-            src_ref=xm_ref,
-            dst_ref=gm_ref.at[(col + m - k) % m],
-            send_sem=send_m.at[k],
-            recv_sem=recv_m.at[(col + m - k) % m],
-            device_id=(me, (col + m - k) % m),
-            device_id_type=MESH,
-        ).wait_recv()
-        to_mp(k).wait_send()
-        return carry
-
-    lax.fori_loop(1, m, land_mp, 0)
-    lax.fori_loop(1, n, land_dp, 0)
+    each(1, row, lambda k: from_row(k).wait_recv())
+    mine.wait()
+    each(1, rows, lambda j: to_col(j).start())
+    each(1, m, lambda k: from_mp(k).wait_recv())
+    each(1, rows, lambda j: from_col(j).wait_recv())
+    each(1, row, lambda k: to_row(k).wait_send())
+    each(1, rows, lambda j: to_col(j).wait_send())
+    each(1, m, lambda k: to_mp(k).wait_send())
 
 
 def direct_gather(xd, xm, n, m):
+    row = 16 if n % 16 == 0 else n
     moved = n * xd.size * 2 + m * xm.size * 2
     return pl.pallas_call(
-        functools.partial(gather_kernel, n, m),
+        functools.partial(gather_kernel, n, m, row),
         out_shape=(
             jax.ShapeDtypeStruct((n,) + xd.shape, xd.dtype),
             jax.ShapeDtypeStruct((m,) + xm.shape, xm.dtype),
@@ -256,10 +291,13 @@
         in_specs=[pl.BlockSpec(memory_space=pltpu.VMEM)] * 2,
         out_specs=(pl.BlockSpec(memory_space=pltpu.VMEM), pl.BlockSpec(memory_space=pltpu.VMEM)),
         scratch_shapes=[
-            pltpu.SemaphoreType.DMA((n,)),
-            pltpu.SemaphoreType.DMA((n,)),
+            pltpu.SemaphoreType.DMA((row,)),
+            pltpu.SemaphoreType.DMA((row,)),
+            pltpu.SemaphoreType.DMA((n // row,)),
+            pltpu.SemaphoreType.DMA((n // row,)),
             pltpu.SemaphoreType.DMA((m,)),
             pltpu.SemaphoreType.DMA((m,)),
+            pltpu.SemaphoreType.DMA(()),
         ],
         compiler_params=pltpu.CompilerParams(collective_id=1, has_side_effects=True),
         cost_estimate=pl.CostEstimate(flops=0, bytes_accessed=moved, transcendentals=0),

time: 179 us -> 182 us (1.017)
  the two profiles are of different devices: /device:TPU:12 before, /device:TPU:18 now
where the time goes in v6:
time: 182 us; the launch traced here: 181 us
  Pallas kernels  92.8 us (51%)
  waiting for transfers between devices  48.4 us (27%)
  matrix products  17.1 us (9%)
  between operations  13.7 us (8%)
  other arithmetic  7.51 us (4%)
    pallas_call x1, Pallas kernels, direct_gather(): pl.pallas_call(functools.partial(gather_kernel, n, m, row), out_shape=(ja...  58.3 us
    reduce_scatter x1, waiting for transfers between devices, per_device(): lax.psum_scatter(partial_terms.astype(jnp.bfloat16), 'mp', scatter_dimens...  47.7 us
    pallas_call x1, Pallas kernels, carried_scan(): pl.pallas_call(functools.partial(scan_kernel, n, rounds), out_shape=jax.S...  34.5 us
  transfers between devices with their start and end apart: 2, of which 1 were waited for; matrix products, arithmetic and copies ran while one was open for 13% of the time, Pallas kernels for 51%

profile of v6, /device:TPU:18, one launch (start us, length us, event | category | flops | bytes accessed | tf_op | source)
XLA Modules:
  0.0 181.2 jit_solution(1419592699872999457)
XLA Ops:
  6.5 0.0 copy-start
  6.5 0.0 all-gather.2.cloned.1.call-start
  6.5 0.7 all-gather.2.cloned.1.call-update
  7.3 0.0 reduce-scatter.2.cloned.1.call-start
  7.3 0.8 reduce-window.8
  8.2 0.7 bitcast_subtract_fusion
  8.8 0.1 convert_reduce_fusion
  8.9 0.7 fusion.33
  9.5 0.7 select_reduce_fusion.1
  10.3 1.4 pad_maximum_fusion.xd_ref
  11.7 0.0 copy-done
  11.7 2.3 %fusion.5.xm_ref = bf16[512,32]{1,0:T(8,128)(2,1)} fusion(bf16[512,2048]{1,0:T(8,128)(2,1)S(1)} %copy-done, bf16[2048,32]{0,1:T(8,128)(2,1)} %param.16, s32[32]{0:T(128)S(1)} %fusion.26, s32[512]{0:T(512)S(1)} %select_reduce_fusion.1), kind=kOutput, calls=%fused_computation.11 | convolution fusion | flops 67158016 | bytes 2263168 | tf_op jit(solution)/shard_map/dot_general | solution.py:331
  14.0 58.3 %shard_map.118 = (bf16[64,32,320]{2,1,0:T(8,128)(2,1)}, bf16[8,512,32]{2,1,0:T(8,128)(2,1)}) custom-call(bf16[32,320]{1,0:T(8,128)(2,1)} %pad_maximum_fusion.xd_ref, bf16[512,32]{1,0:T(8,128)(2,1)} %fusion.5.xm_ref), custom_call_target="tpu_custom_call" | custom-call | bytes 1572864 | tf_op jit(solution)/shard_map/pallas_call | solution.py:285
  72.3 0.0 copy-start.1
  72.3 2.2 %convolution_convert_fusion.2 = bf16[32,512]{1,0:T(8,128)(2,1)S(1)} fusion(bf16[512,2048]{1,0:T(8,128)(2,1)S(1)} %copy-done, bf16[2048,320]{1,0:T(8,128)(2,1)} %bitcast.48), kind=kOutput, calls=%fused_computation.12 | convolution fusion | flops 67125248 | bytes 2654208 | tf_op jit(solution)/shard_map/dot_general | solution.py:345
  74.5 0.1 compare_reduce_fusion
  74.6 0.0 copy-done.1
  74.7 0.3 copy.19
  75.0 1.2 fusion.34
  76.2 0.0 copy-start.3
  76.2 0.0 copy-start.4
  76.2 2.5 %fusion.4 = bf16[512,256]{0,1:T(8,128)(2,1)S(1)} fusion(f32[512,256]{0,1:T(8,128)S(1)} %fusion.34, bf16[512,2048]{1,0:T(8,128)(2,1)S(1)} %copy-done, bf16[2048,320]{1,0:T(8,128)(2,1)} %bitcast.49), kind=kOutput, calls=%fused_computation.8 | convolution fusion | flops 537133056 | bytes 3932160 | tf_op jit(solution)/shard_map/dot_general | solution.py:346
  78.7 0.1 multiply_convert_fusion.1
  78.8 0.1 and_reduce_fusion
  78.9 0.0 copy-done.3
  79.0 0.0 copy-done.4
  79.0 1.3 and_convert_fusion
  80.2 0.2 select_reduce_fusion
  80.4 0.5 convolution_convert_fusion.1
  80.9 0.6 compare_convert_fusion.m_ref
  81.5 0.7 convert_element_type.101.s_ref
  82.1 34.5 %shard_map.119 = f32[546,128]{1,0:T(8,128)} custom-call(bf16[546,128]{1,0:T(8,128)(2,1)} %convert_element_type.101.s_ref, f32[12]{0:T(128)} %compare_convert_fusion.m_ref), custom_call_target="tpu_custom_call" | custom-call | flops 1257984 | bytes 2515968 | tf_op jit(solution)/shard_map/pallas_call | solution.py:148
  116.7 1.0 convert_element_type.104
  117.7 1.8 convolution_convert_fusion.3
  119.5 0.2 fusion.11
  119.7 0.1 multiply_convert_fusion
  119.8 0.0 copy-start.2
  119.9 1.8 %fusion = f32[2,128,512]{2,1,0:T(8,128)} fusion(bf16[512,2,128]{0,2,1:T(8,128)(2,1)S(1)} %bitcast.65, bf16[512,2,16]{0,2,1:T(8,128)(2,1)S(1)} %bitcast.58, bf16[512,2,16]{0,2,1:T(8,128)(2,1)S(1)} %bitcast.55, pred[512,512]{1,0:T(8,128)(4,1)S(1)} %fusion.11), kind=kOutput, calls=%fused_computation.2 | convolution fusion | flops 154664960 | bytes 1114112 | tf_op jit(solution)/shard_map/hij,jhe->ihe/dot_general | solution.py:49
  121.7 1.5 multiply_reduce_fusion
  123.2 0.0 copy-done.2
  123.2 0.1 multiply_convert_fusion.2
  123.4 0.0 all-gather.2.cloned.1.call-done
  123.4 3.3 %convolution_convert_fusion = bf16[512,2048]{1,0:T(8,128)(2,1)} fusion(bf16[512,256]{0,1:T(8,128)(2,1)S(1)} %bitcast.47, bf16[2048,256]{1,0:T(8,128)(2,1)} %all-gather.2.cloned.1.call-done), kind=kOutput, calls=%fused_computation | convolution fusion | flops 537919488 | bytes 3407872 | tf_op jit(solution)/shard_map/dot_general | solution.py:361
  126.7 0.0 reduce-scatter.2.cloned.1.call-update
  126.8 47.7 %reduce-scatter.2.cloned.1.call-done = bf16[512,256]{1,0:T(8,128)(2,1)} async-done(((bf16[512,2048]{1,0:T(8,128)(2,1)}), bf16[512,256]{1,0:T(8,128)(2,1)}) %reduce-scatter.2.cloned.1.call-update) | async-done | bytes 262160 | tf_op jit(solution)/shard_map/reduce_scatter | solution.py:364
  (12 shorter events, 0.1 us)
Async XLA Ops:
  6.5 5.2 %copy-start = (bf16[512,2048]{1,0:T(8,128)(2,1)S(1)}, bf16[512,2048]{1,0:T(8,128)(2,1)}, u32[]{:S(2)}) copy-start(bf16[512,2048]{1,0:T(8,128)(2,1)} %param.12) | copy-start | bytes 6291460
  6.5 116.8 %all-gather.2.cloned.1.call-start = ((), (), s32[]{:S(2)}) async-start(), calls=%async_computation.1 | async-start | bytes 1064960 | tf_op jit(solution)/shard_map/all_gather | solution.py:330
  7.3 167.2 %reduce-scatter.2.cloned.1.call-start = ((), (), s32[]{:S(2)}) async-start(), calls=%async_computation.2 | async-start | bytes 2359296 | tf_op jit(solution)/shard_map/reduce_scatter | solution.py:364
  72.3 2.4 %copy-start.1 = (bf16[8,512,32]{2,1,0:T(8,128)(2,1)S(1)}, bf16[8,512,32]{2,1,0:T(8,128)(2,1)}, u32[]{:S(2)}) copy-start(bf16[8,512,32]{2,1,0:T(8,128)(2,1)} %get-tuple-element.8) | copy-start | bytes 786436
  76.2 2.8 %copy-start.3 = (s32[12]{0:T(128)S(1)}, s32[12]{0:T(128)}, u32[]{:S(2)}) copy-start(s32[12]{0:T(128)} %constant.73) | copy-start | bytes 148
  76.2 2.8 %copy-start.4 = (s32[12]{0:T(128)S(1)}, s32[12]{0:T(128)}, u32[]{:S(2)}) copy-start(s32[12]{0:T(128)} %constant.74) | copy-start | bytes 148
  119.8 3.4 %copy-start.2 = (f32[256]{0:T(256)S(1)}, f32[256]{0:T(256)}, u32[]{:S(2)}) copy-start(f32[256]{0:T(256)} %param.20) | copy-start | bytes 3076
Sparse Core Ops, SparseCore 0:
  10.7 96.5 all-gather.1
  126.9 47.4 reduce-scatter.1

commit v7 on v5

--- a/solution.py
+++ b/solution.py
@@ -266,6 +266,99 @@
     )(xd, xm)
 
 
+def ring_kernel(m, x_ref, o_ref, acc_a, acc_b, got_a, got_b, send_a, recv_a, send_b, recv_b):
+    me = lax.axis_index("dp")
+    col = lax.axis_index("mp")
+    right = (col + 1) % m
+    left = (col + m - 1) % m
+    width = o_ref.shape[1]
+    half = width // 2
+    barrier = pltpu.get_barrier_semaphore()
+    pl.semaphore_signal(barrier, 1, device_id=(me, right), device_id_type=MESH)
+    pl.semaphore_signal(barrier, 1, device_id=(me, left), device_id_type=MESH)
+    pl.semaphore_wait(barrier, 2)
+
+    def piece(t, side):
+        return pl.ds(pl.multiple_of(t * width + side * half, half), half)
+
+    copies = []
+    for s in range(m - 1):
+        ta = (col + 2 * m - 1 - s) % m
+        tb = (col + 1 + s) % m
+        if s == 0:
+            src_a = x_ref.at[:, piece(ta, 0)]
+            src_b = x_ref.at[:, piece(tb, 1)]
+        else:
+            copies[-1][0].wait_recv()
+            copies[-1][1].wait_recv()
+            acc_a[s - 1] = (
+                got_a[s - 1].astype(jnp.float32) + x_ref[:, piece(ta, 0)].astype(jnp.float32)
+            ).astype(acc_a.dtype)
+            acc_b[s - 1] = (
+                got_b[s - 1].astype(jnp.float32) + x_ref[:, piece(tb, 1)].astype(jnp.float32)
+            ).astype(acc_b.dtype)
+            src_a = acc_a.at[s - 1]
+            src_b = acc_b.at[s - 1]
+        ca = pltpu.make_async_remote_copy(
+            src_ref=src_a,
+            dst_ref=got_a.at[s],
+            send_sem=send_a.at[s],
+            recv_sem=recv_a.at[s],
+            device_id=(me, right),
+            device_id_type=MESH,
+        )
+        cb = pltpu.make_async_remote_copy(
+            src_ref=src_b,
+            dst_ref=got_b.at[s],
+            send_sem=send_b.at[s],
+            recv_sem=recv_b.at[s],
+            device_id=(me, left),
+            device_id_type=MESH,
+        )
+        ca.start()
+        cb.start()
+        copies.append((ca, cb))
+    copies[-1][0].wait_recv()
+    copies[-1][1].wait_recv()
+    last = m - 2
+    o_ref[:, :half] = (
+        got_a[last].astype(jnp.float32) + x_ref[:, piece(col, 0)].astype(jnp.float32)
+    ).astype(o_ref.dtype)
+    o_ref[:, half:] = (
+        got_b[last].astype(jnp.float32) + x_ref[:, piece(col, 1)].astype(jnp.float32)
+    ).astype(o_ref.dtype)
+    for ca, cb in copies:
+        ca.wait_send()
+        cb.wait_send()
+
+
+def ring_scatter(x, m):
+    rows, total = x.shape
+    width = total // m
+    half = width // 2
+    slot = (m - 1, rows, half)
+    return pl.pallas_call(
+        functools.partial(ring_kernel, m),
+        out_shape=jax.ShapeDtypeStruct((rows, width), x.dtype),
+        in_specs=[pl.BlockSpec(memory_space=pltpu.VMEM)],
+        out_specs=pl.BlockSpec(memory_space=pltpu.VMEM),
+        scratch_shapes=[
+            pltpu.VMEM(slot, x.dtype),
+            pltpu.VMEM(slot, x.dtype),
+            pltpu.VMEM(slot, x.dtype),
+            pltpu.VMEM(slot, x.dtype),
+            pltpu.SemaphoreType.DMA((m - 1,)),
+            pltpu.SemaphoreType.DMA((m - 1,)),
+            pltpu.SemaphoreType.DMA((m - 1,)),
+            pltpu.SemaphoreType.DMA((m - 1,)),
+        ],
+        compiler_params=pltpu.CompilerParams(collective_id=2, has_side_effects=True),
+        cost_estimate=pl.CostEstimate(
+            flops=2 * rows * total, bytes_accessed=4 * rows * total, transcendentals=0
+        ),
+    )(x)
+
+
 def per_device(
     tokens,
     q_weight,
@@ -323,9 +416,7 @@
     partial_terms = lax.dot_general(
         normed, out_t, (((1,), (1,)), ((), ())), preferred_element_type=jnp.float32
     )
-    return lax.psum_scatter(
-        partial_terms.astype(jnp.bfloat16), "mp", scatter_dimension=1, tiled=True
-    )
+    return ring_scatter(partial_terms.astype(jnp.bfloat16), cols)
 
 
 def solution(mesh):

time: 179 us -> 179 us (level)
  the two profiles are of different devices: /device:TPU:12 before, /device:TPU:58 now
where the time goes in v7:
time: 179 us; the launch traced here: 178 us
  Pallas kernels  136 us (76%)
  matrix products  17.1 us (10%)
  between operations  13.7 us (8%)
  other arithmetic  7.51 us (4%)
  local copies, waits for them, and re-layouts  3.39 us (2%)
    pallas_call x1, Pallas kernels, direct_gather(): pl.pallas_call(functools.partial(gather_kernel, n, m), out_shape=(jax.Sha...  49 us
    pallas_call x1, Pallas kernels, ring_scatter(): pl.pallas_call(functools.partial(ring_kernel, m), out_shape=jax.ShapeDtyp...  46.5 us
    pallas_call x1, Pallas kernels, carried_scan(): pl.pallas_call(functools.partial(scan_kernel, n, rounds), out_shape=jax.S...  40.3 us
  transfers between devices with their start and end apart: 1, of which 0 were waited for; matrix products, arithmetic and copies ran while one was open for 13% of the time, Pallas kernels for 50%

profile of v7, /device:TPU:58, one launch (start us, length us, event | category | flops | bytes accessed | tf_op | source)
XLA Modules:
  0.0 178.2 jit_solution(11645619216280488460)
XLA Ops:
  6.5 0.0 copy-start
  6.5 0.0 all-gather.2.cloned.1.call-start
  6.5 0.7 all-gather.2.cloned.1.call-update
  7.3 0.8 reduce-window.8
  8.1 0.7 bitcast_subtract_fusion
  8.8 0.1 convert_reduce_fusion
  8.8 0.7 fusion.33
  9.5 0.7 select_reduce_fusion.1
  10.2 1.4 pad_maximum_fusion.xd_ref
  11.7 0.0 copy-done
  11.7 2.2 %fusion.5.xm_ref = bf16[512,32]{1,0:T(8,128)(2,1)} fusion(bf16[512,2048]{1,0:T(8,128)(2,1)S(1)} %copy-done, bf16[2048,32]{0,1:T(8,128)(2,1)} %param.16, s32[32]{0:T(128)S(1)} %fusion.26, s32[512]{0:T(512)S(1)} %select_reduce_fusion.1), kind=kOutput, calls=%fused_computation.11 | convolution fusion | flops 67158016 | bytes 2263168 | tf_op jit(solution)/shard_map/dot_general | solution.py:386
  13.9 49.0 %shard_map.118 = (bf16[64,32,320]{2,1,0:T(8,128)(2,1)}, bf16[8,512,32]{2,1,0:T(8,128)(2,1)}) custom-call(bf16[32,320]{1,0:T(8,128)(2,1)} %pad_maximum_fusion.xd_ref, bf16[512,32]{1,0:T(8,128)(2,1)} %fusion.5.xm_ref), custom_call_target="tpu_custom_call" | custom-call | bytes 1572864 | tf_op jit(solution)/shard_map/pallas_call | solution.py:250
  63.0 0.0 copy-start.1
  63.0 2.2 %convolution_convert_fusion.2 = bf16[32,512]{1,0:T(8,128)(2,1)S(1)} fusion(bf16[512,2048]{1,0:T(8,128)(2,1)S(1)} %copy-done, bf16[2048,320]{1,0:T(8,128)(2,1)} %bitcast.48), kind=kOutput, calls=%fused_computation.12 | convolution fusion | flops 67125248 | bytes 2654208 | tf_op jit(solution)/shard_map/dot_general | solution.py:400
  65.2 0.1 compare_reduce_fusion
  65.3 0.0 copy-done.1
  65.4 0.3 copy.19
  65.7 1.2 fusion.34
  66.9 0.0 copy-start.3
  66.9 0.0 copy-start.4
  66.9 2.5 %fusion.4 = bf16[512,256]{0,1:T(8,128)(2,1)S(1)} fusion(f32[512,256]{0,1:T(8,128)S(1)} %fusion.34, bf16[512,2048]{1,0:T(8,128)(2,1)S(1)} %copy-done, bf16[2048,320]{1,0:T(8,128)(2,1)} %bitcast.49), kind=kOutput, calls=%fused_computation.8 | convolution fusion | flops 537133056 | bytes 3932160 | tf_op jit(solution)/shard_map/dot_general | solution.py:401
  69.4 0.1 multiply_convert_fusion.1
  69.5 0.1 and_reduce_fusion
  69.6 0.0 copy-done.3
  69.6 0.0 copy-done.4
  69.7 1.3 and_convert_fusion
  70.9 0.2 select_reduce_fusion
  71.1 0.5 convolution_convert_fusion.1
  71.6 0.6 compare_convert_fusion.m_ref
  72.1 0.7 convert_element_type.101.s_ref
  72.8 40.3 %shard_map.119 = f32[546,128]{1,0:T(8,128)} custom-call(bf16[546,128]{1,0:T(8,128)(2,1)} %convert_element_type.101.s_ref, f32[12]{0:T(128)} %compare_convert_fusion.m_ref), custom_call_target="tpu_custom_call" | custom-call | flops 1257984 | bytes 2515968 | tf_op jit(solution)/shard_map/pallas_call | solution.py:148
  113.1 1.0 convert_element_type.104
  114.1 1.8 convolution_convert_fusion.3
  116.0 0.2 fusion.11
  116.2 0.1 multiply_convert_fusion
  116.3 0.0 copy-start.2
  116.3 1.8 %fusion = f32[2,128,512]{2,1,0:T(8,128)} fusion(bf16[512,2,128]{0,2,1:T(8,128)(2,1)S(1)} %bitcast.65, bf16[512,2,16]{0,2,1:T(8,128)(2,1)S(1)} %bitcast.58, bf16[512,2,16]{0,2,1:T(8,128)(2,1)S(1)} %bitcast.55, pred[512,512]{1,0:T(8,128)(4,1)S(1)} %fusion.11), kind=kOutput, calls=%fused_computation.2 | convolution fusion | flops 154664960 | bytes 1114112 | tf_op jit(solution)/shard_map/hij,jhe->ihe/dot_general | solution.py:49
  118.1 1.5 multiply_reduce_fusion
  119.7 0.0 copy-done.2
  119.7 0.1 multiply_convert_fusion.2
  119.8 0.0 all-gather.2.cloned.1.call-done
  119.8 3.3 %convolution_convert_fusion.x_ref = bf16[512,2048]{1,0:T(8,128)(2,1)} fusion(bf16[512,256]{0,1:T(8,128)(2,1)S(1)} %bitcast.47, bf16[2048,256]{1,0:T(8,128)(2,1)} %all-gather.2.cloned.1.call-done), kind=kOutput, calls=%fused_computation | convolution fusion | flops 537919488 | bytes 3407872 | tf_op jit(solution)/shard_map/dot_general | solution.py:416
  123.2 46.5 %shard_map.120 = bf16[512,256]{1,0:T(8,128)(2,1)} custom-call(bf16[512,2048]{1,0:T(8,128)(2,1)} %convolution_convert_fusion.x_ref), custom_call_target="tpu_custom_call" | custom-call | flops 2097152 | bytes 4194304 | tf_op jit(solution)/shard_map/pallas_call | solution.py:340
  169.7 1.7 copy.24
  (12 shorter events, 0.1 us)
Async XLA Ops:
  6.5 5.1 %copy-start = (bf16[512,2048]{1,0:T(8,128)(2,1)S(1)}, bf16[512,2048]{1,0:T(8,128)(2,1)}, u32[]{:S(2)}) copy-start(bf16[512,2048]{1,0:T(8,128)(2,1)} %param.12) | copy-start | bytes 6291460
  6.5 113.3 %all-gather.2.cloned.1.call-start = ((), (), s32[]{:S(2)}) async-start(), calls=%async_computation | async-start | bytes 1064960 | tf_op jit(solution)/shard_map/all_gather | solution.py:385
  63.0 2.4 %copy-start.1 = (bf16[8,512,32]{2,1,0:T(8,128)(2,1)S(1)}, bf16[8,512,32]{2,1,0:T(8,128)(2,1)}, u32[]{:S(2)}) copy-start(bf16[8,512,32]{2,1,0:T(8,128)(2,1)} %get-tuple-element.8) | copy-start | bytes 786436
  66.9 2.8 %copy-start.3 = (s32[12]{0:T(128)S(1)}, s32[12]{0:T(128)}, u32[]{:S(2)}) copy-start(s32[12]{0:T(128)} %constant.73) | copy-start | bytes 148
  66.9 2.8 %copy-start.4 = (s32[12]{0:T(128)S(1)}, s32[12]{0:T(128)}, u32[]{:S(2)}) copy-start(s32[12]{0:T(128)} %constant.74) | copy-start | bytes 148
  116.3 3.4 %copy-start.2 = (f32[256]{0:T(256)S(1)}, f32[256]{0:T(256)}, u32[]{:S(2)}) copy-start(f32[256]{0:T(256)} %param.20) | copy-start | bytes 3076
Sparse Core Ops, SparseCore 0:
  10.7 92.9 all-gather.1

commit v8 on v7

--- a/solution.py
+++ b/solution.py
@@ -359,6 +359,19 @@
     )(x)
 
 
+def doubling_gather(piece, n, place):
+    held = piece
+    step = 1
+    while step < n:
+        other = lax.ppermute(held, "dp", perm=[(i, i ^ step) for i in range(n)])
+        low = (place // step) % 2 == 0
+        held = jnp.where(
+            low, jnp.concatenate([held, other], axis=0), jnp.concatenate([other, held], axis=0)
+        )
+        step *= 2
+    return held
+
+
 def per_device(
     tokens,
     q_weight,
@@ -382,7 +395,7 @@
     request, starts, adapter = token_tables(lengths, adapter_ids, positions)
 
     local = jnp.concatenate([q_weight, k_weight, v_weight], axis=1)
-    out_t = lax.all_gather(out_weight.T, "dp", axis=0, tiled=True)
+    out_t = doubling_gather(out_weight.T, blocks, place)
     part_low = jnp.dot(tokens, adapter_down, preferred_element_type=jnp.float32)
     owners = lax.axis_index("mp") * (adapter_down.shape[1] // R) + (
         jnp.arange(adapter_down.shape[1], dtype=jnp.int32) // R

time: 179 us -> 223 us (1.25)
  the two profiles are of different devices: /device:TPU:58 before, /device:TPU:52 now
where the time goes in v8:
time: 223 us; the launch traced here: 222 us
  Pallas kernels  139 us (62%)
  waiting for transfers between devices  31.9 us (14%)
  matrix products  19 us (9%)
  starting transfers between devices  14.3 us (6%)
  other arithmetic  12.3 us (6%)
  local copies, waits for them, and re-layouts  4.94 us (2%)
    pallas_call x1, Pallas kernels, direct_gather(): pl.pallas_call(functools.partial(gather_kernel, n, m), out_shape=(jax.Sha...  51.5 us
    pallas_call x1, Pallas kernels, ring_scatter(): pl.pallas_call(functools.partial(ring_kernel, m), out_shape=jax.ShapeDtyp...  47.7 us
    pallas_call x1, Pallas kernels, carried_scan(): pl.pallas_call(functools.partial(scan_kernel, n, rounds), out_shape=jax.S...  39.8 us
    ppermute x6, waiting for transfers between devices, doubling_gather(): other = lax.ppermute(held, 'dp', perm=[(i, i ^ step) for i in range(n)])  31.9 us
    ppermute x6, starting transfers between devices, doubling_gather(): other = lax.ppermute(held, 'dp', perm=[(i, i ^ step) for i in range(n)])  14.3 us
  transfers between devices with their start and end apart: 6, of which 4 were waited for; matrix products, arithmetic and copies ran while one was open for 13% of the time, Pallas kernels for 41%

profile of v8, /device:TPU:52, one launch (start us, length us, event | category | flops | bytes accessed | tf_op | source)
XLA Modules:
  0.0 221.8 jit_solution(4318441058821753913)
XLA Ops:
  0.0 2.0 collective-permute-start
  2.1 0.8 reduce-window.8
  2.9 0.1 convert_reduce_fusion
  3.0 0.7 select_reduce_fusion.1
  3.7 1.4 pad_maximum_fusion.xd_ref
  5.2 2.2 %fusion.5.xm_ref = bf16[512,32]{1,0:T(8,128)(2,1)} fusion(bf16[512,2048]{1,0:T(8,128)(2,1)S(1)} %copy-done, bf16[2048,32]{0,1:T(8,128)(2,1)} %param.16, s32[32]{0:T(128)S(1)} %fusion.32, s32[512]{0:T(512)S(1)} %select_reduce_fusion.1), kind=kOutput, calls=%fused_computation.11 | convolution fusion | flops 67158016 | bytes 2263168 | tf_op jit(solution)/shard_map/dot_general | solution.py:399
  7.4 51.5 %shard_map.118 = (bf16[64,32,320]{2,1,0:T(8,128)(2,1)}, bf16[8,512,32]{2,1,0:T(8,128)(2,1)}) custom-call(bf16[32,320]{1,0:T(8,128)(2,1)} %pad_maximum_fusion.xd_ref, bf16[512,32]{1,0:T(8,128)(2,1)} %fusion.5.xm_ref), custom_call_target="tpu_custom_call" | custom-call | bytes 1572864 | tf_op jit(solution)/shard_map/pallas_call | solution.py:250
  58.9 1.8 convolution_convert_fusion.3
  60.7 0.0 copy-start.9
  60.7 2.2 convolution_convert_fusion.2
  62.9 0.9 fusion.16
  63.8 0.6 multiply_convert_fusion.4
  64.5 0.6 fusion.40
  65.1 0.3 copy.19
  65.4 1.2 fusion.41
  66.6 2.5 %fusion.4 = bf16[512,256]{0,1:T(8,128)(2,1)S(1)} fusion(f32[512,256]{0,1:T(8,128)S(1)} %fusion.41, bf16[512,2048]{1,0:T(8,128)(2,1)S(1)} %copy-done, bf16[2048,320]{1,0:T(8,128)(2,1)} %bitcast.48), kind=kOutput, calls=%fused_computation.8 | convolution fusion | flops 537133056 | bytes 3932160 | tf_op jit(solution)/shard_map/dot_general | solution.py:414
  69.1 0.0 copy-start.7
  69.2 0.1 multiply_convert_fusion.1
  69.3 0.1 compare_reduce_fusion
  69.4 0.1 multiply_convert_fusion
  69.6 1.2 and_convert_fusion
  70.8 1.1 convolution_convert_fusion.1
  71.9 0.6 multiply_convert_fusion.3
  72.5 0.8 maximum_select_fusion.6
  73.3 4.6 %collective-permute-start.1 = (bf16[64,256]{1,0:T(8,128)(2,1)S(1)}, bf16[64,256]{1,0:T(8,128)(2,1)S(1)}, u32[]{:S(2)}, u32[]{:S(2)}) collective-permute-start(bf16[64,256]{1,0:T(8,128)(2,1)S(1)} %maximum_select_fusion.6), channel_id=1, source_target_pairs={{0,16},{8,24},{16,0},{24,8},{32,48},{40,56},{48,32},{56,40},{64,80... | collective-permute-start | bytes 98312 | tf_op jit(solution)/shard_map/ppermute | solution.py:366
  78.0 1.8 collective-permute-done.1
  79.8 1.9 collective-permute-start.2
  81.7 5.7 %collective-permute-done.2 = bf16[128,256]{1,0:T(8,128)(2,1)S(1)} collective-permute-done((bf16[128,256]{1,0:T(8,128)(2,1)S(1)}, bf16[128,256]{1,0:T(8,128)(2,1)S(1)}, u32[]{:S(2)}, u32[]{:S(2)}) %collective-permute-start.2) | collective-permute-done | bytes 65568 | tf_op jit(solution)/shard_map/ppermute | solution.py:366
  87.5 1.9 collective-permute-start.3
  89.4 0.1 and_reduce_fusion
  89.5 0.2 select_reduce_fusion
  89.7 4.6 %collective-permute-done.3 = bf16[256,256]{1,0:T(8,128)(2,1)S(1)} collective-permute-done((bf16[256,256]{1,0:T(8,128)(2,1)S(1)}, bf16[256,256]{1,0:T(8,128)(2,1)S(1)}, u32[]{:S(2)}, u32[]{:S(2)}) %collective-permute-start.3) | collective-permute-done | bytes 131104 | tf_op jit(solution)/shard_map/ppermute | solution.py:366
  94.3 0.1 maximum_select_fusion.3
  94.4 1.9 collective-permute-start.4
  96.4 0.5 compare_convert_fusion.m_ref
  96.9 1.6 convert_element_type.101.s_ref
  98.5 39.8 %shard_map.119 = f32[546,128]{1,0:T(8,128)} custom-call(bf16[546,128]{1,0:T(8,128)(2,1)} %convert_element_type.101.s_ref, f32[12]{0:T(128)} %compare_convert_fusion.m_ref), custom_call_target="tpu_custom_call" | custom-call | flops 1257984 | bytes 2515968 | tf_op jit(solution)/shard_map/pallas_call | solution.py:148
  138.3 1.0 convert_element_type.104
  139.3 0.7 convert_element_type.105
  140.0 2.8 %fusion = f32[2,128,512]{2,1,0:T(8,128)} fusion(bf16[512,2,128]{0,2,1:T(8,128)(2,1)} %bitcast.65, bf16[512,2,16]{0,2,1:T(8,128)(2,1)S(1)} %bitcast.53, bf16[512,2,16]{0,2,1:T(8,128)(2,1)S(1)} %bitcast.56, pred[512,512]{1,0:T(8,128)(4,1)S(1)} %copy-done.2), kind=kOutput, calls=%fused_computation.2 | convolution fusion | flops 154664960 | bytes 1114112 | tf_op jit(solution)/shard_map/hij,jhe->ihe/dot_general | solution.py:49
  142.7 2.0 maximum_select_fusion.2
  144.7 1.9 collective-permute-start.5
  146.7 1.6 multiply_reduce_fusion
  148.3 0.8 multiply_convert_fusion.2
  149.1 19.7 %collective-permute-done.5 = bf16[1024,256]{1,0:T(8,128)(2,1)} collective-permute-done((bf16[1024,256]{1,0:T(8,128)(2,1)}, bf16[1024,256]{1,0:T(8,128)(2,1)}, u32[]{:S(2)}, u32[]{:S(2)}) %collective-permute-start.5) | collective-permute-done | bytes 524320 | tf_op jit(solution)/shard_map/ppermute | solution.py:366
  168.8 3.7 %convolution_convert_fusion.x_ref = bf16[512,2048]{1,0:T(8,128)(2,1)} fusion(bf16[512,256]{0,1:T(8,128)(2,1)S(1)} %bitcast.57, bf16[1024,256]{1,0:T(8,128)(2,1)} %collective-permute-done.5, bf16[1024,256]{1,0:T(8,128)(2,1)} %maximum_select_fusion.2, pred[]{:T(512)S(6)} %eq.118), kind=kOutput, calls=%fused_computation | convolution fusion | flops 542638080 | bytes 3407873 | tf_op jit(solution)/shard_map/dot_general | solution.py:429
  172.5 47.7 %shard_map.120 = bf16[512,256]{1,0:T(8,128)(2,1)} custom-call(bf16[512,2048]{1,0:T(8,128)(2,1)} %convolution_convert_fusion.x_ref), custom_call_target="tpu_custom_call" | custom-call | flops 2097152 | bytes 4194304 | tf_op jit(solution)/shard_map/pallas_call | solution.py:340
  220.1 1.7 copy.24
  (34 shorter events, 0.2 us)
Async XLA Ops:
  0.0 5.2 %copy-start = (bf16[512,2048]{1,0:T(8,128)(2,1)S(1)}, bf16[512,2048]{1,0:T(8,128)(2,1)}, u32[]{:S(2)}) copy-start(bf16[512,2048]{1,0:T(8,128)(2,1)} %param.12) | copy-start | bytes 6291460
  0.0 72.5 %collective-permute-start = (bf16[32,256]{1,0:T(8,128)(2,1)}, bf16[32,256]{1,0:T(8,128)(2,1)}, u32[]{:S(2)}, u32[]{:S(2)}) collective-permute-start(bf16[32,256]{1,0:T(8,128)(2,1)} %bitcast.58), channel_id=1, source_target_pairs={{0,8},{8,0},{16,24},{24,16},{32,40},{40,32},{48,56},{56,48},{64,72... | collective-permute-start | bytes 49160 | tf_op jit(solution)/shard_map/ppermute | solution.py:366
  60.7 4.4 %copy-start.9 = (s32[4]{0:T(128)S(1)}, s32[4]{0:T(128)}, u32[]{:S(2)}) copy-start(s32[4]{0:T(128)} %param.18) | copy-start | bytes 52
  60.7 4.3 %copy-start.1 = (bf16[8,512,32]{2,1,0:T(8,128)(2,1)S(1)}, bf16[8,512,32]{2,1,0:T(8,128)(2,1)}, u32[]{:S(2)}) copy-start(bf16[8,512,32]{2,1,0:T(8,128)(2,1)} %get-tuple-element.8) | copy-start | bytes 786436
  66.6 4.2 %copy-start.4 = (bf16[512,2,16]{0,2,1:T(8,128)(2,1)S(1)}, bf16[512,2,16]{0,2,1:T(8,128)(2,1)}, u32[]{:S(2)}) copy-start(bf16[512,2,16]{0,2,1:T(8,128)(2,1)} %multiply_convert_fusion.4) | copy-start | bytes 98308
  69.1 2.7 %copy-start.10 = (bf16[512,256]{0,1:T(8,128)(2,1)}, bf16[512,256]{0,1:T(8,128)(2,1)S(1)}, u32[]{:S(2)}) copy-start(bf16[512,256]{0,1:T(8,128)(2,1)S(1)} %fusion.4) | copy-start | bytes 786436
  69.1 3.4 %copy-start.5 = (bf16[256,32]{0,1:T(8,128)(2,1)S(1)}, bf16[256,32]{0,1:T(8,128)(2,1)}, u32[]{:S(2)}) copy-start(bf16[256,32]{0,1:T(8,128)(2,1)} %param.21) | copy-start | bytes 49156
  69.1 8.7 %copy-start.7 = (s32[12]{0:T(128)S(1)}, s32[12]{0:T(128)}, u32[]{:S(2)}) copy-start(s32[12]{0:T(128)} %constant.159) | copy-start | bytes 148
  69.2 8.7 %copy-start.8 = (s32[12]{0:T(128)S(1)}, s32[12]{0:T(128)}, u32[]{:S(2)}) copy-start(s32[12]{0:T(128)} %constant.160) | copy-start | bytes 148
  69.6 69.7 %copy-start.6 = (bf16[273]{0:T(512)(128)(2,1)}, bf16[273]{0:T(512)(128)(2,1)S(1)}, u32[]{:S(2)}) copy-start(bf16[273]{0:T(512)(128)(2,1)S(1)} %pad.27.clone) | copy-start | bytes 1642
  70.8 69.2 %copy-start.2 = (pred[512,512]{1,0:T(8,128)(4,1)S(1)}, pred[512,512]{1,0:T(8,128)(4,1)}, u32[]{:S(2)}) copy-start(pred[512,512]{1,0:T(8,128)(4,1)} %fusion.16) | copy-start | bytes 786436
  73.3 6.5 %collective-permute-start.1 = (bf16[64,256]{1,0:T(8,128)(2,1)S(1)}, bf16[64,256]{1,0:T(8,128)(2,1)S(1)}, u32[]{:S(2)}, u32[]{:S(2)}) collective-permute-start(bf16[64,256]{1,0:T(8,128)(2,1)S(1)} %maximum_select_fusion.6), channel_id=1, source_target_pairs={{0,16},{8,24},{16,0},{24,8},{32,48},{40,56},{48,32},{56,40},{64,80... | collective-permute-start | bytes 98312 | tf_op jit(solution)/shard_map/ppermute | solution.py:366
  79.8 7.7 %collective-permute-start.2 = (bf16[128,256]{1,0:T(8,128)(2,1)S(1)}, bf16[128,256]{1,0:T(8,128)(2,1)S(1)}, u32[]{:S(2)}, u32[]{:S(2)}) collective-permute-start(bf16[128,256]{1,0:T(8,128)(2,1)S(1)} %maximum_select_fusion.5), channel_id=1, source_target_pairs={{0,32},{8,40},{16,48},{24,56},{32,0},{40,8},{48,16},{56,24},{64,96... | collective-permute-start | bytes 196616 | tf_op jit(solution)/shard_map/ppermute | solution.py:366
  87.5 6.9 %collective-permute-start.3 = (bf16[256,256]{1,0:T(8,128)(2,1)S(1)}, bf16[256,256]{1,0:T(8,128)(2,1)S(1)}, u32[]{:S(2)}, u32[]{:S(2)}) collective-permute-start(bf16[256,256]{1,0:T(8,128)(2,1)S(1)} %maximum_select_fusion.4), channel_id=1, source_target_pairs={{0,64},{8,72},{16,80},{24,88},{32,96},{40,104},{48,112},{56,120},{... | collective-permute-start | bytes 393224 | tf_op jit(solution)/shard_map/ppermute | solution.py:366
  94.4 48.3 %collective-permute-start.4 = (bf16[512,256]{1,0:T(8,128)(2,1)S(1)}, bf16[512,256]{1,0:T(8,128)(2,1)}, u32[]{:S(2)}, u32[]{:S(2)}) collective-permute-start(bf16[512,256]{1,0:T(8,128)(2,1)S(1)} %maximum_select_fusion.3), channel_id=1, source_target_pairs={{0,128},{8,136},{16,144},{24,152},{32,160},{40,168},{48,176},{56,1... | collective-permute-start | bytes 786440 | tf_op jit(solution)/shard_map/ppermute | solution.py:366
  140.0 6.7 %copy-start.3 = (bf16[2,273,128]{2,1,0:T(8,128)(2,1)S(1)}, bf16[2,273,128]{2,1,0:T(8,128)(2,1)}, u32[]{:S(2)}) copy-start(bf16[2,273,128]{2,1,0:T(8,128)(2,1)} %convert_element_type.105) | copy-start | bytes 419332
  144.7 24.1 %collective-permute-start.5 = (bf16[1024,256]{1,0:T(8,128)(2,1)}, bf16[1024,256]{1,0:T(8,128)(2,1)}, u32[]{:S(2)}, u32[]{:S(2)}) collective-permute-start(bf16[1024,256]{1,0:T(8,128)(2,1)} %maximum_select_fusion.2), channel_id=1, source_target_pairs={{0,256},{8,264},{16,272},{24,280},{32,288},{40,296},{48,304},{56,3... | collective-permute-start | bytes 1572872 | tf_op jit(solution)/shard_map/ppermute | solution.py:366

commit v9 on v7

--- a/solution.py
+++ b/solution.py
@@ -167,32 +167,69 @@
     return out.reshape(shape)
 
 
-def gather_kernel(n, m, xd_ref, xm_ref, gd_ref, gm_ref, send_d, recv_d, send_m, recv_m):
+def gather_kernel(n, m, xd_ref, xm_ref, gd_ref, gm_ref, send_d, recv_d, send_x, recv_x, send_m, recv_m, own):
     me = lax.axis_index("dp")
     col = lax.axis_index("mp")
+    chips = n // 2
+    side = me % 2
+    chip = me // 2
+    mate = me + 1 - 2 * side
     barrier = pltpu.get_barrier_semaphore()
 
-    def greet_dp(k, carry):
-        pl.semaphore_signal(barrier, 1, device_id=((me + k) % n, col), device_id_type=MESH)
-        return carry
-
-    def greet_mp(k, carry):
-        pl.semaphore_signal(barrier, 1, device_id=(me, (col + k) % m), device_id_type=MESH)
-        return carry
-
-    lax.fori_loop(1, n, greet_dp, 0)
-    lax.fori_loop(1, m, greet_mp, 0)
-    pl.semaphore_wait(barrier, n + m - 2)
-
-    def to_dp(k):
+    def each(lo, hi, body):
+        def step(k, carry):
+            body(k)
+            return carry
+
+        lax.fori_loop(lo, hi, step, 0)
+
+    each(1, chips, lambda k: pl.semaphore_signal(
+        barrier, 1, device_id=((me + 2 * k) % n, col), device_id_type=MESH))
+    pl.semaphore_signal(barrier, 1, device_id=(mate, col), device_id_type=MESH)
+    each(1, m, lambda k: pl.semaphore_signal(
+        barrier, 1, device_id=(me, (col + k) % m), device_id_type=MESH))
+    pl.semaphore_wait(barrier, chips + m - 1)
+
+    mine = pltpu.make_async_copy(xd_ref, gd_ref.at[side, chip], own)
+    mine.start()
+
+    def to_far(k):
         return pltpu.make_async_remote_copy(
             src_ref=xd_ref,
-            dst_ref=gd_ref.at[me],
+            dst_ref=gd_ref.at[side, chip],
             send_sem=send_d.at[k],
-            recv_sem=recv_d.at[me],
-            device_id=((me + k) % n, col),
-            device_id_type=MESH,
-        )
+            recv_sem=recv_d.at[chip],
+            device_id=((me + 2 * k) % n, col),
+            device_id_type=MESH,
+        )
+
+    def from_far(k):
+        other = (chip + chips - k) % chips
+        return pltpu.make_async_remote_copy(
+            src_ref=xd_ref,
+            dst_ref=gd_ref.at[side, other],
+            send_sem=send_d.at[k],
+            recv_sem=recv_d.at[other],
+            device_id=(2 * other + side, col),
+            device_id_type=MESH,
+        )
+
+    swap_out = pltpu.make_async_remote_copy(
+        src_ref=gd_ref.at[side],
+        dst_ref=gd_ref.at[side],
+        send_sem=send_x,
+        recv_sem=recv_x,
+        device_id=(mate, col),
+        device_id_type=MESH,
+    )
+    swap_in = pltpu.make_async_remote_copy(
+        src_ref=gd_ref.at[1 - side],
+        dst_ref=gd_ref.at[1 - side],
+        send_sem=send_x,
+        recv_sem=recv_x,
+        device_id=(mate, col),
+        device_id_type=MESH,
+    )
 
     def to_mp(k):
         return pltpu.make_async_remote_copy(
@@ -204,66 +241,53 @@
             device_id_type=MESH,
         )
 
-    def start_mp(k, carry):
-        to_mp(k).start()
-        return carry
-
-    def start_dp(k, carry):
-        to_dp(k).start()
-        return carry
-
-    lax.fori_loop(1, m, start_mp, 0)
-    lax.fori_loop(1, n, start_dp, 0)
-    gd_ref[me] = xd_ref[...]
+    def from_mp(k):
+        other = (col + m - k) % m
+        return pltpu.make_async_remote_copy(
+            src_ref=xm_ref,
+            dst_ref=gm_ref.at[other],
+            send_sem=send_m.at[k],
+            recv_sem=recv_m.at[other],
+            device_id=(me, other),
+            device_id_type=MESH,
+        )
+
+    each(1, chips, lambda k: to_far(k).start())
+    each(1, m, lambda k: to_mp(k).start())
     gm_ref[col] = xm_ref[...]
-
-    def land_dp(k, carry):
-        pltpu.make_async_remote_copy(
-            src_ref=xd_ref,
-            dst_ref=gd_ref.at[(me + n - k) % n],
-            send_sem=send_d.at[k],
-            recv_sem=recv_d.at[(me + n - k) % n],
-            device_id=((me + n - k) % n, col),
-            device_id_type=MESH,
-        ).wait_recv()
-        to_dp(k).wait_send()
-        return carry
-
-    def land_mp(k, carry):
-        pltpu.make_async_remote_copy(
-            src_ref=xm_ref,
-            dst_ref=gm_ref.at[(col + m - k) % m],
-            send_sem=send_m.at[k],
-            recv_sem=recv_m.at[(col + m - k) % m],
-            device_id=(me, (col + m - k) % m),
-            device_id_type=MESH,
-        ).wait_recv()
-        to_mp(k).wait_send()
-        return carry
-
-    lax.fori_loop(1, m, land_mp, 0)
-    lax.fori_loop(1, n, land_dp, 0)
+    each(1, chips, lambda k: from_far(k).wait_recv())
+    mine.wait()
+    swap_out.start()
+    each(1, m, lambda k: from_mp(k).wait_recv())
+    swap_in.wait_recv()
+    each(1, chips, lambda k: to_far(k).wait_send())
+    swap_out.wait_send()
+    each(1, m, lambda k: to_mp(k).wait_send())
 
 
 def direct_gather(xd, xm, n, m):
     moved = n * xd.size * 2 + m * xm.size * 2
-    return pl.pallas_call(
+    gd, gm = pl.pallas_call(
         functools.partial(gather_kernel, n, m),
         out_shape=(
-            jax.ShapeDtypeStruct((n,) + xd.shape, xd.dtype),
+            jax.ShapeDtypeStruct((2, n // 2) + xd.shape, xd.dtype),
             jax.ShapeDtypeStruct((m,) + xm.shape, xm.dtype),
         ),
         in_specs=[pl.BlockSpec(memory_space=pltpu.VMEM)] * 2,
         out_specs=(pl.BlockSpec(memory_space=pltpu.VMEM), pl.BlockSpec(memory_space=pltpu.VMEM)),
         scratch_shapes=[
-            pltpu.SemaphoreType.DMA((n,)),
-            pltpu.SemaphoreType.DMA((n,)),
+            pltpu.SemaphoreType.DMA((n // 2,)),
+            pltpu.SemaphoreType.DMA((n // 2,)),
+            pltpu.SemaphoreType.DMA(()),
+            pltpu.SemaphoreType.DMA(()),
             pltpu.SemaphoreType.DMA((m,)),
             pltpu.SemaphoreType.DMA((m,)),
+            pltpu.SemaphoreType.DMA(()),
         ],
         compiler_params=pltpu.CompilerParams(collective_id=1, has_side_effects=True),
         cost_estimate=pl.CostEstimate(flops=0, bytes_accessed=moved, transcendentals=0),
     )(xd, xm)
+    return jnp.transpose(gd, (1, 0, 2, 3)), gm
 
 
 def ring_kernel(m, x_ref, o_ref, acc_a, acc_b, got_a, got_b, send_a, recv_a, send_b, recv_b):

time: 179 us -> 166 us (0.927)
  the two profiles are of different devices: /device:TPU:58 before, /device:TPU:62 now
where the time goes in v9:
time: 166 us; the launch traced here: 165 us
  Pallas kernels  121 us (73%)
  matrix products  15.9 us (10%)
  between operations  13.7 us (8%)
  other arithmetic  7.4 us (4%)
  local copies, waits for them, and re-layouts  6.16 us (4%)
    pallas_call x1, Pallas kernels, carried_scan(): pl.pallas_call(functools.partial(scan_kernel, n, rounds), out_shape=jax.S...  42.9 us
    pallas_call x1, Pallas kernels, ring_scatter(): pl.pallas_call(functools.partial(ring_kernel, m), out_shape=jax.ShapeDtyp...  40.3 us
    pallas_call x1, Pallas kernels, direct_gather(): pl.pallas_call(functools.partial(gather_kernel, n, m), out_shape=(jax.Sha...  38.2 us
    dot_general x1, matrix products, per_device(): lax.dot_general(normed, out_t, (((1,), (1,)), ((), ())), preferred_elemen...  3.34 us
  transfers between devices with their start and end apart: 1, of which 0 were waited for; matrix products, arithmetic and copies ran while one was open for 14% of the time, Pallas kernels for 49%

profile of v9, /device:TPU:62, one launch (start us, length us, event | category | flops | bytes accessed | tf_op | source)
XLA Modules:
  0.0 165.4 jit_solution(13097446274609593223)
XLA Ops:
  6.5 0.0 copy-start
  6.5 0.0 all-gather.2.cloned.1.call-start
  6.5 0.7 all-gather.2.cloned.1.call-update
  7.3 0.8 reduce-window.8
  8.1 0.1 convert_reduce_fusion
  8.2 0.7 select_reduce_fusion.1
  8.9 1.4 pad_maximum_fusion.xd_ref
  10.4 0.0 copy-done
  10.4 2.2 %fusion.5.xm_ref = bf16[512,32]{1,0:T(8,128)(2,1)} fusion(bf16[512,2048]{1,0:T(8,128)(2,1)S(1)} %copy-done, bf16[2048,32]{0,1:T(8,128)(2,1)} %param.16, s32[32]{0:T(128)S(1)} %fusion.26, s32[512]{0:T(512)S(1)} %select_reduce_fusion.1), kind=kOutput, calls=%fused_computation.11 | convolution fusion | flops 67158016 | bytes 2263168 | tf_op jit(solution)/shard_map/dot_general | solution.py:410
  12.6 38.2 %shard_map.118 = (bf16[2,32,32,320]{3,2,1,0:T(8,128)(2,1)}, bf16[8,512,32]{2,1,0:T(8,128)(2,1)}) custom-call(bf16[32,320]{1,0:T(8,128)(2,1)} %pad_maximum_fusion.xd_ref, bf16[512,32]{1,0:T(8,128)(2,1)} %fusion.5.xm_ref), custom_call_target="tpu_custom_call" | custom-call | bytes 1572864 | tf_op jit(solution)/shard_map/pallas_call | solution.py:270
  50.8 1.7 %copy.20 = bf16[32,2,32,320]{3,2,1,0:T(8,128)(2,1)S(1)} copy(bf16[32,2,32,320]{3,2,0,1:T(8,128)(2,1)} %bitcast.49) | data formatting | bytes 2621440 | tf_op jit(solution)/shard_map/transpose | solution.py:290
  52.5 0.0 copy-start.1
  52.5 0.0 copy-start.7
  52.5 0.0 copy-start.2
  52.5 1.2 copy-done.1
  53.7 1.0 convolution_convert_fusion.2
  54.8 0.6 fusion.33
  55.4 0.0 copy-done.7
  55.4 0.6 iota_multiply_fusion
  56.0 0.3 copy.21
  56.3 1.2 fusion.34
  57.5 0.0 copy-start.6
  57.5 0.0 copy-start.4
  57.5 0.0 copy-start.5
  57.5 2.5 %fusion.4 = bf16[512,256]{0,1:T(8,128)(2,1)S(1)} fusion(f32[512,256]{0,1:T(8,128)S(1)} %fusion.34, bf16[512,2048]{1,0:T(8,128)(2,1)S(1)} %copy-done, bf16[2048,320]{1,0:T(8,128)(2,1)} %bitcast.47), kind=kOutput, calls=%fused_computation.8 | convolution fusion | flops 537133056 | bytes 3932160 | tf_op jit(solution)/shard_map/dot_general | solution.py:425
  60.1 0.1 multiply_convert_fusion.1
  60.2 0.1 compare_reduce_fusion
  60.3 0.0 copy-done.6
  60.3 0.1 and_reduce_fusion
  60.4 1.2 and_convert_fusion
  61.7 0.2 select_reduce_fusion
  61.8 0.5 convolution_convert_fusion.1
  62.3 0.6 compare_convert_fusion.m_ref
  62.9 0.7 convert_element_type.101.s_ref
  63.6 42.9 %shard_map.119 = f32[546,128]{1,0:T(8,128)} custom-call(bf16[546,128]{1,0:T(8,128)(2,1)} %convert_element_type.101.s_ref, f32[12]{0:T(128)} %compare_convert_fusion.m_ref), custom_call_target="tpu_custom_call" | custom-call | flops 1257984 | bytes 2515968 | tf_op jit(solution)/shard_map/pallas_call | solution.py:148
  106.5 1.0 convert_element_type.104
  107.5 1.8 %convolution_convert_fusion.3 = bf16[32,512]{1,0:T(8,128)(2,1)S(1)} fusion(bf16[512,2048]{1,0:T(8,128)(2,1)S(1)} %copy-done, bf16[2048,320]{1,0:T(8,128)(2,1)} %bitcast.48), kind=kOutput, calls=%fused_computation.13 | convolution fusion | flops 67125248 | bytes 2654208 | tf_op jit(solution)/shard_map/dot_general | solution.py:423
  109.3 0.2 fusion.11
  109.5 0.1 multiply_convert_fusion
  109.7 0.0 copy-start.3
  109.7 1.8 %fusion = f32[2,128,512]{2,1,0:T(8,128)} fusion(bf16[512,2,128]{0,2,1:T(8,128)(2,1)S(1)} %bitcast.67, bf16[512,2,16]{0,2,1:T(8,128)(2,1)S(1)} %bitcast.60, bf16[512,2,16]{0,2,1:T(8,128)(2,1)S(1)} %bitcast.57, pred[512,512]{1,0:T(8,128)(4,1)S(1)} %fusion.11), kind=kOutput, calls=%fused_computation.2 | convolution fusion | flops 154664960 | bytes 1114112 | tf_op jit(solution)/shard_map/hij,jhe->ihe/dot_general | solution.py:49
  111.5 1.5 multiply_reduce_fusion
  113.0 0.0 copy-done.3
  113.1 0.1 multiply_convert_fusion.2
  113.2 0.0 all-gather.2.cloned.1.call-done
  113.2 3.3 %convolution_convert_fusion.x_ref = bf16[512,2048]{1,0:T(8,128)(2,1)} fusion(bf16[512,256]{0,1:T(8,128)(2,1)S(1)} %bitcast.52, bf16[2048,256]{1,0:T(8,128)(2,1)} %all-gather.2.cloned.1.call-done), kind=kOutput, calls=%fused_computation | convolution fusion | flops 537919488 | bytes 3407872 | tf_op jit(solution)/shard_map/dot_general | solution.py:440
  116.5 40.3 %shard_map.120 = bf16[512,256]{1,0:T(8,128)(2,1)} custom-call(bf16[512,2048]{1,0:T(8,128)(2,1)} %convolution_convert_fusion.x_ref), custom_call_target="tpu_custom_call" | custom-call | flops 2097152 | bytes 4194304 | tf_op jit(solution)/shard_map/pallas_call | solution.py:364
  156.9 1.7 %copy.26 = bf16[512,256]{1,0:T(8,128)(2,1)} copy(bf16[512,256]{1,0:T(8,128)(2,1)} %shard_map.120) | data formatting | bytes 524288
  (15 shorter events, 0.1 us)
Async XLA Ops:
  6.5 3.8 %copy-start = (bf16[512,2048]{1,0:T(8,128)(2,1)S(1)}, bf16[512,2048]{1,0:T(8,128)(2,1)}, u32[]{:S(2)}) copy-start(bf16[512,2048]{1,0:T(8,128)(2,1)} %param.12) | copy-start | bytes 6291460
  6.5 106.6 %all-gather.2.cloned.1.call-start = ((), (), s32[]{:S(2)}) async-start(), calls=%async_computation | async-start | bytes 1064960 | tf_op jit(solution)/shard_map/all_gather | solution.py:409
  52.5 1.2 copy-start.1
  52.5 2.9 %copy-start.7 = (s32[4]{0:T(128)S(1)}, s32[4]{0:T(128)}, u32[]{:S(2)}) copy-start(s32[4]{0:T(128)} %param.18) | copy-start | bytes 52
  52.5 3.4 %copy-start.2 = (bf16[8,512,32]{2,1,0:T(8,128)(2,1)S(1)}, bf16[8,512,32]{2,1,0:T(8,128)(2,1)}, u32[]{:S(2)}) copy-start(bf16[8,512,32]{2,1,0:T(8,128)(2,1)} %get-tuple-element.8) | copy-start | bytes 786436
  57.5 2.8 %copy-start.6 = (s32[64]{0:T(128)S(1)}, s32[64]{0:T(128)}, u32[]{:S(2)}) copy-start(s32[64]{0:T(128)} %get-tuple-element.18) | copy-start | bytes 772
  57.5 2.9 %copy-start.4 = (s32[12]{0:T(128)S(1)}, s32[12]{0:T(128)}, u32[]{:S(2)}) copy-start(s32[12]{0:T(128)} %constant.73) | copy-start | bytes 148
  57.5 2.9 %copy-start.5 = (s32[12]{0:T(128)S(1)}, s32[12]{0:T(128)}, u32[]{:S(2)}) copy-start(s32[12]{0:T(128)} %constant.74) | copy-start | bytes 148
  109.7 3.4 %copy-start.3 = (f32[256]{0:T(256)S(1)}, f32[256]{0:T(256)}, u32[]{:S(2)}) copy-start(f32[256]{0:T(256)} %param.20) | copy-start | bytes 3076
Sparse Core Ops, SparseCore 0:
  10.7 84.0 all-gather.1

commit v10 on v9

--- a/solution.py
+++ b/solution.py
@@ -79,10 +79,26 @@
     return (hits == 0).astype(jnp.float32)
 
 
-def scan_kernel(n, rounds, s_ref, m_ref, e_ref, parts, recv, send_sem, recv_sem):
+def scan_kernel(n, rounds, s_ref, m_ref, xo_ref, e_ref, go_ref, parts, recv, send_sem, recv_sem,
+                send_o, recv_o, send_x, recv_x, own):
     me = lax.axis_index("dp")
     col = lax.axis_index("mp")
+    chips = n // 2
+    side = me % 2
+    chip = me // 2
+    mate = me + 1 - 2 * side
     barrier = pltpu.get_barrier_semaphore()
+
+    def each(lo, hi, body):
+        def step(k, carry):
+            body(k)
+            return carry
+
+        lax.fori_loop(lo, hi, step, 0)
+
+    each(1, chips, lambda k: pl.semaphore_signal(
+        barrier, 1, device_id=((me + 2 * k) % n, col), device_id_type=MESH))
+    pl.semaphore_signal(barrier, 1, device_id=(mate, col), device_id_type=MESH)
     for k in range(rounds):
         d = 1 << k
 
@@ -98,7 +114,49 @@
     for k in range(rounds):
         d = 1 << k
         peers = peers + (me // d + n - 1) // n + ((n - 1 - me) // d + n - 1) // n
-    pl.semaphore_wait(barrier, peers)
+    pl.semaphore_wait(barrier, peers + chips)
+
+    mine = pltpu.make_async_copy(xo_ref, go_ref.at[side, chip], own)
+    mine.start()
+
+    def to_far(k):
+        return pltpu.make_async_remote_copy(
+            src_ref=xo_ref,
+            dst_ref=go_ref.at[side, chip],
+            send_sem=send_o.at[k],
+            recv_sem=recv_o.at[chip],
+            device_id=((me + 2 * k) % n, col),
+            device_id_type=MESH,
+        )
+
+    def from_far(k):
+        other = (chip + chips - k) % chips
+        return pltpu.make_async_remote_copy(
+            src_ref=xo_ref,
+            dst_ref=go_ref.at[side, other],
+            send_sem=send_o.at[k],
+            recv_sem=recv_o.at[other],
+            device_id=(2 * other + side, col),
+            device_id_type=MESH,
+        )
+
+    swap_out = pltpu.make_async_remote_copy(
+        src_ref=go_ref.at[side],
+        dst_ref=go_ref.at[side],
+        send_sem=send_x,
+        recv_sem=recv_x,
+        device_id=(mate, col),
+        device_id_type=MESH,
+    )
+    swap_in = pltpu.make_async_remote_copy(
+        src_ref=go_ref.at[1 - side],
+        dst_ref=go_ref.at[1 - side],
+        send_sem=send_x,
+        recv_sem=recv_x,
+        device_id=(mate, col),
+        device_id_type=MESH,
+    )
+    each(1, chips, lambda k: to_far(k).start())
 
     e_ref[...] = jnp.zeros_like(e_ref)
     copies = []
@@ -133,6 +191,13 @@
             def _():
                 parts[k] = src[...]
 
+    each(1, chips, lambda k: from_far(k).wait_recv())
+    mine.wait()
+    swap_out.start()
+    swap_in.wait_recv()
+    each(1, chips, lambda k: to_far(k).wait_send())
+    swap_out.wait_send()
+
     for k in range(rounds):
         d = 1 << k
 
@@ -141,30 +206,42 @@
             copies[k].wait_send()
 
 
-def carried_scan(summary, masks, n, rounds):
+def carried_scan(summary, masks, piece, n, rounds):
     shape = summary.shape
     flat = summary.reshape(-1, shape[-1]).astype(jnp.bfloat16)
     size = flat.shape[0] * flat.shape[1]
-    out = pl.pallas_call(
+    out, gathered = pl.pallas_call(
         functools.partial(scan_kernel, n, rounds),
-        out_shape=jax.ShapeDtypeStruct(flat.shape, jnp.float32),
+        out_shape=(
+            jax.ShapeDtypeStruct(flat.shape, jnp.float32),
+            jax.ShapeDtypeStruct((2, n // 2) + piece.shape, piece.dtype),
+        ),
         in_specs=[
             pl.BlockSpec(memory_space=pltpu.VMEM),
             pl.BlockSpec(memory_space=pltpu.SMEM),
+            pl.BlockSpec(memory_space=pltpu.VMEM),
         ],
-        out_specs=pl.BlockSpec(memory_space=pltpu.VMEM),
+        out_specs=(pl.BlockSpec(memory_space=pltpu.VMEM), pl.BlockSpec(memory_space=pltpu.VMEM)),
         scratch_shapes=[
             pltpu.VMEM((max(rounds - 1, 1),) + flat.shape, jnp.bfloat16),
             pltpu.VMEM((rounds,) + flat.shape, jnp.bfloat16),
             pltpu.SemaphoreType.DMA((rounds,)),
             pltpu.SemaphoreType.DMA((rounds,)),
+            pltpu.SemaphoreType.DMA((n // 2,)),
+            pltpu.SemaphoreType.DMA((n // 2,)),
+            pltpu.SemaphoreType.DMA(()),
+            pltpu.SemaphoreType.DMA(()),
+            pltpu.SemaphoreType.DMA(()),
         ],
         compiler_params=pltpu.CompilerParams(collective_id=0, has_side_effects=True),
         cost_estimate=pl.CostEstimate(
-            flops=3 * rounds * size, bytes_accessed=6 * rounds * size, transcendentals=0
+            flops=3 * rounds * size,
+            bytes_accessed=6 * rounds * size + 2 * n * piece.size,
+            transcendentals=0,
         ),
-    )(flat, masks)
-    return out.reshape(shape)
+    )(flat, masks, piece)
+    gathered = jnp.transpose(gathered, (1, 0, 2, 3)).reshape(n * piece.shape[0], piece.shape[1])
+    return out.reshape(shape), gathered
 
 
 def gather_kernel(n, m, xd_ref, xm_ref, gd_ref, gm_ref, send_d, recv_d, send_x, recv_x, send_m, recv_m, own):
@@ -406,7 +483,6 @@
     request, starts, adapter = token_tables(lengths, adapter_ids, positions)
 
     local = jnp.concatenate([q_weight, k_weight, v_weight], axis=1)
-    out_t = lax.all_gather(out_weight.T, "dp", axis=0, tiled=True)
     part_low = jnp.dot(tokens, adapter_down, preferred_element_type=jnp.float32)
     owners = lax.axis_index("mp") * (adapter_down.shape[1] // R) + (
         jnp.arange(adapter_down.shape[1], dtype=jnp.int32) // R
@@ -431,7 +507,7 @@
 
     rounds = max(1, (blocks - 1).bit_length())
     masks = scan_masks(lengths, row_count, place, blocks, rounds)
-    carried = carried_scan(summary, masks, blocks, rounds)
+    carried, out_t = carried_scan(summary, masks, out_weight.T, blocks, rounds)
 
     gains = head_gain.reshape(heads_here, value_width)
     normed = finish(within, query_map, carried, request, starts, gains).reshape(

time: 166 us -> 161 us (0.970)
  the two profiles are of different devices: /device:TPU:62 before, /device:TPU:44 now
where the time goes in v10:
time: 161 us
  Pallas kernels  135 us (84%)
  matrix products  11.4 us (7%)
  other arithmetic  7.23 us (4%)
  local copies, waits for them, and re-layouts  6.42 us (4%)
    pallas_call x1, Pallas kernels, carried_scan(): pl.pallas_call(functools.partial(scan_kernel, n, rounds), out_shape=(jax....  55.8 us
    pallas_call x1, Pallas kernels, ring_scatter(): pl.pallas_call(functools.partial(ring_kernel, m), out_shape=jax.ShapeDtyp...  41.5 us
    pallas_call x1, Pallas kernels, direct_gather(): pl.pallas_call(functools.partial(gather_kernel, n, m), out_shape=(jax.Sha...  38.2 us

profile of v10, /device:TPU:44, one launch (start us, length us, event | category | flops | bytes accessed | tf_op | source)
XLA Modules:
  0.0 160.8 jit_solution(18045449803275752776)
XLA Ops:
  0.0 0.0 copy-start
  0.0 1.6 pad_maximum_fusion.xd_ref
  1.6 0.8 reduce-window.8
  2.4 0.1 convert_reduce_fusion
  2.5 0.0 copy-start.2
  2.5 0.8 select_reduce_fusion.1
  3.3 0.0 copy-done
  3.3 2.2 %fusion.5.xm_ref = bf16[512,32]{1,0:T(8,128)(2,1)} fusion(bf16[512,2048]{1,0:T(8,128)(2,1)S(1)} %copy-done, bf16[2048,32]{0,1:T(8,128)(2,1)} %param.16, s32[32]{0:T(128)S(1)} %fusion.26, s32[512]{0:T(512)S(1)} %select_reduce_fusion.1), kind=kOutput, calls=%fused_computation.11 | convolution fusion | flops 67158016 | bytes 2263168 | tf_op jit(solution)/shard_map/dot_general | solution.py:486
  5.5 38.2 %shard_map.118 = (bf16[2,32,32,320]{3,2,1,0:T(8,128)(2,1)}, bf16[8,512,32]{2,1,0:T(8,128)(2,1)}) custom-call(bf16[32,320]{1,0:T(8,128)(2,1)} %pad_maximum_fusion.xd_ref, bf16[512,32]{1,0:T(8,128)(2,1)} %fusion.5.xm_ref), custom_call_target="tpu_custom_call" | custom-call | bytes 1572864 | tf_op jit(solution)/shard_map/pallas_call | solution.py:347
  43.7 1.5 copy.22
  45.3 0.0 copy-done.2
  45.3 0.3 fusion.34
  45.6 1.7 %copy.21 = bf16[32,2,32,320]{3,2,1,0:T(8,128)(2,1)S(1)} copy(bf16[32,2,32,320]{3,2,0,1:T(8,128)(2,1)} %bitcast.52) | data formatting | bytes 2621440 | tf_op jit(solution)/shard_map/transpose | solution.py:367
  47.3 1.1 fusion.4
  48.4 0.7 convolution_convert_fusion.3
  49.2 1.1 convolution_convert_fusion.2
  50.2 0.2 fusion.11
  50.5 0.0 copy-start.6
  50.5 1.8 %fusion = f32[2,128,512]{2,1,0:T(8,128)} fusion(bf16[512,2,128]{0,2,1:T(8,128)(2,1)S(1)} %bitcast.70, bf16[512,2,16]{0,2,1:T(8,128)(2,1)S(1)} %bitcast.59, bf16[512,2,16]{0,2,1:T(8,128)(2,1)S(1)} %bitcast.62, pred[512,512]{1,0:T(8,128)(4,1)S(1)} %fusion.11), kind=kOutput, calls=%fused_computation.2 | convolution fusion | flops 154664960 | bytes 1114112 | tf_op jit(solution)/shard_map/hij,jhe->ihe/dot_general | solution.py:49
  52.3 0.0 copy-start.4
  52.3 0.0 copy-start.5
  52.3 0.1 multiply_convert_fusion.1
  52.5 0.7 fusion.33
  53.1 0.0 copy-done.6
  53.1 0.1 compare_reduce_fusion
  53.3 1.3 and_convert_fusion
  54.6 0.5 convolution_convert_fusion.1
  55.1 0.0 copy-start.3
  55.1 0.7 convert_element_type.101.s_ref
  55.8 0.1 and_reduce_fusion
  55.9 0.0 copy-done.4
  55.9 0.0 copy-done.5
  55.9 0.2 select_reduce_fusion
  56.1 0.6 compare_convert_fusion.m_ref
  56.7 55.8 %shard_map.119 = (f32[546,128]{1,0:T(8,128)}, bf16[2,32,32,256]{3,2,1,0:T(8,128)(2,1)}) custom-call(bf16[546,128]{1,0:T(8,128)(2,1)} %convert_element_type.101.s_ref, f32[12]{0:T(128)} %compare_convert_fusion.m_ref, bf16[32,256]{1,0:T(8,128)(2,1)} %bitcast.65), custom_call_target="tpu_custom_call" | custom-call | flops 1257984 | bytes 3564544 | tf_op jit(solution)/shard_map/pallas_call | solution.py:213
  112.5 0.0 copy-start.1
  112.5 1.1 convert_element_type.104
  113.6 0.1 multiply_convert_fusion
  113.7 1.5 multiply_reduce_fusion
  115.3 0.0 copy-done.3
  115.3 0.1 multiply_convert_fusion.2
  115.4 0.0 copy-done.1
  115.4 0.1 copy.24
  115.5 2.1 %convolution_convert_fusion.x_ref = bf16[512,2048]{1,0:T(8,128)(2,1)} fusion(bf16[512,256]{0,1:T(8,128)(2,1)S(1)} %bitcast.56, bf16[2048,256]{1,0:T(8,128)(2,1)S(1)} %bitcast.51), kind=kOutput, calls=%fused_computation | convolution fusion | flops 537919488 | bytes 3407872 | tf_op jit(solution)/shard_map/dot_general | solution.py:516
  117.6 41.5 %shard_map.120 = bf16[512,256]{1,0:T(8,128)(2,1)} custom-call(bf16[512,2048]{1,0:T(8,128)(2,1)} %convolution_convert_fusion.x_ref), custom_call_target="tpu_custom_call" | custom-call | flops 2097152 | bytes 4194304 | tf_op jit(solution)/shard_map/pallas_call | solution.py:441
  159.1 1.7 %copy.28 = bf16[512,256]{1,0:T(8,128)(2,1)} copy(bf16[512,256]{1,0:T(8,128)(2,1)} %shard_map.120) | data formatting | bytes 524288
  (13 shorter events, 0.1 us)
Async XLA Ops:
  0.0 3.3 %copy-start = (bf16[512,2048]{1,0:T(8,128)(2,1)S(1)}, bf16[512,2048]{1,0:T(8,128)(2,1)}, u32[]{:S(2)}) copy-start(bf16[512,2048]{1,0:T(8,128)(2,1)} %param.12) | copy-start | bytes 6291460
  2.5 42.8 %copy-start.2 = (bf16[256,256]{1,0:T(8,128)(2,1)S(1)}, bf16[256,256]{1,0:T(8,128)(2,1)}, u32[]{:S(2)}) copy-start(bf16[256,256]{1,0:T(8,128)(2,1)} %param.17) | copy-start | bytes 393220
  50.5 2.7 %copy-start.6 = (s32[4]{0:T(128)S(1)}, s32[4]{0:T(128)}, u32[]{:S(2)}) copy-start(s32[4]{0:T(128)} %param.18) | copy-start | bytes 52
  52.3 3.6 %copy-start.4 = (s32[12]{0:T(128)S(1)}, s32[12]{0:T(128)}, u32[]{:S(2)}) copy-start(s32[12]{0:T(128)} %constant.73) | copy-start | bytes 148
  52.3 3.6 %copy-start.5 = (s32[12]{0:T(128)S(1)}, s32[12]{0:T(128)}, u32[]{:S(2)}) copy-start(s32[12]{0:T(128)} %constant.74) | copy-start | bytes 148
  55.1 60.2 %copy-start.3 = (f32[256]{0:T(256)S(1)}, f32[256]{0:T(256)}, u32[]{:S(2)}) copy-start(f32[256]{0:T(256)} %param.20) | copy-start | bytes 3076
  112.5 3.0 %copy-start.1 = (bf16[2,32,32,256]{3,2,1,0:T(8,128)(2,1)S(1)}, bf16[2,32,32,256]{3,2,1,0:T(8,128)(2,1)}, u32[]{:S(2)}) copy-start(bf16[2,32,32,256]{3,2,1,0:T(8,128)(2,1)} %get-tuple-element.12) | copy-start | bytes 3145732

commit v11 on v10

--- a/solution.py
+++ b/solution.py
@@ -4,6 +4,7 @@
 
 import jax
 import jax.numpy as jnp
+import numpy as np
 from jax import lax
 from jax.experimental import pallas as pl
 from jax.experimental.pallas import tpu as pltpu
@@ -24,6 +25,15 @@
     )
     constant = jnp.ones(inputs.shape[:-1] + (1,), jnp.float32)
     return jnp.concatenate([constant, 0.5 * inputs, squares * (0.25 / math.sqrt(2.0))], axis=-1)
+
+
+def packed_features(width):
+    index, weight = list(range(1 + width)), [1.0] * (1 + width)
+    for a in range(width):
+        for b in range(a, width):
+            index.append(1 + width + a * width + b)
+            weight.append(1.0 if a == b else 2.0)
+    return np.asarray(index, np.int32), np.asarray(weight, np.float32)
 
 
 def request_of(bounds, positions):
@@ -47,8 +57,10 @@
     allowed = (indexes[None, :] <= indexes[:, None]) & (request[None, :] == request[:, None])
     weights = jnp.where(allowed[None], weights, 0.0).astype(jnp.bfloat16)
     within = jnp.einsum("hij,jhe->ihe", weights, values, preferred_element_type=jnp.float32)
+    index, weight = packed_features(query.shape[-1])
     query_map = taylor(query.astype(jnp.float32)).astype(jnp.bfloat16)
-    key_map = taylor(key_rows.astype(jnp.float32)).astype(jnp.bfloat16)
+    query_map = query_map[..., index] * jnp.asarray(weight, jnp.bfloat16)
+    key_map = taylor(key_rows.astype(jnp.float32)).astype(jnp.bfloat16)[..., index]
     tail_mask = (request == request[-1]).astype(jnp.bfloat16)
     masked_keys = key_map * tail_mask[:, None, None]
     summary = jnp.einsum("ihf,ihe->hfe", masked_keys, values, preferred_element_type=jnp.float32)

time: 161 us -> 159 us (0.988)
  the two profiles are of different devices: /device:TPU:44 before, /device:TPU:62 now
where the time goes in v11:
time: 159 us
  Pallas kernels  124 us (78%)
  matrix products  11.8 us (7%)
  other arithmetic  11.3 us (7%)
  local copies, waits for them, and re-layouts  10.6 us (7%)
    pallas_call x1, Pallas kernels, carried_scan(): pl.pallas_call(functools.partial(scan_kernel, n, rounds), out_shape=(jax....  44.6 us
    pallas_call x1, Pallas kernels, ring_scatter(): pl.pallas_call(functools.partial(ring_kernel, m), out_shape=jax.ShapeDtyp...  41.6 us
    pallas_call x1, Pallas kernels, direct_gather(): pl.pallas_call(functools.partial(gather_kernel, n, m), out_shape=(jax.Sha...  38.2 us

profile of v11, /device:TPU:62, one launch (start us, length us, event | category | flops | bytes accessed | tf_op | source)
XLA Modules:
  0.0 158.5 jit_solution(7321869278366400212)
XLA Ops:
  0.0 1.6 pad_maximum_fusion.2.xd_ref
  1.6 0.8 reduce-window.8
  2.4 0.1 convert_reduce_fusion
  2.5 0.8 select_reduce_fusion.1
  3.3 2.2 %fusion.5.xm_ref = bf16[512,32]{1,0:T(8,128)(2,1)} fusion(bf16[512,2048]{1,0:T(8,128)(2,1)S(1)} %copy-done, bf16[2048,32]{0,1:T(8,128)(2,1)} %param.20, s32[32]{0:T(128)S(1)} %fusion.18, s32[512]{0:T(512)S(1)} %select_reduce_fusion.1), kind=kOutput, calls=%fused_computation.12 | convolution fusion | flops 67158016 | bytes 2263168 | tf_op jit(solution)/shard_map/dot_general | solution.py:498
  5.5 38.2 %shard_map.154 = (bf16[2,32,32,320]{3,2,1,0:T(8,128)(2,1)}, bf16[8,512,32]{2,1,0:T(8,128)(2,1)}) custom-call(bf16[32,320]{1,0:T(8,128)(2,1)} %pad_maximum_fusion.2.xd_ref, bf16[512,32]{1,0:T(8,128)(2,1)} %fusion.5.xm_ref), custom_call_target="tpu_custom_call" | custom-call | bytes 1572864 | tf_op jit(solution)/shard_map/pallas_call | solution.py:359
  43.8 0.0 copy-done.8
  43.8 1.5 copy.57
  45.3 0.3 fusion.24
  45.6 1.7 %copy.56 = bf16[32,2,32,320]{3,2,1,0:T(8,128)(2,1)S(1)} copy(bf16[32,2,32,320]{3,2,0,1:T(8,128)(2,1)} %bitcast.58) | data formatting | bytes 2621440 | tf_op jit(solution)/shard_map/transpose | solution.py:379
  47.3 1.1 fusion.4
  48.5 0.0 copy-start.9
  48.5 0.7 convolution_convert_fusion.3
  49.2 1.1 convolution_convert_fusion.2
  50.3 0.2 fusion.11
  50.5 0.0 copy-done.9
  50.5 1.8 %fusion = f32[2,128,512]{2,1,0:T(8,128)} fusion(bf16[512,2,128]{0,2,1:T(8,128)(2,1)S(1)} %bitcast.74, bf16[512,2,16]{0,2,1:T(8,128)(2,1)S(1)} %bitcast.66, bf16[512,2,16]{0,2,1:T(8,128)(2,1)S(1)} %bitcast.63, pred[512,512]{1,0:T(8,128)(4,1)S(1)} %fusion.11), kind=kOutput, calls=%fused_computation.4 | convolution fusion | flops 154664960 | bytes 1114112 | tf_op jit(solution)/shard_map/hij,jhe->ihe/dot_general | solution.py:59
  52.4 0.1 multiply_convert_fusion
  52.5 0.5 copy.63
  53.1 0.0 copy-start.5
  53.1 0.1 multiply_convert_fusion.1
  53.2 0.5 copy.59
  53.8 0.0 copy-start.6
  53.9 0.0 copy-start.7
  53.9 2.3 %pad_maximum_fusion.1 = (bf16[512,2,273]{0,1,2:T(2,128)(2,1)S(1)}, bf16[512,2,273]{0,1,2:T(2,128)(2,1)S(1)}) fusion(bf16[512,2,256]{0,1,2:T(2,128)(2,1)S(1)} %copy.63, bf16[512,2,16]{0,1,2:T(2,128)(2,1)S(1)} %copy.62, bf16[273]{0:T(512)(128)(2,1)S(1)} %pad.3.clone, bf16[512,2,256]{0,1,2:T(2,128)(2,1)S(1)} %copy.59, bf16[512,2,16]{0,1,2:T(2,128)(2,1)S(1)} %copy.58), kind=kLoop, calls=%fused_computation.27 | loop fusion | flops 1118208 | bytes 2232866 | tf_op jit(solution)/shard_map/concatenate | solution.py:27
  56.2 1.3 gather_fusion
  57.4 0.6 fusion.23
  58.0 0.7 bitcast_subtract_fusion
  58.7 0.1 compare_reduce_fusion
  58.8 1.3 and_convert_fusion
  60.1 0.3 multiply_bitcast_fusion.1
  60.4 1.2 convolution_convert_fusion.1
  61.6 0.0 copy-start.4
  61.6 0.7 convert_element_type.101.s_ref
  62.3 0.1 and_reduce_fusion
  62.4 0.2 select_reduce_fusion
  62.6 0.6 compare_convert_fusion.m_ref
  63.1 44.6 %shard_map.155 = (f32[306,128]{1,0:T(8,128)}, bf16[2,32,32,256]{3,2,1,0:T(8,128)(2,1)}) custom-call(bf16[306,128]{1,0:T(8,128)(2,1)} %convert_element_type.101.s_ref, f32[12]{0:T(128)} %compare_convert_fusion.m_ref, bf16[32,256]{1,0:T(8,128)(2,1)} %bitcast.69), custom_call_target="tpu_custom_call" | custom-call | flops 705024 | bytes 2458624 | tf_op jit(solution)/shard_map/pallas_call | solution.py:225
  107.7 0.9 convert_element_type.104
  108.7 0.7 convert_element_type.105
  109.3 1.3 gather_fusion.1
  110.6 1.1 multiply_bitcast_fusion
  111.7 1.2 multiply_reduce_fusion
  112.9 0.1 multiply_convert_fusion.2
  113.0 0.1 copy.65
  113.1 2.1 %convolution_convert_fusion.x_ref = bf16[512,2048]{1,0:T(8,128)(2,1)} fusion(bf16[512,256]{0,1:T(8,128)(2,1)S(1)} %bitcast.62, bf16[2048,256]{1,0:T(8,128)(2,1)S(1)} %bitcast.55), kind=kOutput, calls=%fused_computation.2 | convolution fusion | flops 537919488 | bytes 3407872 | tf_op jit(solution)/shard_map/dot_general | solution.py:528
  115.2 41.6 %shard_map.156 = bf16[512,256]{1,0:T(8,128)(2,1)} custom-call(bf16[512,2048]{1,0:T(8,128)(2,1)} %convolution_convert_fusion.x_ref), custom_call_target="tpu_custom_call" | custom-call | flops 2097152 | bytes 4194304 | tf_op jit(solution)/shard_map/pallas_call | solution.py:453
  156.8 1.7 %copy.75 = bf16[512,256]{1,0:T(8,128)(2,1)} copy(bf16[512,256]{1,0:T(8,128)(2,1)} %shard_map.156) | data formatting | bytes 524288
  (27 shorter events, 0.2 us)
Async XLA Ops:
  0.0 3.3 %copy-start = (bf16[512,2048]{1,0:T(8,128)(2,1)S(1)}, bf16[512,2048]{1,0:T(8,128)(2,1)}, u32[]{:S(2)}) copy-start(bf16[512,2048]{1,0:T(8,128)(2,1)} %param.16) | copy-start | bytes 6291460
  2.4 41.4 %copy-start.8 = (s32[4,1]{0,1:T(1,128)}, s32[4,1]{0,1:T(1,128)S(1)}, u32[]{:S(2)}) copy-start(s32[4,1]{0,1:T(1,128)S(1)} %reduce-window.8) | copy-start | bytes 52
  2.5 42.8 %copy-start.3 = (bf16[256,256]{1,0:T(8,128)(2,1)S(1)}, bf16[256,256]{1,0:T(8,128)(2,1)}, u32[]{:S(2)}) copy-start(bf16[256,256]{1,0:T(8,128)(2,1)} %param.21) | copy-start | bytes 393220
  48.5 2.1 %copy-start.9 = (bf16[512,256]{0,1:T(8,128)(2,1)}, bf16[512,256]{0,1:T(8,128)(2,1)S(1)}, u32[]{:S(2)}) copy-start(bf16[512,256]{0,1:T(8,128)(2,1)S(1)} %fusion.4) | copy-start | bytes 786436
  53.1 3.1 %copy-start.5 = (s32[153]{0:T(256)S(1)}, s32[153]{0:T(256)}, u32[]{:S(2)}) copy-start(s32[153]{0:T(256)} %constant.87) | copy-start | bytes 1840
  53.8 8.5 %copy-start.6 = (s32[12]{0:T(128)S(1)}, s32[12]{0:T(128)}, u32[]{:S(2)}) copy-start(s32[12]{0:T(128)} %constant.85) | copy-start | bytes 148
  53.9 8.5 %copy-start.7 = (s32[12]{0:T(128)S(1)}, s32[12]{0:T(128)}, u32[]{:S(2)}) copy-start(s32[12]{0:T(128)} %constant.86) | copy-start | bytes 148
  57.4 54.3 %copy-start.2 = (f32[2,128,512]{2,1,0:T(8,128)S(1)}, f32[2,128,512]{2,1,0:T(8,128)}, u32[]{:S(2)}) copy-start(f32[2,128,512]{2,1,0:T(8,128)} %fusion) | copy-start | bytes 1572868
  61.6 51.3 %copy-start.4 = (f32[256]{0:T(256)S(1)}, f32[256]{0:T(256)}, u32[]{:S(2)}) copy-start(f32[256]{0:T(256)} %param.24) | copy-start | bytes 3076
  110.6 2.5 %copy-start.1 = (bf16[2,32,32,256]{3,2,1,0:T(8,128)(2,1)S(1)}, bf16[2,32,32,256]{3,2,1,0:T(8,128)(2,1)}, u32[]{:S(2)}) copy-start(bf16[2,32,32,256]{3,2,1,0:T(8,128)(2,1)} %get-tuple-element.12) | copy-start | bytes 3145732

commit v12 on v11

--- a/solution.py
+++ b/solution.py
@@ -256,7 +256,7 @@
     return out.reshape(shape), gathered
 
 
-def gather_kernel(n, m, xd_ref, xm_ref, gd_ref, gm_ref, send_d, recv_d, send_x, recv_x, send_m, recv_m, own):
+def gather_kernel(n, m, xd_ref, xm_ref, early_ref, gd_ref, gm_ref, send_d, recv_d, send_x, recv_x, send_m, recv_m, own):
     me = lax.axis_index("dp")
     col = lax.axis_index("mp")
     chips = n // 2
@@ -354,7 +354,7 @@
     each(1, m, lambda k: to_mp(k).wait_send())
 
 
-def direct_gather(xd, xm, n, m):
+def direct_gather(xd, xm, early, n, m):
     moved = n * xd.size * 2 + m * xm.size * 2
     gd, gm = pl.pallas_call(
         functools.partial(gather_kernel, n, m),
@@ -362,7 +362,7 @@
             jax.ShapeDtypeStruct((2, n // 2) + xd.shape, xd.dtype),
             jax.ShapeDtypeStruct((m,) + xm.shape, xm.dtype),
         ),
-        in_specs=[pl.BlockSpec(memory_space=pltpu.VMEM)] * 2,
+        in_specs=[pl.BlockSpec(memory_space=pltpu.VMEM)] * 2 + [pl.BlockSpec(memory_space=pltpu.SMEM)],
         out_specs=(pl.BlockSpec(memory_space=pltpu.VMEM), pl.BlockSpec(memory_space=pltpu.VMEM)),
         scratch_shapes=[
             pltpu.SemaphoreType.DMA((n // 2,)),
@@ -375,7 +375,7 @@
         ],
         compiler_params=pltpu.CompilerParams(collective_id=1, has_side_effects=True),
         cost_estimate=pl.CostEstimate(flops=0, bytes_accessed=moved, transcendentals=0),
-    )(xd, xm)
+    )(xd, xm, early)
     return jnp.transpose(gd, (1, 0, 2, 3)), gm
 
 
@@ -501,7 +501,9 @@
     )
     part_low = jnp.where(adapter[:, None] == owners[None, :], part_low, 0.0).astype(jnp.bfloat16)
     cols = lax.axis_size("mp")
-    gathered, low_parts = direct_gather(local, part_low, blocks, cols)
+    rounds = max(1, (blocks - 1).bit_length())
+    masks = scan_masks(lengths, row_count, place, blocks, rounds)
+    gathered, low_parts = direct_gather(local, part_low, masks, blocks, cols)
     gathered = gathered.reshape(blocks * local.shape[0], local.shape[1])
     q_full = gathered[:, :qf]
     k_full = gathered[:, qf : 2 * qf]
@@ -517,8 +519,6 @@
     values = values.astype(jnp.bfloat16).reshape(row_count, heads_here, value_width)
     within, query_map, summary = block_local(query, key_rows, values, request, starts)
 
-    rounds = max(1, (blocks - 1).bit_length())
-    masks = scan_masks(lengths, row_count, place, blocks, rounds)
     carried, out_t = carried_scan(summary, masks, out_weight.T, blocks, rounds)
 
     gains = head_gain.reshape(heads_here, value_width)

time: 159 us -> 157 us (0.987)
  no operation moved by 1% of the time
where the time goes in v12:
time: 157 us
  Pallas kernels  124 us (79%)
  matrix products  11.8 us (8%)
  local copies, waits for them, and re-layouts  10.6 us (7%)
  other arithmetic  9.8 us (6%)
    pallas_call x1, Pallas kernels, carried_scan(): pl.pallas_call(functools.partial(scan_kernel, n, rounds), out_shape=(jax....  44.8 us
    pallas_call x1, Pallas kernels, ring_scatter(): pl.pallas_call(functools.partial(ring_kernel, m), out_shape=jax.ShapeDtyp...  40.5 us
    pallas_call x1, Pallas kernels, direct_gather(): pl.pallas_call(functools.partial(gather_kernel, n, m), out_shape=(jax.Sha...  38.6 us

profile of v12, /device:TPU:62, one launch (start us, length us, event | category | flops | bytes accessed | tf_op | source)
XLA Modules:
  0.0 156.5 jit_solution(7225538050296742746)
XLA Ops:
  0.0 0.0 copy-start.9
  0.0 1.6 %pad_maximum_fusion.2.xd_ref = bf16[32,320]{1,0:T(8,128)(2,1)} fusion(bf16[32,256]{1,0:T(8,128)(2,1)} %param.19, bf16[32,32]{1,0:T(8,128)(2,1)} %param.18, bf16[32,32]{1,0:T(8,128)(2,1)} %param.17), kind=kLoop, calls=%fused_computation.38 | loop fusion | flops 61440 | bytes 40960 | tf_op jit(solution)/shard_map/concatenate | solution.py:497
  1.6 0.8 reduce-window.8
  2.4 0.1 convert_reduce_fusion
  2.5 0.7 select_reduce_fusion.1
  3.3 2.3 %fusion.5.xm_ref = bf16[512,32]{1,0:T(8,128)(2,1)} fusion(bf16[512,2048]{1,0:T(8,128)(2,1)S(1)} %copy-done, bf16[2048,32]{0,1:T(8,128)(2,1)} %param.20, s32[32]{0:T(128)S(1)} %fusion.18, s32[512]{0:T(512)S(1)} %select_reduce_fusion.1), kind=kOutput, calls=%fused_computation.12 | convolution fusion | flops 67158016 | bytes 2263168 | tf_op jit(solution)/shard_map/dot_general | solution.py:498
  5.6 0.1 and_reduce_fusion
  5.7 0.2 select_reduce_fusion
  5.9 0.5 compare_convert_fusion.1.early_ref.m_ref
  6.4 38.6 %shard_map.154 = (bf16[2,32,32,320]{3,2,1,0:T(8,128)(2,1)}, bf16[8,512,32]{2,1,0:T(8,128)(2,1)}) custom-call(bf16[32,320]{1,0:T(8,128)(2,1)} %pad_maximum_fusion.2.xd_ref, bf16[512,32]{1,0:T(8,128)(2,1)} %fusion.5.xm_ref, f32[12]{0:T(128)} %compare_convert_fusion.1.early_ref.m_ref), custom_call_target="tpu_custom_call" | custom-call | bytes 1572864 | tf_op jit(solution)/shard_map/pallas_call | solution.py:359
  45.0 1.5 copy.57
  46.5 0.0 copy-done.3
  46.5 0.3 fusion.24
  46.8 1.7 %copy.56 = bf16[32,2,32,320]{3,2,1,0:T(8,128)(2,1)S(1)} copy(bf16[32,2,32,320]{3,2,0,1:T(8,128)(2,1)} %bitcast.58) | data formatting | bytes 2621440 | tf_op jit(solution)/shard_map/transpose | solution.py:379
  48.5 1.1 fusion.4
  49.6 0.0 copy-start.10
  49.6 0.7 convolution_convert_fusion.3
  50.4 1.1 convolution_convert_fusion.2
  51.5 0.2 fusion.11
  51.7 1.8 %fusion = f32[2,128,512]{2,1,0:T(8,128)} fusion(bf16[512,2,128]{0,2,1:T(8,128)(2,1)S(1)} %bitcast.74, bf16[512,2,16]{0,2,1:T(8,128)(2,1)S(1)} %bitcast.66, bf16[512,2,16]{0,2,1:T(8,128)(2,1)S(1)} %bitcast.63, pred[512,512]{1,0:T(8,128)(4,1)S(1)} %fusion.11), kind=kOutput, calls=%fused_computation.4 | convolution fusion | flops 154664960 | bytes 1114112 | tf_op jit(solution)/shard_map/hij,jhe->ihe/dot_general | solution.py:59
  53.5 0.1 multiply_convert_fusion
  53.6 0.5 copy.63
  54.2 0.0 copy-start.5
  54.3 0.1 multiply_convert_fusion.1
  54.4 0.5 copy.59
  55.0 2.3 %pad_maximum_fusion.1 = (bf16[512,2,273]{0,1,2:T(2,128)(2,1)S(1)}, bf16[512,2,273]{0,1,2:T(2,128)(2,1)S(1)}) fusion(bf16[512,2,256]{0,1,2:T(2,128)(2,1)S(1)} %copy.63, bf16[512,2,16]{0,1,2:T(2,128)(2,1)S(1)} %copy.62, bf16[273]{0:T(512)(128)(2,1)S(1)} %pad.3.clone, bf16[512,2,256]{0,1,2:T(2,128)(2,1)S(1)} %copy.59, bf16[512,2,16]{0,1,2:T(2,128)(2,1)S(1)} %copy.58), kind=kLoop, calls=%fused_computation.27 | loop fusion | flops 1118208 | bytes 2232866 | tf_op jit(solution)/shard_map/concatenate | solution.py:27
  57.3 0.0 copy-start.8
  57.3 0.0 copy-done.5
  57.3 1.3 gather_fusion
  58.6 0.6 fusion.23
  59.2 0.1 compare_reduce_fusion
  59.3 1.3 and_convert_fusion
  60.6 0.3 multiply_bitcast_fusion.1
  60.9 0.0 copy-start.4
  60.9 1.2 convolution_convert_fusion.1
  62.1 0.7 convert_element_type.103.s_ref
  62.7 44.8 %shard_map.155 = (f32[306,128]{1,0:T(8,128)}, bf16[2,32,32,256]{3,2,1,0:T(8,128)(2,1)}) custom-call(bf16[306,128]{1,0:T(8,128)(2,1)} %convert_element_type.103.s_ref, f32[12]{0:T(128)} %compare_convert_fusion.1.early_ref.m_ref, bf16[32,256]{1,0:T(8,128)(2,1)} %bitcast.69), custom_call_target="tpu_custom_call" | custom-call | flops 705024 | bytes 2458624 | tf_op jit(solution)/shard_map/pallas_call | solution.py:225
  107.5 0.9 convert_element_type.104
  108.5 0.7 convert_element_type.105
  109.1 1.3 gather_fusion.1
  110.4 0.0 copy-done.8
  110.4 0.4 multiply_bitcast_fusion
  110.8 1.2 multiply_reduce_fusion
  112.0 0.1 multiply_convert_fusion.2
  112.1 0.1 copy.65
  112.2 2.1 %convolution_convert_fusion.x_ref = bf16[512,2048]{1,0:T(8,128)(2,1)} fusion(bf16[512,256]{0,1:T(8,128)(2,1)S(1)} %bitcast.62, bf16[2048,256]{1,0:T(8,128)(2,1)S(1)} %bitcast.55), kind=kOutput, calls=%fused_computation.2 | convolution fusion | flops 537919488 | bytes 3407872 | tf_op jit(solution)/shard_map/dot_general | solution.py:528
  114.3 40.5 %shard_map.156 = bf16[512,256]{1,0:T(8,128)(2,1)} custom-call(bf16[512,2048]{1,0:T(8,128)(2,1)} %convolution_convert_fusion.x_ref), custom_call_target="tpu_custom_call" | custom-call | flops 2097152 | bytes 4194304 | tf_op jit(solution)/shard_map/pallas_call | solution.py:453
  154.8 1.7 %copy.75 = bf16[512,256]{1,0:T(8,128)(2,1)} copy(bf16[512,256]{1,0:T(8,128)(2,1)} %shard_map.156) | data formatting | bytes 524288
  (29 shorter events, 0.2 us)
Async XLA Ops:
  0.0 3.3 %copy-start = (bf16[512,2048]{1,0:T(8,128)(2,1)S(1)}, bf16[512,2048]{1,0:T(8,128)(2,1)}, u32[]{:S(2)}) copy-start(bf16[512,2048]{1,0:T(8,128)(2,1)} %param.16) | copy-start | bytes 6291460
  0.0 5.7 %copy-start.6 = (s32[12]{0:T(128)S(1)}, s32[12]{0:T(128)}, u32[]{:S(2)}) copy-start(s32[12]{0:T(128)} %constant.84) | copy-start | bytes 148
  0.0 5.7 %copy-start.7 = (s32[12]{0:T(128)S(1)}, s32[12]{0:T(128)}, u32[]{:S(2)}) copy-start(s32[12]{0:T(128)} %constant.85) | copy-start | bytes 148
  0.0 5.6 %copy-start.9 = (s32[4]{0:T(128)S(1)}, s32[4]{0:T(128)}, u32[]{:S(2)}) copy-start(s32[4]{0:T(128)} %param.22) | copy-start | bytes 52
  3.3 43.2 %copy-start.3 = (bf16[256,256]{1,0:T(8,128)(2,1)S(1)}, bf16[256,256]{1,0:T(8,128)(2,1)}, u32[]{:S(2)}) copy-start(bf16[256,256]{1,0:T(8,128)(2,1)} %param.21) | copy-start | bytes 393220
  49.6 4.5 %copy-start.10 = (bf16[512,256]{0,1:T(8,128)(2,1)}, bf16[512,256]{0,1:T(8,128)(2,1)S(1)}, u32[]{:S(2)}) copy-start(bf16[512,256]{0,1:T(8,128)(2,1)S(1)} %fusion.4) | copy-start | bytes 786436
  54.2 3.1 %copy-start.5 = (s32[153]{0:T(256)S(1)}, s32[153]{0:T(256)}, u32[]{:S(2)}) copy-start(s32[153]{0:T(256)} %constant.87) | copy-start | bytes 1840
  57.3 53.1 %copy-start.8 = (bf16[153]{0:T(256)(128)(2,1)S(1)}, bf16[153]{0:T(256)(128)(2,1)}, u32[]{:S(2)}) copy-start(bf16[153]{0:T(256)(128)(2,1)} %constant.79.clone) | copy-start | bytes 922
  58.6 52.2 %copy-start.2 = (f32[2,128,512]{2,1,0:T(8,128)S(1)}, f32[2,128,512]{2,1,0:T(8,128)}, u32[]{:S(2)}) copy-start(f32[2,128,512]{2,1,0:T(8,128)} %fusion) | copy-start | bytes 1572868
  60.9 51.1 %copy-start.4 = (f32[256]{0:T(256)S(1)}, f32[256]{0:T(256)}, u32[]{:S(2)}) copy-start(f32[256]{0:T(256)} %param.24) | copy-start | bytes 3076
  110.4 1.7 %copy-start.1 = (bf16[2,32,32,256]{3,2,1,0:T(8,128)(2,1)S(1)}, bf16[2,32,32,256]{3,2,1,0:T(8,128)(2,1)}, u32[]{:S(2)}) copy-start(bf16[2,32,32,256]{3,2,1,0:T(8,128)(2,1)} %get-tuple-element.12) | copy-start | bytes 3145732

commit v13 on v12

--- a/solution.py
+++ b/solution.py
@@ -77,21 +77,33 @@
     return (combined * factor * gains[None]).astype(jnp.bfloat16)
 
 
+def scan_rounds(n):
+    rounds = 1
+    while 4 ** rounds < n:
+        rounds += 1
+    return rounds
+
+
 def scan_masks(lengths, row_count, place, blocks, rounds):
     openings = jnp.cumsum(lengths) - lengths
     ids = jnp.arange(blocks, dtype=jnp.int32)
     firsts = ids * row_count
     inside = (openings[None, :] >= firsts[:, None]) & (openings[None, :] < firsts[:, None] + row_count)
     flags = jnp.any(inside, axis=1).astype(jnp.int32)
-    spans = jnp.asarray([1 << (k // 2) for k in range(2 * rounds)], jnp.int32)
-    tops = place - jnp.asarray([k % 2 for k in range(2 * rounds)], jnp.int32)
-    lows = place - spans + 1
+    reach, drop = [], []
+    for k in range(rounds):
+        for j in range(1, 4):
+            for top in (0, 1):
+                reach.append(j * 4**k - 1)
+                drop.append(top)
+    lows = place - jnp.asarray(reach, jnp.int32)
+    tops = place - jnp.asarray(drop, jnp.int32)
     covered = (ids[None, :] >= lows[:, None]) & (ids[None, :] <= tops[:, None])
     hits = jnp.sum(jnp.where(covered, flags[None, :], 0), axis=1)
     return (hits == 0).astype(jnp.float32)
 
 
-def scan_kernel(n, rounds, s_ref, m_ref, xo_ref, e_ref, go_ref, parts, recv, send_sem, recv_sem,
+def scan_kernel(n, rounds, s_ref, m_ref, xo_ref, e_ref, go_ref, parts, recv, acc, send_sem, recv_sem,
                 send_o, recv_o, send_x, recv_x, own):
     me = lax.axis_index("dp")
     col = lax.axis_index("mp")
@@ -111,21 +123,20 @@
     each(1, chips, lambda k: pl.semaphore_signal(
         barrier, 1, device_id=((me + 2 * k) % n, col), device_id_type=MESH))
     pl.semaphore_signal(barrier, 1, device_id=(mate, col), device_id_type=MESH)
-    for k in range(rounds):
-        d = 1 << k
-
-        @pl.when(me + d < n)
-        def _():
-            pl.semaphore_signal(barrier, 1, device_id=(me + d, col), device_id_type=MESH)
-
-        @pl.when(me >= d)
-        def _():
-            pl.semaphore_signal(barrier, 1, device_id=(me - d, col), device_id_type=MESH)
-
     peers = 0
     for k in range(rounds):
-        d = 1 << k
-        peers = peers + (me // d + n - 1) // n + ((n - 1 - me) // d + n - 1) // n
+        for j in range(1, 4):
+            d = j * 4**k
+
+            @pl.when(me + d < n)
+            def _():
+                pl.semaphore_signal(barrier, 1, device_id=(me + d, col), device_id_type=MESH)
+
+            @pl.when(me >= d)
+            def _():
+                pl.semaphore_signal(barrier, 1, device_id=(me - d, col), device_id_type=MESH)
+
+            peers = peers + (me // d + n - 1) // n + ((n - 1 - me) // d + n - 1) // n
     pl.semaphore_wait(barrier, peers + chips)
 
     mine = pltpu.make_async_copy(xo_ref, go_ref.at[side, chip], own)
@@ -173,35 +184,40 @@
     e_ref[...] = jnp.zeros_like(e_ref)
     copies = []
     for k in range(rounds):
-        d = 1 << k
         src = s_ref if k == 0 else parts.at[k - 1]
-        copy = pltpu.make_async_remote_copy(
-            src_ref=src,
-            dst_ref=recv.at[k],
-            send_sem=send_sem.at[k],
-            recv_sem=recv_sem.at[k],
-            device_id=(me + d, col),
-            device_id_type=MESH,
-        )
-        copies.append(copy)
-
-        @pl.when(me + d < n)
-        def _():
-            copy.start()
-
-        @pl.when(me >= d)
-        def _():
-            copy.wait_recv()
-            got = recv[k].astype(jnp.float32)
-            if k < rounds - 1:
-                parts[k] = (src[...].astype(jnp.float32) + m_ref[2 * k] * got).astype(parts.dtype)
-            e_ref[...] += m_ref[2 * k + 1] * got
-
         if k < rounds - 1:
-
-            @pl.when(me < d)
+            acc[...] = src[...].astype(jnp.float32)
+        for j in range(1, 4):
+            d = j * 4**k
+            copy = pltpu.make_async_remote_copy(
+                src_ref=src,
+                dst_ref=recv.at[k, j - 1],
+                send_sem=send_sem.at[k, j - 1],
+                recv_sem=recv_sem.at[k, j - 1],
+                device_id=(me + d, col),
+                device_id_type=MESH,
+            )
+            copies.append((copy, d))
+
+            @pl.when(me + d < n)
             def _():
-                parts[k] = src[...]
+                copy.start()
+
+        for j in range(1, 4):
+            d = j * 4**k
+            copy = copies[3 * k + j - 1][0]
+            row = 6 * k + 2 * (j - 1)
+
+            @pl.when(me >= d)
+            def _():
+                copy.wait_recv()
+                got = recv[k, j - 1].astype(jnp.float32)
+                if k < rounds - 1:
+                    acc[...] += m_ref[row] * got
+                e_ref[...] += m_ref[row + 1] * got
+
+        if k < rounds - 1:
+            parts[k] = acc[...].astype(parts.dtype)
 
     each(1, chips, lambda k: from_far(k).wait_recv())
     mine.wait()
@@ -210,12 +226,11 @@
     each(1, chips, lambda k: to_far(k).wait_send())
     swap_out.wait_send()
 
-    for k in range(rounds):
-        d = 1 << k
+    for copy, d in copies:
 
         @pl.when(me + d < n)
         def _():
-            copies[k].wait_send()
+            copy.wait_send()
 
 
 def carried_scan(summary, masks, piece, n, rounds):
@@ -236,9 +251,10 @@
         out_specs=(pl.BlockSpec(memory_space=pltpu.VMEM), pl.BlockSpec(memory_space=pltpu.VMEM)),
         scratch_shapes=[
             pltpu.VMEM((max(rounds - 1, 1),) + flat.shape, jnp.bfloat16),
-            pltpu.VMEM((rounds,) + flat.shape, jnp.bfloat16),
-            pltpu.SemaphoreType.DMA((rounds,)),
-            pltpu.SemaphoreType.DMA((rounds,)),
+            pltpu.VMEM((rounds, 3) + flat.shape, jnp.bfloat16),
+            pltpu.VMEM(flat.shape, jnp.float32),
+            pltpu.SemaphoreType.DMA((rounds, 3)),
+            pltpu.SemaphoreType.DMA((rounds, 3)),
             pltpu.SemaphoreType.DMA((n // 2,)),
             pltpu.SemaphoreType.DMA((n // 2,)),
             pltpu.SemaphoreType.DMA(()),
@@ -248,7 +264,7 @@
         compiler_params=pltpu.CompilerParams(collective_id=0, has_side_effects=True),
         cost_estimate=pl.CostEstimate(
             flops=3 * rounds * size,
-            bytes_accessed=6 * rounds * size + 2 * n * piece.size,
+            bytes_accessed=18 * rounds * size + 2 * n * piece.size,
             transcendentals=0,
         ),
     )(flat, masks, piece)
@@ -501,7 +517,7 @@
     )
     part_low = jnp.where(adapter[:, None] == owners[None, :], part_low, 0.0).astype(jnp.bfloat16)
     cols = lax.axis_size("mp")
-    rounds = max(1, (blocks - 1).bit_length())
+    rounds = scan_rounds(blocks)
     masks = scan_masks(lengths, row_count, place, blocks, rounds)
     gathered, low_parts = direct_gather(local, part_low, masks, blocks, cols)
     gathered = gathered.reshape(blocks * local.shape[0], local.shape[1])

time: 157 us -> 160 us (1.019)
  the two profiles are of different devices: /device:TPU:62 before, /device:TPU:58 now
where the time goes in v13:
time: 160 us; the launch traced here: 159 us
  Pallas kernels  127 us (79%)
  matrix products  11.8 us (7%)
  local copies, waits for them, and re-layouts  10.6 us (7%)
  other arithmetic  9.8 us (6%)
    pallas_call x1, Pallas kernels, ring_scatter(): pl.pallas_call(functools.partial(ring_kernel, m), out_shape=jax.ShapeDtyp...  45.9 us
    pallas_call x1, Pallas kernels, carried_scan(): pl.pallas_call(functools.partial(scan_kernel, n, rounds), out_shape=(jax....  42.1 us
    pallas_call x1, Pallas kernels, direct_gather(): pl.pallas_call(functools.partial(gather_kernel, n, m), out_shape=(jax.Sha...  38.9 us

profile of v13, /device:TPU:58, one launch (start us, length us, event | category | flops | bytes accessed | tf_op | source)
XLA Modules:
  0.0 159.5 jit_solution(15240147615446538050)
XLA Ops:
  0.0 0.0 copy-start
  0.0 0.0 copy-start.9
  0.0 1.6 pad_maximum_fusion.2.xd_ref
  1.6 0.8 reduce-window.8
  2.4 0.1 convert_reduce_fusion
  2.5 0.7 select_reduce_fusion.1
  3.3 2.3 %fusion.5.xm_ref = bf16[512,32]{1,0:T(8,128)(2,1)} fusion(bf16[512,2048]{1,0:T(8,128)(2,1)S(1)} %copy-done, bf16[2048,32]{0,1:T(8,128)(2,1)} %param.20, s32[32]{0:T(128)S(1)} %fusion.18, s32[512]{0:T(512)S(1)} %select_reduce_fusion.1), kind=kOutput, calls=%fused_computation.12 | convolution fusion | flops 67158016 | bytes 2263168 | tf_op jit(solution)/shard_map/dot_general | solution.py:514
  5.6 0.1 and_reduce_fusion
  5.7 0.0 copy-done.6
  5.7 0.2 select_reduce_fusion
  5.9 0.5 compare_convert_fusion.1.early_ref.m_ref
  6.4 38.9 %shard_map.154 = (bf16[2,32,32,320]{3,2,1,0:T(8,128)(2,1)}, bf16[8,512,32]{2,1,0:T(8,128)(2,1)}) custom-call(bf16[32,320]{1,0:T(8,128)(2,1)} %pad_maximum_fusion.2.xd_ref, bf16[512,32]{1,0:T(8,128)(2,1)} %fusion.5.xm_ref, f32[18]{0:T(128)} %compare_convert_fusion.1.early_ref.m_ref), custom_call_target="tpu_custom_call" | custom-call | bytes 1572864 | tf_op jit(solution)/shard_map/pallas_call | solution.py:375
  45.3 1.5 copy.57
  46.8 0.0 copy-done.3
  46.8 0.3 fusion.24
  47.1 1.7 %copy.56 = bf16[32,2,32,320]{3,2,1,0:T(8,128)(2,1)S(1)} copy(bf16[32,2,32,320]{3,2,0,1:T(8,128)(2,1)} %bitcast.58) | data formatting | bytes 2621440 | tf_op jit(solution)/shard_map/transpose | solution.py:395
  48.8 1.1 fusion.4
  49.9 0.0 copy-start.10
  50.0 0.7 convolution_convert_fusion.3
  50.7 1.1 convolution_convert_fusion.2
  51.8 0.2 fusion.11
  52.0 1.8 %fusion = f32[2,128,512]{2,1,0:T(8,128)} fusion(bf16[512,2,128]{0,2,1:T(8,128)(2,1)S(1)} %bitcast.74, bf16[512,2,16]{0,2,1:T(8,128)(2,1)S(1)} %bitcast.66, bf16[512,2,16]{0,2,1:T(8,128)(2,1)S(1)} %bitcast.63, pred[512,512]{1,0:T(8,128)(4,1)S(1)} %fusion.11), kind=kOutput, calls=%fused_computation.4 | convolution fusion | flops 154664960 | bytes 1114112 | tf_op jit(solution)/shard_map/hij,jhe->ihe/dot_general | solution.py:59
  53.8 0.1 multiply_convert_fusion
  53.9 0.5 copy.63
  54.6 0.0 copy-start.5
  54.6 0.1 multiply_convert_fusion.1
  54.7 0.5 copy.59
  55.3 2.3 %pad_maximum_fusion.1 = (bf16[512,2,273]{0,1,2:T(2,128)(2,1)S(1)}, bf16[512,2,273]{0,1,2:T(2,128)(2,1)S(1)}) fusion(bf16[512,2,256]{0,1,2:T(2,128)(2,1)S(1)} %copy.63, bf16[512,2,16]{0,1,2:T(2,128)(2,1)S(1)} %copy.62, bf16[273]{0:T(512)(128)(2,1)S(1)} %pad.3.clone, bf16[512,2,256]{0,1,2:T(2,128)(2,1)S(1)} %copy.59, bf16[512,2,16]{0,1,2:T(2,128)(2,1)S(1)} %copy.58), kind=kLoop, calls=%fused_computation.27 | loop fusion | flops 1118208 | bytes 2232866 | tf_op jit(solution)/shard_map/concatenate | solution.py:27
  57.6 0.0 copy-start.8
  57.6 1.3 gather_fusion
  58.9 0.6 fusion.23
  59.5 0.1 compare_reduce_fusion
  59.6 1.3 and_convert_fusion
  60.9 0.3 multiply_bitcast_fusion.1
  61.2 0.0 copy-start.4
  61.2 1.2 convolution_convert_fusion.1
  62.4 0.7 convert_element_type.103.s_ref
  63.1 42.1 %shard_map.155 = (f32[306,128]{1,0:T(8,128)}, bf16[2,32,32,256]{3,2,1,0:T(8,128)(2,1)}) custom-call(bf16[306,128]{1,0:T(8,128)(2,1)} %convert_element_type.103.s_ref, f32[18]{0:T(128)} %compare_convert_fusion.1.early_ref.m_ref, bf16[32,256]{1,0:T(8,128)(2,1)} %bitcast.69), custom_call_target="tpu_custom_call" | custom-call | flops 352512 | bytes 3163648 | tf_op jit(solution)/shard_map/pallas_call | solution.py:240
  105.1 0.9 convert_element_type.104
  106.1 0.7 convert_element_type.105
  106.7 1.3 gather_fusion.1
  108.0 0.4 multiply_bitcast_fusion
  108.4 1.2 multiply_reduce_fusion
  109.6 0.1 multiply_convert_fusion.2
  109.7 0.1 copy.65
  109.8 2.1 %convolution_convert_fusion.x_ref = bf16[512,2048]{1,0:T(8,128)(2,1)} fusion(bf16[512,256]{0,1:T(8,128)(2,1)S(1)} %bitcast.62, bf16[2048,256]{1,0:T(8,128)(2,1)S(1)} %bitcast.55), kind=kOutput, calls=%fused_computation.2 | convolution fusion | flops 537919488 | bytes 3407872 | tf_op jit(solution)/shard_map/dot_general | solution.py:544
  111.9 45.9 %shard_map.156 = bf16[512,256]{1,0:T(8,128)(2,1)} custom-call(bf16[512,2048]{1,0:T(8,128)(2,1)} %convolution_convert_fusion.x_ref), custom_call_target="tpu_custom_call" | custom-call | flops 2097152 | bytes 4194304 | tf_op jit(solution)/shard_map/pallas_call | solution.py:469
  157.8 1.7 %copy.75 = bf16[512,256]{1,0:T(8,128)(2,1)} copy(bf16[512,256]{1,0:T(8,128)(2,1)} %shard_map.156) | data formatting | bytes 524288
  (29 shorter events, 0.2 us)
Async XLA Ops:
  0.0 3.3 %copy-start = (bf16[512,2048]{1,0:T(8,128)(2,1)S(1)}, bf16[512,2048]{1,0:T(8,128)(2,1)}, u32[]{:S(2)}) copy-start(bf16[512,2048]{1,0:T(8,128)(2,1)} %param.16) | copy-start | bytes 6291460
  0.0 5.7 %copy-start.6 = (s32[18]{0:T(128)S(1)}, s32[18]{0:T(128)}, u32[]{:S(2)}) copy-start(s32[18]{0:T(128)} %constant.84) | copy-start | bytes 220
  0.0 5.7 %copy-start.7 = (s32[18]{0:T(128)S(1)}, s32[18]{0:T(128)}, u32[]{:S(2)}) copy-start(s32[18]{0:T(128)} %constant.83) | copy-start | bytes 220
  0.0 5.5 %copy-start.9 = (s32[4]{0:T(128)S(1)}, s32[4]{0:T(128)}, u32[]{:S(2)}) copy-start(s32[4]{0:T(128)} %param.22) | copy-start | bytes 52
  3.3 43.6 %copy-start.3 = (bf16[256,256]{1,0:T(8,128)(2,1)S(1)}, bf16[256,256]{1,0:T(8,128)(2,1)}, u32[]{:S(2)}) copy-start(bf16[256,256]{1,0:T(8,128)(2,1)} %param.21) | copy-start | bytes 393220
  49.9 4.5 %copy-start.10 = (bf16[512,256]{0,1:T(8,128)(2,1)}, bf16[512,256]{0,1:T(8,128)(2,1)S(1)}, u32[]{:S(2)}) copy-start(bf16[512,256]{0,1:T(8,128)(2,1)S(1)} %fusion.4) | copy-start | bytes 786436
  54.6 3.1 %copy-start.5 = (s32[153]{0:T(256)S(1)}, s32[153]{0:T(256)}, u32[]{:S(2)}) copy-start(s32[153]{0:T(256)} %constant.86) | copy-start | bytes 1840
  57.6 50.4 %copy-start.8 = (bf16[153]{0:T(256)(128)(2,1)S(1)}, bf16[153]{0:T(256)(128)(2,1)}, u32[]{:S(2)}) copy-start(bf16[153]{0:T(256)(128)(2,1)} %constant.78.clone) | copy-start | bytes 922
  58.9 49.5 %copy-start.2 = (f32[2,128,512]{2,1,0:T(8,128)S(1)}, f32[2,128,512]{2,1,0:T(8,128)}, u32[]{:S(2)}) copy-start(f32[2,128,512]{2,1,0:T(8,128)} %fusion) | copy-start | bytes 1572868
  61.2 48.4 %copy-start.4 = (f32[256]{0:T(256)S(1)}, f32[256]{0:T(256)}, u32[]{:S(2)}) copy-start(f32[256]{0:T(256)} %param.24) | copy-start | bytes 3076
  108.0 1.7 %copy-start.1 = (bf16[2,32,32,256]{3,2,1,0:T(8,128)(2,1)S(1)}, bf16[2,32,32,256]{3,2,1,0:T(8,128)(2,1)}, u32[]{:S(2)}) copy-start(bf16[2,32,32,256]{3,2,1,0:T(8,128)(2,1)} %get-tuple-element.12) | copy-start | bytes 3145732

commit v14 on v12

--- a/solution.py
+++ b/solution.py
@@ -379,87 +379,82 @@
     return jnp.transpose(gd, (1, 0, 2, 3)), gm
 
 
-def ring_kernel(m, x_ref, o_ref, acc_a, acc_b, got_a, got_b, send_a, recv_a, send_b, recv_b):
+def ring_kernel(m, n_ref, w_ref, o_ref, acc_a, acc_b, got_a, got_b, send_a, recv_a, send_b, recv_b):
     me = lax.axis_index("dp")
     col = lax.axis_index("mp")
     right = (col + 1) % m
     left = (col + m - 1) % m
-    width = o_ref.shape[1]
-    half = width // 2
+    half = o_ref.shape[2]
+    width = 2 * half
     barrier = pltpu.get_barrier_semaphore()
     pl.semaphore_signal(barrier, 1, device_id=(me, right), device_id_type=MESH)
     pl.semaphore_signal(barrier, 1, device_id=(me, left), device_id_type=MESH)
     pl.semaphore_wait(barrier, 2)
 
-    def piece(t, side):
-        return pl.ds(pl.multiple_of(t * width + side * half, half), half)
+    def own(t, side):
+        rows = w_ref[pl.ds(pl.multiple_of(t * width + side * half, half), half), :]
+        return lax.dot_general(
+            n_ref[...], rows, (((1,), (1,)), ((), ())), preferred_element_type=jnp.float32
+        )
 
     copies = []
     for s in range(m - 1):
         ta = (col + 2 * m - 1 - s) % m
         tb = (col + 1 + s) % m
-        if s == 0:
-            src_a = x_ref.at[:, piece(ta, 0)]
-            src_b = x_ref.at[:, piece(tb, 1)]
-        else:
+        part_a = own(ta, 0)
+        part_b = own(tb, 1)
+        if s > 0:
             copies[-1][0].wait_recv()
-            copies[-1][1].wait_recv()
-            acc_a[s - 1] = (
-                got_a[s - 1].astype(jnp.float32) + x_ref[:, piece(ta, 0)].astype(jnp.float32)
-            ).astype(acc_a.dtype)
-            acc_b[s - 1] = (
-                got_b[s - 1].astype(jnp.float32) + x_ref[:, piece(tb, 1)].astype(jnp.float32)
-            ).astype(acc_b.dtype)
-            src_a = acc_a.at[s - 1]
-            src_b = acc_b.at[s - 1]
+            part_a = part_a + got_a[s - 1].astype(jnp.float32)
+        acc_a[s] = part_a.astype(acc_a.dtype)
         ca = pltpu.make_async_remote_copy(
-            src_ref=src_a,
+            src_ref=acc_a.at[s],
             dst_ref=got_a.at[s],
             send_sem=send_a.at[s],
             recv_sem=recv_a.at[s],
             device_id=(me, right),
             device_id_type=MESH,
         )
+        ca.start()
+        if s > 0:
+            copies[-1][1].wait_recv()
+            part_b = part_b + got_b[s - 1].astype(jnp.float32)
+        acc_b[s] = part_b.astype(acc_b.dtype)
         cb = pltpu.make_async_remote_copy(
-            src_ref=src_b,
+            src_ref=acc_b.at[s],
             dst_ref=got_b.at[s],
             send_sem=send_b.at[s],
             recv_sem=recv_b.at[s],
             device_id=(me, left),
             device_id_type=MESH,
         )
-        ca.start()
         cb.start()
         copies.append((ca, cb))
     copies[-1][0].wait_recv()
     copies[-1][1].wait_recv()
-    last = m - 2
-    o_ref[:, :half] = (
-        got_a[last].astype(jnp.float32) + x_ref[:, piece(col, 0)].astype(jnp.float32)
-    ).astype(o_ref.dtype)
-    o_ref[:, half:] = (
-        got_b[last].astype(jnp.float32) + x_ref[:, piece(col, 1)].astype(jnp.float32)
-    ).astype(o_ref.dtype)
+    o_ref[0] = got_a[m - 2]
+    o_ref[1] = got_b[m - 2]
     for ca, cb in copies:
         ca.wait_send()
         cb.wait_send()
 
 
-def ring_scatter(x, m):
-    rows, total = x.shape
+def ring_scatter(normed, out_t, m):
+    rows = normed.shape[0]
+    total = out_t.shape[0]
     width = total // m
     half = width // 2
     slot = (m - 1, rows, half)
-    return pl.pallas_call(
+    got = pl.pallas_call(
         functools.partial(ring_kernel, m),
-        out_shape=jax.ShapeDtypeStruct((rows, width), x.dtype),
-        in_specs=[pl.BlockSpec(memory_space=pltpu.VMEM)],
+        out_shape=jax.ShapeDtypeStruct((2, rows, half), jnp.bfloat16),
+        in_specs=[pl.BlockSpec(memory_space=pltpu.VMEM)] * 2,
         out_specs=pl.BlockSpec(memory_space=pltpu.VMEM),
         scratch_shapes=[
-            pltpu.VMEM(slot, x.dtype),
-            pltpu.VMEM(slot, x.dtype),
-            pltpu.VMEM(slot, x.dtype),
-            pltpu.VMEM(slot, x.dtype),
+            pltpu.VMEM(slot, jnp.bfloat16),
+            pltpu.VMEM(slot, jnp.bfloat16),
+            pltpu.VMEM(slot, jnp.bfloat16),
+            pltpu.VMEM(slot, jnp.bfloat16),
             pltpu.SemaphoreType.DMA((m - 1,)),
             pltpu.SemaphoreType.DMA((m - 1,)),
             pltpu.SemaphoreType.DMA((m - 1,)),
@@ -467,9 +462,16 @@
         ],
         compiler_params=pltpu.CompilerParams(collective_id=2, has_side_effects=True),
         cost_estimate=pl.CostEstimate(
-            flops=2 * rows * total, bytes_accessed=4 * rows * total, transcendentals=0
+            flops=2 * rows * normed.shape[1] * total,
+            bytes_accessed=2 * (normed.size + out_t.size) + 4 * rows * total,
+            transcendentals=0,
         ),
-    )(x)
+    )(normed, out_t)
+    col = lax.axis_index("mp")
+    mine = lax.dynamic_slice_in_dim(out_t, col * width, width, axis=0)
+    own = lax.dot_general(normed, mine, (((1,), (1,)), ((), ())), preferred_element_type=jnp.float32)
+    got = jnp.concatenate([got[0], got[1]], axis=1).astype(jnp.float32)
+    return (got + own).astype(jnp.bfloat16)
 
 
 def per_device(
@@ -525,10 +527,7 @@
     normed = finish(within, query_map, carried, request, starts, gains).reshape(
         row_count, heads_here * value_width
     )
-    partial_terms = lax.dot_general(
-        normed, out_t, (((1,), (1,)), ((), ())), preferred_element_type=jnp.float32
-    )
-    return ring_scatter(partial_terms.astype(jnp.bfloat16), cols)
+    return ring_scatter(normed, out_t, cols)
 
 
 def solution(mesh):

time: 157 us -> 156 us (level)
  the two profiles are of different devices: /device:TPU:62 before, /device:TPU:60 now
where the time goes in v14:
time: 156 us
  Pallas kernels  123 us (79%)
  matrix products  11.8 us (8%)
  local copies, waits for them, and re-layouts  11.1 us (7%)
  other arithmetic  9.8 us (6%)
    pallas_call x1, Pallas kernels, carried_scan(): pl.pallas_call(functools.partial(scan_kernel, n, rounds), out_shape=(jax....  44 us
    pallas_call x1, Pallas kernels, ring_scatter(): pl.pallas_call(functools.partial(ring_kernel, m), out_shape=jax.ShapeDtyp...  40.1 us
    pallas_call x1, Pallas kernels, direct_gather(): pl.pallas_call(functools.partial(gather_kernel, n, m), out_shape=(jax.Sha...  38.6 us

profile of v14, /device:TPU:60, one launch (start us, length us, event | category | flops | bytes accessed | tf_op | source)
XLA Modules:
  0.0 155.8 jit_solution(9362762319572994651)
XLA Ops:
  0.0 0.0 copy-start.8
  0.0 1.6 %pad_maximum_fusion.2.xd_ref = bf16[32,320]{1,0:T(8,128)(2,1)} fusion(bf16[32,256]{1,0:T(8,128)(2,1)} %param.19, bf16[32,32]{1,0:T(8,128)(2,1)} %param.18, bf16[32,32]{1,0:T(8,128)(2,1)} %param.17), kind=kLoop, calls=%fused_computation.42 | loop fusion | flops 61440 | bytes 40960 | tf_op jit(solution)/shard_map/concatenate | solution.py:499
  1.6 0.8 reduce-window.8
  2.4 0.1 convert_reduce_fusion
  2.5 0.7 select_reduce_fusion.1
  3.3 2.3 %fusion.6.xm_ref = bf16[512,32]{1,0:T(8,128)(2,1)} fusion(bf16[512,2048]{1,0:T(8,128)(2,1)S(1)} %copy-done, bf16[2048,32]{0,1:T(8,128)(2,1)} %param.20, s32[32]{0:T(128)S(1)} %fusion.20, s32[512]{0:T(512)S(1)} %select_reduce_fusion.1), kind=kOutput, calls=%fused_computation.13 | convolution fusion | flops 67158016 | bytes 2263168 | tf_op jit(solution)/shard_map/dot_general | solution.py:500
  5.6 0.0 copy-done.8
  5.6 0.1 and_reduce_fusion
  5.7 0.2 select_reduce_fusion
  5.9 0.5 compare_convert_fusion.1.early_ref.m_ref
  6.4 38.6 %shard_map.154 = (bf16[2,32,32,320]{3,2,1,0:T(8,128)(2,1)}, bf16[8,512,32]{2,1,0:T(8,128)(2,1)}) custom-call(bf16[32,320]{1,0:T(8,128)(2,1)} %pad_maximum_fusion.2.xd_ref, bf16[512,32]{1,0:T(8,128)(2,1)} %fusion.6.xm_ref, f32[12]{0:T(128)} %compare_convert_fusion.1.early_ref.m_ref), custom_call_target="tpu_custom_call" | custom-call | bytes 1572864 | tf_op jit(solution)/shard_map/pallas_call | solution.py:359
  45.0 1.5 copy.61
  46.5 0.3 fusion.27
  46.8 1.7 %copy.60 = bf16[32,2,32,320]{3,2,1,0:T(8,128)(2,1)S(1)} copy(bf16[32,2,32,320]{3,2,0,1:T(8,128)(2,1)} %bitcast.60) | data formatting | bytes 2621440 | tf_op jit(solution)/shard_map/transpose | solution.py:379
  48.5 1.1 fusion.4
  49.6 0.0 copy-start.9
  49.6 0.7 convolution_convert_fusion.2
  50.4 1.1 convolution_convert_fusion.1
  51.5 0.2 fusion.12
  51.7 1.8 %fusion = f32[2,128,512]{2,1,0:T(8,128)} fusion(bf16[512,2,128]{0,2,1:T(8,128)(2,1)S(1)} %bitcast.79, bf16[512,2,16]{0,2,1:T(8,128)(2,1)S(1)} %bitcast.71, bf16[512,2,16]{0,2,1:T(8,128)(2,1)S(1)} %bitcast.68, pred[512,512]{1,0:T(8,128)(4,1)S(1)} %fusion.12), kind=kOutput, calls=%fused_computation.3 | convolution fusion | flops 154664960 | bytes 1114112 | tf_op jit(solution)/shard_map/hij,jhe->ihe/dot_general | solution.py:59
  53.5 0.1 multiply_convert_fusion
  53.6 0.5 copy.67
  54.3 0.0 copy-start.4
  54.3 0.1 multiply_convert_fusion.1
  54.4 0.5 copy.63
  55.0 2.3 %pad_maximum_fusion.1 = (bf16[512,2,273]{0,1,2:T(2,128)(2,1)S(1)}, bf16[512,2,273]{0,1,2:T(2,128)(2,1)S(1)}) fusion(bf16[512,2,256]{0,1,2:T(2,128)(2,1)S(1)} %copy.67, bf16[512,2,16]{0,1,2:T(2,128)(2,1)S(1)} %copy.66, bf16[273]{0:T(512)(128)(2,1)S(1)} %pad.5.clone, bf16[512,2,256]{0,1,2:T(2,128)(2,1)S(1)} %copy.63, bf16[512,2,16]{0,1,2:T(2,128)(2,1)S(1)} %copy.62), kind=kLoop, calls=%fused_computation.28 | loop fusion | flops 1118208 | bytes 2232866 | tf_op jit(solution)/shard_map/concatenate | solution.py:27
  57.3 0.0 copy-start.7
  57.3 0.0 copy-done.4
  57.3 1.3 gather_fusion
  58.6 0.6 fusion.26
  59.2 0.1 compare_reduce_fusion
  59.3 1.3 and_convert_fusion
  60.6 0.3 multiply_bitcast_fusion.1
  60.9 0.0 copy-start.3
  60.9 1.2 convolution_convert_fusion
  62.1 0.7 convert_element_type.106.s_ref
  62.7 44.0 %shard_map.155 = (f32[306,128]{1,0:T(8,128)}, bf16[2,32,32,256]{3,2,1,0:T(8,128)(2,1)}) custom-call(bf16[306,128]{1,0:T(8,128)(2,1)} %convert_element_type.106.s_ref, f32[12]{0:T(128)} %compare_convert_fusion.1.early_ref.m_ref, bf16[32,256]{1,0:T(8,128)(2,1)} %bitcast.74), custom_call_target="tpu_custom_call" | custom-call | flops 705024 | bytes 2458624 | tf_op jit(solution)/shard_map/pallas_call | solution.py:225
  106.7 0.9 convert_element_type.107
  107.7 1.3 gather_fusion.1
  108.9 0.4 multiply_bitcast_fusion
  109.3 1.4 multiply_reduce_fusion
  110.8 0.1 multiply_convert_fusion.2
  110.9 0.8 copy.73.n_ref
  111.7 0.0 copy-done.1
  111.7 1.1 copy.70
  112.8 40.1 %shard_map.156 = bf16[2,512,128]{2,1,0:T(8,128)(2,1)} custom-call(bf16[512,256]{1,0:T(8,128)(2,1)} %copy.73.n_ref, bf16[2048,256]{1,0:T(8,128)(2,1)} %bitcast.64), custom_call_target="tpu_custom_call" | custom-call | flops 536870912 | bytes 5505024 | tf_op jit(solution)/shard_map/pallas_call | solution.py:448
  152.9 1.0 slice_bitcast_fusion.1
  153.9 1.9 %fusion.5 = bf16[512,256]{1,0:T(8,128)(2,1)} fusion(bf16[512,256]{0,1:T(8,128)(2,1)S(1)} %bitcast.67, bf16[512,128]{1,0:T(8,128)(2,1)S(1)} %get-tuple-element.14, bf16[512,128]{1,0:T(8,128)(2,1)S(1)} %get-tuple-element.13, bf16[2048,256]{1,0:T(8,128)(2,1)} %bitcast.65, s32[]{:T(128)S(6)} %select_n.41), kind=kOutput, calls=%fused_computation.11 | convolution fusion | flops 67895296 | bytes 917508 | tf_op jit(solution)/shard_map/dot_general | solution.py:472
  (28 shorter events, 0.2 us)
Async XLA Ops:
  0.0 3.3 %copy-start = (bf16[512,2048]{1,0:T(8,128)(2,1)S(1)}, bf16[512,2048]{1,0:T(8,128)(2,1)}, u32[]{:S(2)}) copy-start(bf16[512,2048]{1,0:T(8,128)(2,1)} %param.16) | copy-start | bytes 6291460
  0.0 5.7 %copy-start.5 = (s32[12]{0:T(128)S(1)}, s32[12]{0:T(128)}, u32[]{:S(2)}) copy-start(s32[12]{0:T(128)} %constant.88) | copy-start | bytes 148
  0.0 5.7 %copy-start.6 = (s32[12]{0:T(128)S(1)}, s32[12]{0:T(128)}, u32[]{:S(2)}) copy-start(s32[12]{0:T(128)} %constant.89) | copy-start | bytes 148
  0.0 5.6 %copy-start.8 = (s32[4]{0:T(128)S(1)}, s32[4]{0:T(128)}, u32[]{:S(2)}) copy-start(s32[4]{0:T(128)} %param.22) | copy-start | bytes 52
  3.3 43.2 %copy-start.2 = (bf16[256,256]{1,0:T(8,128)(2,1)S(1)}, bf16[256,256]{1,0:T(8,128)(2,1)}, u32[]{:S(2)}) copy-start(bf16[256,256]{1,0:T(8,128)(2,1)} %param.21) | copy-start | bytes 393220
  49.6 2.1 %copy-start.9 = (bf16[512,256]{0,1:T(8,128)(2,1)}, bf16[512,256]{0,1:T(8,128)(2,1)S(1)}, u32[]{:S(2)}) copy-start(bf16[512,256]{0,1:T(8,128)(2,1)S(1)} %fusion.4) | copy-start | bytes 786436
  54.3 3.1 %copy-start.4 = (s32[153]{0:T(256)S(1)}, s32[153]{0:T(256)}, u32[]{:S(2)}) copy-start(s32[153]{0:T(256)} %constant.91) | copy-start | bytes 1840
  57.3 51.6 %copy-start.7 = (bf16[153]{0:T(256)(128)(2,1)S(1)}, bf16[153]{0:T(256)(128)(2,1)}, u32[]{:S(2)}) copy-start(bf16[153]{0:T(256)(128)(2,1)} %constant.83.clone) | copy-start | bytes 922
  60.9 49.9 %copy-start.3 = (f32[256]{0:T(256)S(1)}, f32[256]{0:T(256)}, u32[]{:S(2)}) copy-start(f32[256]{0:T(256)} %param.24) | copy-start | bytes 3076
  109.3 2.4 %copy-start.1 = (bf16[2,32,32,256]{3,2,1,0:T(8,128)(2,1)S(1)}, bf16[2,32,32,256]{3,2,1,0:T(8,128)(2,1)}, u32[]{:S(2)}) copy-start(bf16[2,32,32,256]{3,2,1,0:T(8,128)(2,1)} %get-tuple-element.12) | copy-start | bytes 3145732

commit v15 on v14

--- a/solution.py
+++ b/solution.py
@@ -25,6 +25,15 @@
     )
     constant = jnp.ones(inputs.shape[:-1] + (1,), jnp.float32)
     return jnp.concatenate([constant, 0.5 * inputs, squares * (0.25 / math.sqrt(2.0))], axis=-1)
+
+
+def packed_taylor(inputs):
+    width = inputs.shape[-1]
+    squares = [inputs[..., a : a + 1] * inputs[..., a:] for a in range(width)]
+    constant = jnp.ones(inputs.shape[:-1] + (1,), jnp.float32)
+    return jnp.concatenate(
+        [constant, 0.5 * inputs] + [s * (0.25 / math.sqrt(2.0)) for s in squares], axis=-1
+    )
 
 
 def packed_features(width):
@@ -57,10 +66,10 @@
     allowed = (indexes[None, :] <= indexes[:, None]) & (request[None, :] == request[:, None])
     weights = jnp.where(allowed[None], weights, 0.0).astype(jnp.bfloat16)
     within = jnp.einsum("hij,jhe->ihe", weights, values, preferred_element_type=jnp.float32)
-    index, weight = packed_features(query.shape[-1])
-    query_map = taylor(query.astype(jnp.float32)).astype(jnp.bfloat16)
-    query_map = query_map[..., index] * jnp.asarray(weight, jnp.bfloat16)
-    key_map = taylor(key_rows.astype(jnp.float32)).astype(jnp.bfloat16)[..., index]
+    _, weight = packed_features(query.shape[-1])
+    query_map = packed_taylor(query.astype(jnp.float32)).astype(jnp.bfloat16)
+    query_map = query_map * jnp.asarray(weight, jnp.bfloat16)
+    key_map = packed_taylor(key_rows.astype(jnp.float32)).astype(jnp.bfloat16)
     tail_mask = (request == request[-1]).astype(jnp.bfloat16)
     masked_keys = key_map * tail_mask[:, None, None]
     summary = jnp.einsum("ihf,ihe->hfe", masked_keys, values, preferred_element_type=jnp.float32)

time: 156 us -> 177 us (1.13)
  the two profiles are of different devices: /device:TPU:60 before, /device:TPU:62 now
where the time goes in v15:
time: 177 us; the launch traced here: 175 us
  Pallas kernels  123 us (69%)
  local copies, waits for them, and re-layouts  23.1 us (13%)
  other arithmetic  18 us (10%)
  matrix products  10.8 us (6%)
    pallas_call x1, Pallas kernels, carried_scan(): pl.pallas_call(functools.partial(scan_kernel, n, rounds), out_shape=(jax....  44.6 us
    pallas_call x1, Pallas kernels, ring_scatter(): pl.pallas_call(functools.partial(ring_kernel, m), out_shape=jax.ShapeDtyp...  39.5 us
    pallas_call x1, Pallas kernels, direct_gather(): pl.pallas_call(functools.partial(gather_kernel, n, m), out_shape=(jax.Sha...  38.5 us
    concatenate x2, local copies, waits for them, and re-layouts, packed_taylor(): jnp.concatenate([constant, 0.5 * inputs] + [s * (0.25 / math.sqrt(2.0)) f...  15.4 us
    another operation x33, other arithmetic  10.9 us

profile of v15, /device:TPU:62, one launch (start us, length us, event | category | flops | bytes accessed | tf_op | source)
XLA Modules:
  0.0 175.0 jit_solution(15395782686588378230)
XLA Ops:
  0.0 1.6 pad_maximum_fusion.xd_ref
  1.6 0.8 reduce-window.8
  2.4 0.1 convert_reduce_fusion
  2.5 0.7 select_reduce_fusion.1
  3.3 2.3 %fusion.6.xm_ref = bf16[512,32]{1,0:T(8,128)(2,1)} fusion(bf16[512,2048]{1,0:T(8,128)(2,1)S(1)} %copy-done, bf16[2048,32]{0,1:T(8,128)(2,1)} %param.17, s32[32]{0:T(128)S(1)} %fusion.82, s32[512]{0:T(512)S(1)} %select_reduce_fusion.1), kind=kOutput, calls=%fused_computation.11 | convolution fusion | flops 67158016 | bytes 2263168 | tf_op jit(solution)/shard_map/dot_general | solution.py:509
  5.6 0.1 and_reduce_fusion
  5.7 0.2 select_reduce_fusion
  5.9 0.5 compare_convert_fusion.1.early_ref.m_ref
  6.4 38.5 %shard_map.127 = (bf16[2,32,32,320]{3,2,1,0:T(8,128)(2,1)}, bf16[8,512,32]{2,1,0:T(8,128)(2,1)}) custom-call(bf16[32,320]{1,0:T(8,128)(2,1)} %pad_maximum_fusion.xd_ref, bf16[512,32]{1,0:T(8,128)(2,1)} %fusion.6.xm_ref, f32[12]{0:T(128)} %compare_convert_fusion.1.early_ref.m_ref), custom_call_target="tpu_custom_call" | custom-call | bytes 1572864 | tf_op jit(solution)/shard_map/pallas_call | solution.py:368
  44.9 1.5 copy.26
  46.5 0.3 fusion.91
  46.8 1.7 copy.25
  48.5 1.1 fusion.4
  49.6 0.7 convolution_convert_fusion.2
  50.4 1.1 convolution_convert_fusion.1
  51.4 0.2 fusion.12
  51.7 1.8 %fusion = f32[2,128,512]{2,1,0:T(8,128)} fusion(bf16[512,2,128]{0,2,1:T(8,128)(2,1)S(1)} %bitcast.192, bf16[512,2,16]{0,2,1:T(8,128)(2,1)S(1)} %bitcast.149, bf16[512,2,16]{0,2,1:T(8,128)(2,1)S(1)} %bitcast.153, pred[512,512]{1,0:T(8,128)(4,1)S(1)} %fusion.12), kind=kOutput, calls=%fused_computation.1 | convolution fusion | flops 154664960 | bytes 1114112 | tf_op jit(solution)/shard_map/hij,jhe->ihe/dot_general | solution.py:68
  54.1 1.7 concatenate.15
  55.7 0.7 fusion.90
  56.5 1.9 %and_convert_fusion = (f32[512]{0:T(512)}, bf16[512]{0:T(512)(128)(2,1)S(1)}) fusion(s32[512]{0:T(512)S(1)} %convert_reduce_fusion, s32[]{:T(128)} %bitcast.12, pred[]{:T(512)} %bitcast.13, s32[]{:T(128)} %bitcast.15), kind=kLoop, calls=%fused_computation.170 | loop fusion | flops 2560 | bytes 5129 | tf_op jit(solution)/shard_map/convert_element_type | solution.py:80
  58.4 0.2 convolution_convert_fusion
  58.6 0.7 convert_element_type.90.s_ref
  59.3 44.6 %shard_map.128 = (f32[306,128]{1,0:T(8,128)}, bf16[2,32,32,256]{3,2,1,0:T(8,128)(2,1)}) custom-call(bf16[306,128]{1,0:T(8,128)(2,1)} %convert_element_type.90.s_ref, f32[12]{0:T(128)} %compare_convert_fusion.1.early_ref.m_ref, bf16[32,256]{1,0:T(8,128)(2,1)} %bitcast.179), custom_call_target="tpu_custom_call" | custom-call | flops 705024 | bytes 2458624 | tf_op jit(solution)/shard_map/pallas_call | solution.py:234
  103.9 0.9 convert_element_type.91
  104.9 0.6 multiply_convert_fusion.1
  105.6 0.6 fusion.34
  106.2 0.6 fusion.32
  106.8 0.6 fusion.30
  107.4 0.6 fusion.28
  108.1 0.6 fusion.26
  108.7 0.6 fusion.24
  109.3 0.6 fusion.22
  109.9 0.6 fusion.56
  110.5 0.6 fusion.54
  111.1 0.6 fusion.52
  111.8 0.6 fusion.50
  112.4 0.6 fusion.68
  113.0 0.6 fusion.66
  113.6 0.6 fusion.74
  114.2 0.6 fusion.79
  114.8 13.7 %concatenate.16 = bf16[512,2,153]{0,2,1:T(8,128)(2,1)S(1)} concatenate(bf16[512,2,1]{0,2,1:T(2,128)(2,1)} %copy-done.3, bf16[512,2,16]{0,2,1:T(8,128)(2,1)} %get-tuple-element.31, bf16[512,2,16]{0,2,1:T(8,128)(2,1)} %get-tuple-element.30, bf16[512,2,15]{0,2,1:T(8,128)(2,1)} %fusion.34, bf16[512,2,14]{0,2,1:T(8,128)(2,1)} %fusion.32, bf16[512,2,13]{0,2,1:T(8,128)(2,1)} %fusion.30, ...), dimensions={2} | concatenate | bytes 626688 | tf_op jit(solution)/shard_map/concatenate | solution.py:34
  128.5 1.4 multiply_reduce_fusion
  129.9 0.8 multiply_convert_fusion
  130.7 0.8 copy.32.n_ref
  131.6 1.1 copy.29
  132.7 39.5 %shard_map.129 = bf16[2,512,128]{2,1,0:T(8,128)(2,1)} custom-call(bf16[512,256]{1,0:T(8,128)(2,1)} %copy.32.n_ref, bf16[2048,256]{1,0:T(8,128)(2,1)} %bitcast.145), custom_call_target="tpu_custom_call" | custom-call | flops 536870912 | bytes 5505024 | tf_op jit(solution)/shard_map/pallas_call | solution.py:457
  172.1 1.0 slice_bitcast_fusion.1
  173.1 1.9 %fusion.5 = bf16[512,256]{1,0:T(8,128)(2,1)} fusion(bf16[512,256]{0,1:T(8,128)(2,1)S(1)} %bitcast.148, bf16[512,128]{1,0:T(8,128)(2,1)S(1)} %get-tuple-element.14, bf16[512,128]{1,0:T(8,128)(2,1)S(1)} %get-tuple-element.13, bf16[2048,256]{1,0:T(8,128)(2,1)} %bitcast.146, s32[]{:T(128)S(6)} %select_n.33), kind=kOutput, calls=%fused_computation.9 | convolution fusion | flops 67895296 | bytes 917508 | tf_op jit(solution)/shard_map/dot_general | solution.py:481
  (74 shorter events, 0.6 us)
Async XLA Ops:
  0.0 3.3 %copy-start = (bf16[512,2048]{1,0:T(8,128)(2,1)S(1)}, bf16[512,2048]{1,0:T(8,128)(2,1)}, u32[]{:S(2)}) copy-start(bf16[512,2048]{1,0:T(8,128)(2,1)} %param.13) | copy-start | bytes 6291460
  0.0 5.7 %copy-start.4 = (s32[12]{0:T(128)S(1)}, s32[12]{0:T(128)}, u32[]{:S(2)}) copy-start(s32[12]{0:T(128)} %constant.95) | copy-start | bytes 148
  0.0 5.7 %copy-start.5 = (s32[12]{0:T(128)S(1)}, s32[12]{0:T(128)}, u32[]{:S(2)}) copy-start(s32[12]{0:T(128)} %constant.96) | copy-start | bytes 148
  0.0 5.5 %copy-start.6 = (s32[4]{0:T(128)S(1)}, s32[4]{0:T(128)}, u32[]{:S(2)}) copy-start(s32[4]{0:T(128)} %param.19) | copy-start | bytes 52
  3.3 43.2 %copy-start.2 = (bf16[256,256]{1,0:T(8,128)(2,1)S(1)}, bf16[256,256]{1,0:T(8,128)(2,1)}, u32[]{:S(2)}) copy-start(bf16[256,256]{1,0:T(8,128)(2,1)} %param.18) | copy-start | bytes 393220
  54.1 54.0 %copy-start.3 = (bf16[512,2,1]{0,2,1:T(2,128)(2,1)}, bf16[512,2,1]{0,2,1:T(2,128)(2,1)S(1)}, u32[]{:S(2)}) copy-start(bf16[512,2,1]{0,2,1:T(2,128)(2,1)S(1)} %broadcast.174) | copy-start | bytes 6148
  108.1 23.5 %copy-start.1 = (bf16[2,32,32,256]{3,2,1,0:T(8,128)(2,1)S(1)}, bf16[2,32,32,256]{3,2,1,0:T(8,128)(2,1)}, u32[]{:S(2)}) copy-start(bf16[2,32,32,256]{3,2,1,0:T(8,128)(2,1)} %get-tuple-element.12) | copy-start | bytes 3145732

commit v16 on v15

--- a/solution.py
+++ b/solution.py
@@ -66,9 +66,9 @@
     allowed = (indexes[None, :] <= indexes[:, None]) & (request[None, :] == request[:, None])
     weights = jnp.where(allowed[None], weights, 0.0).astype(jnp.bfloat16)
     within = jnp.einsum("hij,jhe->ihe", weights, values, preferred_element_type=jnp.float32)
-    _, weight = packed_features(query.shape[-1])
-    query_map = packed_taylor(query.astype(jnp.float32)).astype(jnp.bfloat16)
-    query_map = query_map * jnp.asarray(weight, jnp.bfloat16)
+    index, weight = packed_features(query.shape[-1])
+    query_map = taylor(query.astype(jnp.float32)).astype(jnp.bfloat16)
+    query_map = query_map[..., index] * jnp.asarray(weight, jnp.bfloat16)
     key_map = packed_taylor(key_rows.astype(jnp.float32)).astype(jnp.bfloat16)
     tail_mask = (request == request[-1]).astype(jnp.bfloat16)
     masked_keys = key_map * tail_mask[:, None, None]

time: 177 us -> 155 us (0.88)
  the two profiles are of different devices: /device:TPU:62 before, /device:TPU:60 now
where the time goes in v16:
time: 155 us; the launch traced here: 154 us
  Pallas kernels  123 us (79%)
  local copies, waits for them, and re-layouts  11.2 us (7%)
  matrix products  10.9 us (7%)
  other arithmetic  8.89 us (6%)
    pallas_call x1, Pallas kernels, carried_scan(): pl.pallas_call(functools.partial(scan_kernel, n, rounds), out_shape=(jax....  44.1 us
    pallas_call x1, Pallas kernels, ring_scatter(): pl.pallas_call(functools.partial(ring_kernel, m), out_shape=jax.ShapeDtyp...  40 us
    pallas_call x1, Pallas kernels, direct_gather(): pl.pallas_call(functools.partial(gather_kernel, n, m), out_shape=(jax.Sha...  38.6 us

profile of v16, /device:TPU:60, one launch (start us, length us, event | category | flops | bytes accessed | tf_op | source)
XLA Modules:
  0.0 154.1 jit_solution(10182437527465946645)
XLA Ops:
  0.0 0.0 copy-start
  0.0 0.0 copy-start.8
  0.0 1.6 %pad_maximum_fusion.1.xd_ref = bf16[32,320]{1,0:T(8,128)(2,1)} fusion(bf16[32,256]{1,0:T(8,128)(2,1)} %param.18, bf16[32,32]{1,0:T(8,128)(2,1)} %param.17, bf16[32,32]{1,0:T(8,128)(2,1)} %param.16), kind=kLoop, calls=%fused_computation.73 | loop fusion | flops 61440 | bytes 40960 | tf_op jit(solution)/shard_map/concatenate | solution.py:508
  1.6 0.8 reduce-window.8
  2.4 0.1 convert_reduce_fusion
  2.5 0.7 select_reduce_fusion.1
  3.3 0.0 copy-done
  3.3 2.3 %fusion.6.xm_ref = bf16[512,32]{1,0:T(8,128)(2,1)} fusion(bf16[512,2048]{1,0:T(8,128)(2,1)S(1)} %copy-done, bf16[2048,32]{0,1:T(8,128)(2,1)} %param.19, s32[32]{0:T(128)S(1)} %fusion.51, s32[512]{0:T(512)S(1)} %select_reduce_fusion.1), kind=kOutput, calls=%fused_computation.12 | convolution fusion | flops 67158016 | bytes 2263168 | tf_op jit(solution)/shard_map/dot_general | solution.py:509
  5.6 0.0 copy-done.8
  5.6 0.1 and_reduce_fusion
  5.7 0.0 copy-done.5
  5.7 0.2 select_reduce_fusion
  5.9 0.5 compare_convert_fusion.1.early_ref.m_ref
  6.4 38.6 %shard_map.145 = (bf16[2,32,32,320]{3,2,1,0:T(8,128)(2,1)}, bf16[8,512,32]{2,1,0:T(8,128)(2,1)}) custom-call(bf16[32,320]{1,0:T(8,128)(2,1)} %pad_maximum_fusion.1.xd_ref, bf16[512,32]{1,0:T(8,128)(2,1)} %fusion.6.xm_ref, f32[12]{0:T(128)} %compare_convert_fusion.1.early_ref.m_ref), custom_call_target="tpu_custom_call" | custom-call | bytes 1572864 | tf_op jit(solution)/shard_map/pallas_call | solution.py:368
  45.0 1.5 copy.52
  46.5 0.0 copy-done.2
  46.5 0.3 fusion.59
  46.8 1.7 %copy.51 = bf16[32,2,32,320]{3,2,1,0:T(8,128)(2,1)S(1)} copy(bf16[32,2,32,320]{3,2,0,1:T(8,128)(2,1)} %bitcast.101) | data formatting | bytes 2621440 | tf_op jit(solution)/shard_map/transpose | solution.py:388
  48.5 1.1 fusion.4
  49.6 0.7 convolution_convert_fusion.2
  50.4 1.1 convolution_convert_fusion.1
  51.4 0.2 fusion.12
  51.7 1.8 %fusion = f32[2,128,512]{2,1,0:T(8,128)} fusion(bf16[512,2,128]{0,2,1:T(8,128)(2,1)S(1)} %bitcast.136, bf16[512,2,16]{0,2,1:T(8,128)(2,1)S(1)} %bitcast.113, bf16[512,2,16]{0,2,1:T(8,128)(2,1)S(1)} %bitcast.109, pred[512,512]{1,0:T(8,128)(4,1)S(1)} %fusion.12), kind=kOutput, calls=%fused_computation.2 | convolution fusion | flops 154664960 | bytes 1114112 | tf_op jit(solution)/shard_map/hij,jhe->ihe/dot_general | solution.py:68
  54.1 1.7 %concatenate.15 = bf16[512,2,153]{0,2,1:T(8,128)(2,1)S(1)} concatenate(bf16[512,2,1]{0,2,1:T(2,128)(2,1)S(1)} %broadcast.130, bf16[512,2,16]{0,2,1:T(8,128)(2,1)S(1)} %get-tuple-element.31, bf16[512,2,16]{0,2,1:T(8,128)(2,1)S(1)} %get-tuple-element.30, bf16[512,2,15]{0,2,1:T(8,128)(2,1)S(1)} %fusion.33, bf16[512,2,14]{0,2,1:T(8,128)(2,1)S(1)} %fusion.31, ...), dimensions={2} | concatenate | bytes 626688 | tf_op jit(solution)/shard_map/concatenate | solution.py:34
  55.7 0.7 fusion.58
  56.4 0.1 compare_reduce_fusion
  56.5 1.3 and_convert_fusion
  57.9 0.0 copy-start.4
  57.9 0.2 convolution_convert_fusion
  58.2 0.7 convert_element_type.98.s_ref
  58.8 44.1 %shard_map.146 = (f32[306,128]{1,0:T(8,128)}, bf16[2,32,32,256]{3,2,1,0:T(8,128)(2,1)}) custom-call(bf16[306,128]{1,0:T(8,128)(2,1)} %convert_element_type.98.s_ref, f32[12]{0:T(128)} %compare_convert_fusion.1.early_ref.m_ref, bf16[32,256]{1,0:T(8,128)(2,1)} %bitcast.127), custom_call_target="tpu_custom_call" | custom-call | flops 705024 | bytes 2458624 | tf_op jit(solution)/shard_map/pallas_call | solution.py:234
  102.9 0.9 convert_element_type.99
  103.8 0.0 copy-start.7
  103.9 0.1 multiply_convert_fusion
  104.0 0.5 copy.56
  104.6 0.0 copy-start.3
  104.6 1.4 pad_maximum_fusion
  106.1 1.3 gather_fusion
  107.4 0.4 multiply_bitcast_fusion
  107.7 0.0 copy-start.1
  107.7 1.4 multiply_reduce_fusion
  109.2 0.1 multiply_convert_fusion.1
  109.3 0.8 copy.62.n_ref
  110.2 0.0 copy-done.1
  110.2 1.1 copy.59
  111.2 40.0 %shard_map.147 = bf16[2,512,128]{2,1,0:T(8,128)(2,1)} custom-call(bf16[512,256]{1,0:T(8,128)(2,1)} %copy.62.n_ref, bf16[2048,256]{1,0:T(8,128)(2,1)} %bitcast.105), custom_call_target="tpu_custom_call" | custom-call | flops 536870912 | bytes 5505024 | tf_op jit(solution)/shard_map/pallas_call | solution.py:457
  151.2 1.0 slice_bitcast_fusion.1
  152.2 1.9 %fusion.5 = bf16[512,256]{1,0:T(8,128)(2,1)} fusion(bf16[512,256]{0,1:T(8,128)(2,1)S(1)} %bitcast.108, bf16[512,128]{1,0:T(8,128)(2,1)S(1)} %get-tuple-element.14, bf16[512,128]{1,0:T(8,128)(2,1)S(1)} %get-tuple-element.13, bf16[2048,256]{1,0:T(8,128)(2,1)} %bitcast.106, s32[]{:T(128)S(6)} %select_n.37), kind=kOutput, calls=%fused_computation.10 | convolution fusion | flops 67895296 | bytes 917508 | tf_op jit(solution)/shard_map/dot_general | solution.py:481
  (54 shorter events, 0.5 us)
Async XLA Ops:
  0.0 3.3 %copy-start = (bf16[512,2048]{1,0:T(8,128)(2,1)S(1)}, bf16[512,2048]{1,0:T(8,128)(2,1)}, u32[]{:S(2)}) copy-start(bf16[512,2048]{1,0:T(8,128)(2,1)} %param.15) | copy-start | bytes 6291460
  0.0 5.7 %copy-start.5 = (s32[12]{0:T(128)S(1)}, s32[12]{0:T(128)}, u32[]{:S(2)}) copy-start(s32[12]{0:T(128)} %constant.104) | copy-start | bytes 148
  0.0 5.7 %copy-start.6 = (s32[12]{0:T(128)S(1)}, s32[12]{0:T(128)}, u32[]{:S(2)}) copy-start(s32[12]{0:T(128)} %constant.105) | copy-start | bytes 148
  0.0 5.6 %copy-start.8 = (s32[4]{0:T(128)S(1)}, s32[4]{0:T(128)}, u32[]{:S(2)}) copy-start(s32[4]{0:T(128)} %param.21) | copy-start | bytes 52
  3.3 43.2 %copy-start.2 = (bf16[256,256]{1,0:T(8,128)(2,1)S(1)}, bf16[256,256]{1,0:T(8,128)(2,1)}, u32[]{:S(2)}) copy-start(bf16[256,256]{1,0:T(8,128)(2,1)} %param.20) | copy-start | bytes 393220
  57.9 48.2 %copy-start.4 = (s32[153]{0:T(256)S(1)}, s32[153]{0:T(256)}, u32[]{:S(2)}) copy-start(s32[153]{0:T(256)} %constant.107) | copy-start | bytes 1840
  103.8 3.5 %copy-start.7 = (bf16[153]{0:T(256)(128)(2,1)S(1)}, bf16[153]{0:T(256)(128)(2,1)}, u32[]{:S(2)}) copy-start(bf16[153]{0:T(256)(128)(2,1)} %constant.99.clone) | copy-start | bytes 922
  104.6 4.6 %copy-start.3 = (f32[256]{0:T(256)S(1)}, f32[256]{0:T(256)}, u32[]{:S(2)}) copy-start(f32[256]{0:T(256)} %param.23) | copy-start | bytes 3076
  107.7 2.4 %copy-start.1 = (bf16[2,32,32,256]{3,2,1,0:T(8,128)(2,1)S(1)}, bf16[2,32,32,256]{3,2,1,0:T(8,128)(2,1)}, u32[]{:S(2)}) copy-start(bf16[2,32,32,256]{3,2,1,0:T(8,128)(2,1)} %get-tuple-element.12) | copy-start | bytes 3145732

commit v17 on v15

--- a/solution.py
+++ b/solution.py
@@ -66,9 +66,7 @@
     allowed = (indexes[None, :] <= indexes[:, None]) & (request[None, :] == request[:, None])
     weights = jnp.where(allowed[None], weights, 0.0).astype(jnp.bfloat16)
     within = jnp.einsum("hij,jhe->ihe", weights, values, preferred_element_type=jnp.float32)
-    _, weight = packed_features(query.shape[-1])
     query_map = packed_taylor(query.astype(jnp.float32)).astype(jnp.bfloat16)
-    query_map = query_map * jnp.asarray(weight, jnp.bfloat16)
     key_map = packed_taylor(key_rows.astype(jnp.float32)).astype(jnp.bfloat16)
     tail_mask = (request == request[-1]).astype(jnp.bfloat16)
     masked_keys = key_map * tail_mask[:, None, None]
@@ -78,9 +76,9 @@
 
 def finish(within, query_map, carried, request, starts, gains):
     follows = ((request == request[0]) & jnp.logical_not(starts[0])).astype(jnp.float32)
-    cross = jnp.einsum(
-        "ihf,hfe->ihe", query_map, carried.astype(jnp.bfloat16), preferred_element_type=jnp.float32
-    )
+    _, weight = packed_features(F)
+    pairs = carried.astype(jnp.bfloat16) * jnp.asarray(weight, jnp.bfloat16)[None, :, None]
+    cross = jnp.einsum("ihf,hfe->ihe", query_map, pairs, preferred_element_type=jnp.float32)
     combined = within + follows[:, None, None] * cross
     factor = lax.rsqrt(jnp.mean(combined * combined, axis=-1, keepdims=True) + EPSILON)
     return (combined * factor * gains[None]).astype(jnp.bfloat16)

time: 177 us -> 156 us (0.88)
  local copies, waits for them, and re-layouts: 23.1 us -> 11.9 us
  other arithmetic: 18 us -> 9.09 us
    concatenate x2, local copies, waits for them, and re-layouts: 15.4 us -> 3.37 us  [packed_taylor(): jnp.concatenate([constant, 0.5 * inputs] + [s * (0.25 / math.sqrt(2.0)) f...]
    another operation x33, other arithmetic: 10.9 us -> 1.26 us
where the time goes in v17:
time: 156 us; the launch traced here: 155 us
  Pallas kernels  123 us (79%)
  local copies, waits for them, and re-layouts  11.9 us (8%)
  matrix products  10.9 us (7%)
  other arithmetic  9.09 us (6%)
    pallas_call x1, Pallas kernels, carried_scan(): pl.pallas_call(functools.partial(scan_kernel, n, rounds), out_shape=(jax....  44.6 us
    pallas_call x1, Pallas kernels, ring_scatter(): pl.pallas_call(functools.partial(ring_kernel, m), out_shape=jax.ShapeDtyp...  39.5 us
    pallas_call x1, Pallas kernels, direct_gather(): pl.pallas_call(functools.partial(gather_kernel, n, m), out_shape=(jax.Sha...  38.5 us
    concatenate x2, local copies, waits for them, and re-layouts, packed_taylor(): jnp.concatenate([constant, 0.5 * inputs] + [s * (0.25 / math.sqrt(2.0)) f...  3.37 us

profile of v17, /device:TPU:62, one launch (start us, length us, event | category | flops | bytes accessed | tf_op | source)
XLA Modules:
  0.0 155.2 jit_solution(7494915050145201554)
XLA Ops:
  0.0 0.0 copy-start
  0.0 0.0 copy-start.3
  0.0 0.0 copy-start.4
  0.0 0.0 copy-start.5
  0.0 1.6 %pad_maximum_fusion.xd_ref = bf16[32,320]{1,0:T(8,128)(2,1)} fusion(bf16[32,256]{1,0:T(8,128)(2,1)} %param.16, bf16[32,32]{1,0:T(8,128)(2,1)} %param.15, bf16[32,32]{1,0:T(8,128)(2,1)} %param.14), kind=kLoop, calls=%fused_computation.104 | loop fusion | flops 61440 | bytes 40960 | tf_op jit(solution)/shard_map/concatenate | solution.py:506
  1.6 0.8 reduce-window.8
  2.4 0.1 convert_reduce_fusion
  2.5 0.7 select_reduce_fusion.1
  3.3 0.0 copy-done
  3.3 0.0 copy-start.2
  3.3 2.3 %fusion.6.xm_ref = bf16[512,32]{1,0:T(8,128)(2,1)} fusion(bf16[512,2048]{1,0:T(8,128)(2,1)S(1)} %copy-done, bf16[2048,32]{0,1:T(8,128)(2,1)} %param.17, s32[32]{0:T(128)S(1)} %fusion.82, s32[512]{0:T(512)S(1)} %select_reduce_fusion.1), kind=kOutput, calls=%fused_computation.11 | convolution fusion | flops 67158016 | bytes 2263168 | tf_op jit(solution)/shard_map/dot_general | solution.py:507
  5.6 0.0 copy-done.5
  5.6 0.1 and_reduce_fusion
  5.7 0.0 copy-done.3
  5.7 0.0 copy-done.4
  5.7 0.2 select_reduce_fusion
  5.9 0.5 compare_convert_fusion.1.early_ref.m_ref
  6.4 38.5 %shard_map.127 = (bf16[2,32,32,320]{3,2,1,0:T(8,128)(2,1)}, bf16[8,512,32]{2,1,0:T(8,128)(2,1)}) custom-call(bf16[32,320]{1,0:T(8,128)(2,1)} %pad_maximum_fusion.xd_ref, bf16[512,32]{1,0:T(8,128)(2,1)} %fusion.6.xm_ref, f32[12]{0:T(128)} %compare_convert_fusion.1.early_ref.m_ref), custom_call_target="tpu_custom_call" | custom-call | bytes 1572864 | tf_op jit(solution)/shard_map/pallas_call | solution.py:366
  44.9 1.5 copy.26
  46.5 0.0 copy-done.2
  46.5 0.3 fusion.91
  46.8 1.7 %copy.25 = bf16[32,2,32,320]{3,2,1,0:T(8,128)(2,1)S(1)} copy(bf16[32,2,32,320]{3,2,0,1:T(8,128)(2,1)} %bitcast.141) | data formatting | bytes 2621440 | tf_op jit(solution)/shard_map/transpose | solution.py:386
  48.5 1.1 fusion.4
  49.6 0.7 convolution_convert_fusion.2
  50.4 1.1 convolution_convert_fusion.1
  51.4 0.2 fusion.12
  51.7 1.8 %fusion = f32[2,128,512]{2,1,0:T(8,128)} fusion(bf16[512,2,128]{0,2,1:T(8,128)(2,1)S(1)} %bitcast.192, bf16[512,2,16]{0,2,1:T(8,128)(2,1)S(1)} %bitcast.153, bf16[512,2,16]{0,2,1:T(8,128)(2,1)S(1)} %bitcast.149, pred[512,512]{1,0:T(8,128)(4,1)S(1)} %fusion.12), kind=kOutput, calls=%fused_computation.1 | convolution fusion | flops 154664960 | bytes 1114112 | tf_op jit(solution)/shard_map/hij,jhe->ihe/dot_general | solution.py:68
  54.1 1.7 %concatenate.16 = bf16[512,2,153]{0,2,1:T(8,128)(2,1)S(1)} concatenate(bf16[512,2,1]{0,2,1:T(2,128)(2,1)S(1)} %broadcast.174, bf16[512,2,16]{0,2,1:T(8,128)(2,1)S(1)} %get-tuple-element.48, bf16[512,2,16]{0,2,1:T(8,128)(2,1)S(1)} %get-tuple-element.47, bf16[512,2,15]{0,2,1:T(8,128)(2,1)S(1)} %fusion.33, bf16[512,2,14]{0,2,1:T(8,128)(2,1)S(1)} %fusion.31, ...), dimensions={2} | concatenate | bytes 626688 | tf_op jit(solution)/shard_map/concatenate | solution.py:34
  56.3 1.7 %concatenate.15 = bf16[512,2,153]{0,2,1:T(8,128)(2,1)S(1)} concatenate(bf16[512,2,1]{0,2,1:T(2,128)(2,1)S(1)} %broadcast.174, bf16[512,2,16]{0,2,1:T(8,128)(2,1)S(1)} %get-tuple-element.31, bf16[512,2,16]{0,2,1:T(8,128)(2,1)S(1)} %get-tuple-element.30, bf16[512,2,15]{0,2,1:T(8,128)(2,1)S(1)} %fusion.47, bf16[512,2,14]{0,2,1:T(8,128)(2,1)S(1)} %fusion.45, ...), dimensions={2} | concatenate | bytes 626688 | tf_op jit(solution)/shard_map/concatenate | solution.py:34
  58.0 0.6 fusion.90
  58.6 0.1 compare_reduce_fusion
  58.7 1.8 %compare_convert_fusion = (bf16[512]{0:T(512)(128)(2,1)S(1)}, f32[512]{0:T(512)}) fusion(s32[512]{0:T(512)S(1)} %convert_reduce_fusion, s32[]{:T(128)} %bitcast.15, pred[]{:T(512)} %bitcast.13, s32[]{:T(128)} %bitcast.12), kind=kLoop, calls=%fused_computation.169 | loop fusion | flops 2560 | bytes 5129 | tf_op jit(solution)/shard_map/convert_element_type | solution.py:71
  60.5 0.2 convolution_convert_fusion
  60.8 0.7 convert_element_type.90.s_ref
  61.5 44.6 %shard_map.128 = (f32[306,128]{1,0:T(8,128)}, bf16[2,32,32,256]{3,2,1,0:T(8,128)(2,1)}) custom-call(bf16[306,128]{1,0:T(8,128)(2,1)} %convert_element_type.90.s_ref, f32[12]{0:T(128)} %compare_convert_fusion.1.early_ref.m_ref, bf16[32,256]{1,0:T(8,128)(2,1)} %bitcast.179), custom_call_target="tpu_custom_call" | custom-call | flops 705024 | bytes 2458624 | tf_op jit(solution)/shard_map/pallas_call | solution.py:232
  106.0 0.0 copy-start.1
  106.1 1.6 %convert_element_type.91 = bf16[306,128]{1,0:T(8,128)(2,1)} convert(f32[306,128]{1,0:T(8,128)} %get-tuple-element.11) | non-fusion elementwise | flops 39168 | bytes 235008 | tf_op jit(solution)/shard_map/convert_element_type | solution.py:80
  107.7 0.9 convert_element_type.92
  108.6 1.4 multiply_reduce_fusion
  110.1 0.8 multiply_convert_fusion
  110.8 0.8 copy.32.n_ref
  111.7 0.0 copy-done.1
  111.7 1.1 copy.29
  112.8 39.5 %shard_map.129 = bf16[2,512,128]{2,1,0:T(8,128)(2,1)} custom-call(bf16[512,256]{1,0:T(8,128)(2,1)} %copy.32.n_ref, bf16[2048,256]{1,0:T(8,128)(2,1)} %bitcast.145), custom_call_target="tpu_custom_call" | custom-call | flops 536870912 | bytes 5505024 | tf_op jit(solution)/shard_map/pallas_call | solution.py:455
  152.3 1.0 slice_bitcast_fusion.1
  153.3 1.9 %fusion.5 = bf16[512,256]{1,0:T(8,128)(2,1)} fusion(bf16[512,256]{0,1:T(8,128)(2,1)S(1)} %bitcast.148, bf16[512,128]{1,0:T(8,128)(2,1)S(1)} %get-tuple-element.14, bf16[512,128]{1,0:T(8,128)(2,1)S(1)} %get-tuple-element.13, bf16[2048,256]{1,0:T(8,128)(2,1)} %bitcast.146, s32[]{:T(128)S(6)} %select_n.33), kind=kOutput, calls=%fused_computation.9 | convolution fusion | flops 67895296 | bytes 917508 | tf_op jit(solution)/shard_map/dot_general | solution.py:479
  (74 shorter events, 0.7 us)
Async XLA Ops:
  0.0 3.3 %copy-start = (bf16[512,2048]{1,0:T(8,128)(2,1)S(1)}, bf16[512,2048]{1,0:T(8,128)(2,1)}, u32[]{:S(2)}) copy-start(bf16[512,2048]{1,0:T(8,128)(2,1)} %param.13) | copy-start | bytes 6291460
  0.0 5.7 %copy-start.3 = (s32[12]{0:T(128)S(1)}, s32[12]{0:T(128)}, u32[]{:S(2)}) copy-start(s32[12]{0:T(128)} %constant.95) | copy-start | bytes 148
  0.0 5.7 %copy-start.4 = (s32[12]{0:T(128)S(1)}, s32[12]{0:T(128)}, u32[]{:S(2)}) copy-start(s32[12]{0:T(128)} %constant.96) | copy-start | bytes 148
  0.0 5.5 %copy-start.5 = (s32[4]{0:T(128)S(1)}, s32[4]{0:T(128)}, u32[]{:S(2)}) copy-start(s32[4]{0:T(128)} %param.19) | copy-start | bytes 52
  3.3 43.2 %copy-start.2 = (bf16[256,256]{1,0:T(8,128)(2,1)S(1)}, bf16[256,256]{1,0:T(8,128)(2,1)}, u32[]{:S(2)}) copy-start(bf16[256,256]{1,0:T(8,128)(2,1)} %param.18) | copy-start | bytes 393220
  106.0 5.6 %copy-start.1 = (bf16[2,32,32,256]{3,2,1,0:T(8,128)(2,1)S(1)}, bf16[2,32,32,256]{3,2,1,0:T(8,128)(2,1)}, u32[]{:S(2)}) copy-start(bf16[2,32,32,256]{3,2,1,0:T(8,128)(2,1)} %get-tuple-element.12) | copy-start | bytes 3145732

commit v18 on v16

--- a/solution.py
+++ b/solution.py
@@ -519,14 +519,14 @@
     q_full = gathered[:, :qf]
     k_full = gathered[:, qf : 2 * qf]
     v_full = gathered[:, 2 * qf :]
-    low_rank = jnp.transpose(low_parts, (1, 0, 2)).reshape(row_count, cols * part_low.shape[1])
 
     query_sum = jnp.dot(tokens, q_full, preferred_element_type=jnp.float32)
     key_sum = jnp.dot(tokens, k_full, preferred_element_type=jnp.float32)
     value_sum = jnp.dot(tokens, v_full, preferred_element_type=jnp.float32)
     query = query_sum.astype(jnp.bfloat16).reshape(row_count, heads_here, F)
     key_rows = key_sum.astype(jnp.bfloat16).reshape(row_count, heads_here, F)
-    values = value_sum + jnp.dot(low_rank, adapter_up, preferred_element_type=jnp.float32)
+    ups = adapter_up.reshape(cols, part_low.shape[1], adapter_up.shape[1])
+    values = value_sum + jnp.einsum("mtc,mce->te", low_parts, ups, preferred_element_type=jnp.float32)
     values = values.astype(jnp.bfloat16).reshape(row_count, heads_here, value_width)
     within, query_map, summary = block_local(query, key_rows, values, request, starts)
 

time: 155 us -> 153 us (0.987)
  the two profiles are of different devices: /device:TPU:60 before, /device:TPU:62 now
where the time goes in v18:
time: 153 us
  Pallas kernels  123 us (80%)
  matrix products  12.3 us (8%)
  other arithmetic  8.89 us (6%)
  local copies, waits for them, and re-layouts  8.18 us (5%)
    pallas_call x1, Pallas kernels, carried_scan(): pl.pallas_call(functools.partial(scan_kernel, n, rounds), out_shape=(jax....  44.8 us
    pallas_call x1, Pallas kernels, ring_scatter(): pl.pallas_call(functools.partial(ring_kernel, m), out_shape=jax.ShapeDtyp...  39.5 us
    pallas_call x1, Pallas kernels, direct_gather(): pl.pallas_call(functools.partial(gather_kernel, n, m), out_shape=(jax.Sha...  38.6 us

profile of v18, /device:TPU:62, one launch (start us, length us, event | category | flops | bytes accessed | tf_op | source)
XLA Modules:
  0.0 152.8 jit_solution(16551500018989740727)
XLA Ops:
  0.0 0.0 copy-start
  0.0 0.0 copy-start.9
  0.0 0.0 copy-start.8
  0.0 1.6 %pad_maximum_fusion.1.xd_ref = bf16[32,320]{1,0:T(8,128)(2,1)} fusion(bf16[32,256]{1,0:T(8,128)(2,1)} %param.18, bf16[32,32]{1,0:T(8,128)(2,1)} %param.17, bf16[32,32]{1,0:T(8,128)(2,1)} %param.16), kind=kLoop, calls=%fused_computation.74 | loop fusion | flops 61440 | bytes 40960 | tf_op jit(solution)/shard_map/concatenate | solution.py:508
  1.6 0.8 reduce-window.8
  2.4 0.1 convert_reduce_fusion
  2.5 0.7 select_reduce_fusion.1
  3.3 0.0 copy-done
  3.3 2.3 %fusion.6.xm_ref = bf16[512,32]{1,0:T(8,128)(2,1)} fusion(bf16[512,2048]{1,0:T(8,128)(2,1)S(1)} %copy-done, bf16[2048,32]{0,1:T(8,128)(2,1)} %param.19, s32[32]{0:T(128)S(1)} %fusion.51, s32[512]{0:T(512)S(1)} %select_reduce_fusion.1), kind=kOutput, calls=%fused_computation.13 | convolution fusion | flops 67158016 | bytes 2263168 | tf_op jit(solution)/shard_map/dot_general | solution.py:509
  5.5 0.0 copy-done.9
  5.5 0.1 and_reduce_fusion
  5.6 0.0 copy-done.5
  5.6 0.0 copy-done.6
  5.7 0.2 select_reduce_fusion
  5.8 0.5 compare_convert_fusion.1.early_ref.m_ref
  6.4 38.6 %shard_map.145 = (bf16[2,32,32,320]{3,2,1,0:T(8,128)(2,1)}, bf16[8,512,32]{2,1,0:T(8,128)(2,1)}) custom-call(bf16[32,320]{1,0:T(8,128)(2,1)} %pad_maximum_fusion.1.xd_ref, bf16[512,32]{1,0:T(8,128)(2,1)} %fusion.6.xm_ref, f32[12]{0:T(128)} %compare_convert_fusion.1.early_ref.m_ref), custom_call_target="tpu_custom_call" | custom-call | bytes 1572864 | tf_op jit(solution)/shard_map/pallas_call | solution.py:368
  44.9 0.0 copy-start.1
  44.9 1.8 %convolution_bitcast_fusion = f32[512,256]{0,1:T(8,128)S(1)} fusion(bf16[8,512,32]{2,1,0:T(8,128)(2,1)} %get-tuple-element.10, bf16[8,32,256]{2,1,0:T(8,128)(2,1)S(1)} %bitcast.134), kind=kOutput, calls=%fused_computation.3 | convolution fusion | flops 67108864 | bytes 917504 | tf_op jit(solution)/shard_map/mtc,mce->te/dot_general | solution.py:529
  46.8 0.3 copy.52
  47.0 1.1 fusion.4
  48.2 0.7 convolution_convert_fusion.2
  48.9 1.1 convolution_convert_fusion.1
  50.0 0.2 fusion.12
  50.2 1.8 %fusion = f32[2,128,512]{2,1,0:T(8,128)} fusion(bf16[512,2,128]{0,2,1:T(8,128)(2,1)S(1)} %bitcast.136, bf16[512,2,16]{0,2,1:T(8,128)(2,1)S(1)} %bitcast.112, bf16[512,2,16]{0,2,1:T(8,128)(2,1)S(1)} %bitcast.108, pred[512,512]{1,0:T(8,128)(4,1)S(1)} %fusion.12), kind=kOutput, calls=%fused_computation.2 | convolution fusion | flops 154664960 | bytes 1114112 | tf_op jit(solution)/shard_map/hij,jhe->ihe/dot_general | solution.py:68
  52.6 1.7 %concatenate.15 = bf16[512,2,153]{0,2,1:T(8,128)(2,1)S(1)} concatenate(bf16[512,2,1]{0,2,1:T(2,128)(2,1)S(1)} %broadcast.130, bf16[512,2,16]{0,2,1:T(8,128)(2,1)S(1)} %get-tuple-element.31, bf16[512,2,16]{0,2,1:T(8,128)(2,1)S(1)} %get-tuple-element.30, bf16[512,2,15]{0,2,1:T(8,128)(2,1)S(1)} %fusion.33, bf16[512,2,14]{0,2,1:T(8,128)(2,1)S(1)} %fusion.31, ...), dimensions={2} | concatenate | bytes 626688 | tf_op jit(solution)/shard_map/concatenate | solution.py:34
  54.3 0.7 fusion.58
  54.9 0.1 compare_reduce_fusion
  55.1 1.3 and_convert_fusion
  56.4 0.0 copy-start.4
  56.4 0.2 convolution_convert_fusion
  56.7 0.7 convert_element_type.98.s_ref
  57.3 44.8 %shard_map.146 = (f32[306,128]{1,0:T(8,128)}, bf16[2,32,32,256]{3,2,1,0:T(8,128)(2,1)}) custom-call(bf16[306,128]{1,0:T(8,128)(2,1)} %convert_element_type.98.s_ref, f32[12]{0:T(128)} %compare_convert_fusion.1.early_ref.m_ref, bf16[32,256]{1,0:T(8,128)(2,1)} %bitcast.126), custom_call_target="tpu_custom_call" | custom-call | flops 705024 | bytes 2458624 | tf_op jit(solution)/shard_map/pallas_call | solution.py:234
  102.2 0.9 convert_element_type.99
  103.1 0.0 copy-start.7
  103.2 0.1 multiply_convert_fusion
  103.3 0.5 copy.57
  103.9 0.0 copy-start.3
  103.9 1.4 pad_maximum_fusion
  105.4 1.2 gather_fusion
  106.7 0.4 multiply_bitcast_fusion
  107.0 1.3 multiply_reduce_fusion
  108.4 0.0 copy-done.3
  108.4 0.1 multiply_convert_fusion.1
  108.5 0.8 copy.64.n_ref
  109.4 1.1 copy.60
  110.4 39.5 %shard_map.147 = bf16[2,512,128]{2,1,0:T(8,128)(2,1)} custom-call(bf16[512,256]{1,0:T(8,128)(2,1)} %copy.64.n_ref, bf16[2048,256]{1,0:T(8,128)(2,1)} %bitcast.104), custom_call_target="tpu_custom_call" | custom-call | flops 536870912 | bytes 5505024 | tf_op jit(solution)/shard_map/pallas_call | solution.py:457
  149.9 1.0 slice_bitcast_fusion.1
  150.9 1.9 %fusion.5 = bf16[512,256]{1,0:T(8,128)(2,1)} fusion(bf16[512,256]{0,1:T(8,128)(2,1)S(1)} %bitcast.107, bf16[512,128]{1,0:T(8,128)(2,1)S(1)} %get-tuple-element.14, bf16[512,128]{1,0:T(8,128)(2,1)S(1)} %get-tuple-element.13, bf16[2048,256]{1,0:T(8,128)(2,1)} %bitcast.105, s32[]{:T(128)S(6)} %select_n.37), kind=kOutput, calls=%fused_computation.11 | convolution fusion | flops 67895296 | bytes 917508 | tf_op jit(solution)/shard_map/dot_general | solution.py:481
  (55 shorter events, 0.5 us)
Async XLA Ops:
  0.0 3.3 %copy-start = (bf16[512,2048]{1,0:T(8,128)(2,1)S(1)}, bf16[512,2048]{1,0:T(8,128)(2,1)}, u32[]{:S(2)}) copy-start(bf16[512,2048]{1,0:T(8,128)(2,1)} %param.15) | copy-start | bytes 6291460
  0.0 5.6 %copy-start.5 = (s32[12]{0:T(128)S(1)}, s32[12]{0:T(128)}, u32[]{:S(2)}) copy-start(s32[12]{0:T(128)} %constant.104) | copy-start | bytes 148
  0.0 5.6 %copy-start.6 = (s32[12]{0:T(128)S(1)}, s32[12]{0:T(128)}, u32[]{:S(2)}) copy-start(s32[12]{0:T(128)} %constant.105) | copy-start | bytes 148
  0.0 5.5 %copy-start.9 = (s32[4]{0:T(128)S(1)}, s32[4]{0:T(128)}, u32[]{:S(2)}) copy-start(s32[4]{0:T(128)} %param.21) | copy-start | bytes 52
  0.0 44.9 %copy-start.8 = (bf16[256,256]{1,0:T(8,128)(2,1)S(1)}, bf16[256,256]{1,0:T(8,128)(2,1)}, u32[]{:S(2)}) copy-start(bf16[256,256]{1,0:T(8,128)(2,1)} %param.20) | copy-start | bytes 393220
  44.9 1.8 %copy-start.1 = (bf16[2,32,32,320]{3,2,1,0:T(8,128)(2,1)S(1)}, bf16[2,32,32,320]{3,2,1,0:T(8,128)(2,1)}, u32[]{:S(2)}) copy-start(bf16[2,32,32,320]{3,2,1,0:T(8,128)(2,1)} %get-tuple-element.9) | copy-start | bytes 3932164
  56.4 48.9 %copy-start.4 = (s32[153]{0:T(256)S(1)}, s32[153]{0:T(256)}, u32[]{:S(2)}) copy-start(s32[153]{0:T(256)} %constant.107) | copy-start | bytes 1840
  103.1 3.5 %copy-start.7 = (bf16[153]{0:T(256)(128)(2,1)S(1)}, bf16[153]{0:T(256)(128)(2,1)}, u32[]{:S(2)}) copy-start(bf16[153]{0:T(256)(128)(2,1)} %constant.99.clone) | copy-start | bytes 922
  103.9 4.5 %copy-start.3 = (f32[256]{0:T(256)S(1)}, f32[256]{0:T(256)}, u32[]{:S(2)}) copy-start(f32[256]{0:T(256)} %param.23) | copy-start | bytes 3076
  106.7 2.7 %copy-start.2 = (bf16[2,32,32,256]{3,2,1,0:T(8,128)(2,1)S(1)}, bf16[2,32,32,256]{3,2,1,0:T(8,128)(2,1)}, u32[]{:S(2)}) copy-start(bf16[2,32,32,256]{3,2,1,0:T(8,128)(2,1)} %get-tuple-element.12) | copy-start | bytes 3145732

commit v19 on v18

--- a/solution.py
+++ b/solution.py
@@ -100,7 +100,7 @@
     return (hits == 0).astype(jnp.float32)
 
 
-def scan_kernel(n, rounds, s_ref, m_ref, xo_ref, e_ref, go_ref, parts, recv, send_sem, recv_sem,
+def scan_kernel(n, rounds, s_ref, m_ref, xo_ref, e_ref, go_ref, parts, recv, total, send_sem, recv_sem,
                 send_o, recv_o, send_x, recv_x, own):
     me = lax.axis_index("dp")
     col = lax.axis_index("mp")
@@ -179,7 +179,7 @@
     )
     each(1, chips, lambda k: to_far(k).start())
 
-    e_ref[...] = jnp.zeros_like(e_ref)
+    total[...] = jnp.zeros_like(total)
     copies = []
     for k in range(rounds):
         d = 1 << k
@@ -204,7 +204,7 @@
             got = recv[k].astype(jnp.float32)
             if k < rounds - 1:
                 parts[k] = (src[...].astype(jnp.float32) + m_ref[2 * k] * got).astype(parts.dtype)
-            e_ref[...] += m_ref[2 * k + 1] * got
+            total[...] += m_ref[2 * k + 1] * got
 
         if k < rounds - 1:
 
@@ -212,6 +212,7 @@
             def _():
                 parts[k] = src[...]
 
+    e_ref[...] = total[...].astype(e_ref.dtype)
     each(1, chips, lambda k: from_far(k).wait_recv())
     mine.wait()
     swap_out.start()
@@ -234,7 +235,7 @@
     out, gathered = pl.pallas_call(
         functools.partial(scan_kernel, n, rounds),
         out_shape=(
-            jax.ShapeDtypeStruct(flat.shape, jnp.float32),
+            jax.ShapeDtypeStruct(flat.shape, jnp.bfloat16),
             jax.ShapeDtypeStruct((2, n // 2) + piece.shape, piece.dtype),
         ),
         in_specs=[
@@ -246,6 +247,7 @@
         scratch_shapes=[
             pltpu.VMEM((max(rounds - 1, 1),) + flat.shape, jnp.bfloat16),
             pltpu.VMEM((rounds,) + flat.shape, jnp.bfloat16),
+            pltpu.VMEM(flat.shape, jnp.float32),
             pltpu.SemaphoreType.DMA((rounds,)),
             pltpu.SemaphoreType.DMA((rounds,)),
             pltpu.SemaphoreType.DMA((n // 2,)),

time: 153 us -> 153 us (level)
  no operation moved by 1% of the time
where the time goes in v19:
time: 153 us
  Pallas kernels  123 us (80%)
  matrix products  12.3 us (8%)
  local copies, waits for them, and re-layouts  9.07 us (6%)
  other arithmetic  7.96 us (5%)
    pallas_call x1, Pallas kernels, carried_scan(): pl.pallas_call(functools.partial(scan_kernel, n, rounds), out_shape=(jax....  44.8 us
    pallas_call x1, Pallas kernels, ring_scatter(): pl.pallas_call(functools.partial(ring_kernel, m), out_shape=jax.ShapeDtyp...  39.5 us
    pallas_call x1, Pallas kernels, direct_gather(): pl.pallas_call(functools.partial(gather_kernel, n, m), out_shape=(jax.Sha...  38.6 us

profile of v19, /device:TPU:62, one launch (start us, length us, event | category | flops | bytes accessed | tf_op | source)
XLA Modules:
  0.0 152.8 jit_solution(9372431020999786952)
XLA Ops:
  0.0 0.0 copy-start
  0.0 0.0 copy-start.9
  0.0 0.0 copy-start.8
  0.0 1.6 %pad_maximum_fusion.1.xd_ref = bf16[32,320]{1,0:T(8,128)(2,1)} fusion(bf16[32,256]{1,0:T(8,128)(2,1)} %param.18, bf16[32,32]{1,0:T(8,128)(2,1)} %param.17, bf16[32,32]{1,0:T(8,128)(2,1)} %param.16), kind=kLoop, calls=%fused_computation.74 | loop fusion | flops 61440 | bytes 40960 | tf_op jit(solution)/shard_map/concatenate | solution.py:510
  1.6 0.8 reduce-window.8
  2.4 0.1 convert_reduce_fusion
  2.5 0.7 select_reduce_fusion.1
  3.3 0.0 copy-done
  3.3 2.3 %fusion.6.xm_ref = bf16[512,32]{1,0:T(8,128)(2,1)} fusion(bf16[512,2048]{1,0:T(8,128)(2,1)S(1)} %copy-done, bf16[2048,32]{0,1:T(8,128)(2,1)} %param.19, s32[32]{0:T(128)S(1)} %fusion.51, s32[512]{0:T(512)S(1)} %select_reduce_fusion.1), kind=kOutput, calls=%fused_computation.13 | convolution fusion | flops 67158016 | bytes 2263168 | tf_op jit(solution)/shard_map/dot_general | solution.py:511
  5.5 0.0 copy-done.9
  5.5 0.1 and_reduce_fusion
  5.6 0.0 copy-done.5
  5.6 0.0 copy-done.6
  5.7 0.2 select_reduce_fusion
  5.8 0.5 compare_convert_fusion.1.early_ref.m_ref
  6.4 38.6 %shard_map.145 = (bf16[2,32,32,320]{3,2,1,0:T(8,128)(2,1)}, bf16[8,512,32]{2,1,0:T(8,128)(2,1)}) custom-call(bf16[32,320]{1,0:T(8,128)(2,1)} %pad_maximum_fusion.1.xd_ref, bf16[512,32]{1,0:T(8,128)(2,1)} %fusion.6.xm_ref, f32[12]{0:T(128)} %compare_convert_fusion.1.early_ref.m_ref), custom_call_target="tpu_custom_call" | custom-call | bytes 1572864 | tf_op jit(solution)/shard_map/pallas_call | solution.py:370
  44.9 0.0 copy-start.1
  44.9 1.8 %convolution_bitcast_fusion = f32[512,256]{0,1:T(8,128)S(1)} fusion(bf16[8,512,32]{2,1,0:T(8,128)(2,1)} %get-tuple-element.10, bf16[8,32,256]{2,1,0:T(8,128)(2,1)S(1)} %bitcast.134), kind=kOutput, calls=%fused_computation.3 | convolution fusion | flops 67108864 | bytes 917504 | tf_op jit(solution)/shard_map/mtc,mce->te/dot_general | solution.py:531
  46.8 0.3 copy.52
  47.0 1.1 fusion.4
  48.2 0.7 convolution_convert_fusion.2
  48.9 1.1 convolution_convert_fusion.1
  50.0 0.2 fusion.12
  50.2 1.8 %fusion = f32[2,128,512]{2,1,0:T(8,128)} fusion(bf16[512,2,128]{0,2,1:T(8,128)(2,1)S(1)} %bitcast.136, bf16[512,2,16]{0,2,1:T(8,128)(2,1)S(1)} %bitcast.112, bf16[512,2,16]{0,2,1:T(8,128)(2,1)S(1)} %bitcast.108, pred[512,512]{1,0:T(8,128)(4,1)S(1)} %fusion.12), kind=kOutput, calls=%fused_computation.2 | convolution fusion | flops 154664960 | bytes 1114112 | tf_op jit(solution)/shard_map/hij,jhe->ihe/dot_general | solution.py:68
  52.6 1.7 %concatenate.15 = bf16[512,2,153]{0,2,1:T(8,128)(2,1)S(1)} concatenate(bf16[512,2,1]{0,2,1:T(2,128)(2,1)S(1)} %broadcast.130, bf16[512,2,16]{0,2,1:T(8,128)(2,1)S(1)} %get-tuple-element.31, bf16[512,2,16]{0,2,1:T(8,128)(2,1)S(1)} %get-tuple-element.30, bf16[512,2,15]{0,2,1:T(8,128)(2,1)S(1)} %fusion.33, bf16[512,2,14]{0,2,1:T(8,128)(2,1)S(1)} %fusion.31, ...), dimensions={2} | concatenate | bytes 626688 | tf_op jit(solution)/shard_map/concatenate | solution.py:34
  54.3 0.7 fusion.58
  54.9 0.1 compare_reduce_fusion
  55.1 1.3 and_convert_fusion
  56.4 0.0 copy-start.4
  56.4 0.2 convolution_convert_fusion
  56.7 0.7 convert_element_type.92.s_ref
  57.3 44.8 %shard_map.146 = (bf16[306,128]{1,0:T(8,128)(2,1)}, bf16[2,32,32,256]{3,2,1,0:T(8,128)(2,1)}) custom-call(bf16[306,128]{1,0:T(8,128)(2,1)} %convert_element_type.92.s_ref, f32[12]{0:T(128)} %compare_convert_fusion.1.early_ref.m_ref, bf16[32,256]{1,0:T(8,128)(2,1)} %bitcast.126), custom_call_target="tpu_custom_call" | custom-call | flops 705024 | bytes 2458624 | tf_op jit(solution)/shard_map/pallas_call | solution.py:235
  102.2 0.0 copy-start.7
  102.2 0.9 reshape.166
  103.1 0.1 multiply_convert_fusion
  103.2 0.5 copy.57
  103.9 0.0 copy-start.3
  103.9 1.4 pad_maximum_fusion
  105.3 0.0 copy-done.4
  105.3 1.2 gather_fusion
  106.6 0.4 multiply_bitcast_fusion
  107.0 1.3 multiply_reduce_fusion
  108.4 0.1 multiply_convert_fusion.1
  108.5 0.8 copy.64.n_ref
  109.3 1.1 copy.60
  110.4 39.5 %shard_map.147 = bf16[2,512,128]{2,1,0:T(8,128)(2,1)} custom-call(bf16[512,256]{1,0:T(8,128)(2,1)} %copy.64.n_ref, bf16[2048,256]{1,0:T(8,128)(2,1)} %bitcast.104), custom_call_target="tpu_custom_call" | custom-call | flops 536870912 | bytes 5505024 | tf_op jit(solution)/shard_map/pallas_call | solution.py:459
  149.9 1.0 slice_bitcast_fusion.1
  150.9 1.9 %fusion.5 = bf16[512,256]{1,0:T(8,128)(2,1)} fusion(bf16[512,256]{0,1:T(8,128)(2,1)S(1)} %bitcast.107, bf16[512,128]{1,0:T(8,128)(2,1)S(1)} %get-tuple-element.14, bf16[512,128]{1,0:T(8,128)(2,1)S(1)} %get-tuple-element.13, bf16[2048,256]{1,0:T(8,128)(2,1)} %bitcast.105, s32[]{:T(128)S(6)} %select_n.37), kind=kOutput, calls=%fused_computation.11 | convolution fusion | flops 67895296 | bytes 917508 | tf_op jit(solution)/shard_map/dot_general | solution.py:483
  (54 shorter events, 0.4 us)
Async XLA Ops:
  0.0 3.3 %copy-start = (bf16[512,2048]{1,0:T(8,128)(2,1)S(1)}, bf16[512,2048]{1,0:T(8,128)(2,1)}, u32[]{:S(2)}) copy-start(bf16[512,2048]{1,0:T(8,128)(2,1)} %param.15) | copy-start | bytes 6291460
  0.0 5.6 %copy-start.5 = (s32[12]{0:T(128)S(1)}, s32[12]{0:T(128)}, u32[]{:S(2)}) copy-start(s32[12]{0:T(128)} %constant.104) | copy-start | bytes 148
  0.0 5.6 %copy-start.6 = (s32[12]{0:T(128)S(1)}, s32[12]{0:T(128)}, u32[]{:S(2)}) copy-start(s32[12]{0:T(128)} %constant.105) | copy-start | bytes 148
  0.0 5.5 %copy-start.9 = (s32[4]{0:T(128)S(1)}, s32[4]{0:T(128)}, u32[]{:S(2)}) copy-start(s32[4]{0:T(128)} %param.21) | copy-start | bytes 52
  0.0 44.9 %copy-start.8 = (bf16[256,256]{1,0:T(8,128)(2,1)S(1)}, bf16[256,256]{1,0:T(8,128)(2,1)}, u32[]{:S(2)}) copy-start(bf16[256,256]{1,0:T(8,128)(2,1)} %param.20) | copy-start | bytes 393220
  44.9 1.8 %copy-start.1 = (bf16[2,32,32,320]{3,2,1,0:T(8,128)(2,1)S(1)}, bf16[2,32,32,320]{3,2,1,0:T(8,128)(2,1)}, u32[]{:S(2)}) copy-start(bf16[2,32,32,320]{3,2,1,0:T(8,128)(2,1)} %get-tuple-element.9) | copy-start | bytes 3932164
  56.4 48.9 %copy-start.4 = (s32[153]{0:T(256)S(1)}, s32[153]{0:T(256)}, u32[]{:S(2)}) copy-start(s32[153]{0:T(256)} %constant.107) | copy-start | bytes 1840
  102.2 4.4 %copy-start.7 = (bf16[153]{0:T(256)(128)(2,1)S(1)}, bf16[153]{0:T(256)(128)(2,1)}, u32[]{:S(2)}) copy-start(bf16[153]{0:T(256)(128)(2,1)} %constant.99.clone) | copy-start | bytes 922
  103.9 4.5 %copy-start.3 = (f32[256]{0:T(256)S(1)}, f32[256]{0:T(256)}, u32[]{:S(2)}) copy-start(f32[256]{0:T(256)} %param.23) | copy-start | bytes 3076
  106.6 2.7 %copy-start.2 = (bf16[2,32,32,256]{3,2,1,0:T(8,128)(2,1)S(1)}, bf16[2,32,32,256]{3,2,1,0:T(8,128)(2,1)}, u32[]{:S(2)}) copy-start(bf16[2,32,32,256]{3,2,1,0:T(8,128)(2,1)} %get-tuple-element.12) | copy-start | bytes 3145732
